TPU v7x, 32 devices: a whole 2x2x4 slice. The times are simulated.
32 devices in a mesh: loop: 4 (over y, core), inner: 8 (over z, x).
Axes of the slice: x: 2, y: 2, z: 4, core: 2. Of those that a mesh axis runs over, the one named last changes fastest.
Arguments:
- snapshots: bfloat16 [8192, 1024], P(('loop', 'inner')), may hold values from -6 to 6
- bins: int32 [8192], replicated, may hold values from 0 to 63, as said below
- pairs: int32 [256, 2], replicated, may hold values from 0 to 63, as said below
- start_weights: bfloat16 [1024, 32], replicated, may hold values from -0.1875 to 0.1875
Outputs:
- basis: float32 [8192, 96], P(('loop', 'inner'))
- coefficients: float32 [4, 32, 32], replicated
Inputs may be any that keep to these rules, and one draw needn't show every extreme that they name: `bins`: the snapshot in row n has a bin in [r * 8, (r + 1) * 8), where r = (n // 256) mod (8). `pairs`: every row (a, b) has a <= b <= a + 8; every bin is paired with itself.
All inputs are finite; a program needn't handle non-finite values.
Results may differ from a plain program's by a relative error of at most 0.0003.
Values may be sent and summed in bfloat16 or wider, within the bound.
No kernel may reach another device: no remote copies, remote signals or barrier semaphores. Data moves between devices by JAX's collectives and lax.ppermute only.
A program may use at most 64 MiB of HBM per device.

v0:
```python
import functools

import jax
import jax.numpy as jnp
from jax import lax
from jax.experimental import pallas as pl
from jax.experimental.pallas import tpu as pltpu
from jax.sharding import Mesh, PartitionSpec as P

BINS_COL = 8
LANES = 128
KERNEL_VMEM = 16 * 2**20
ALL = ("row", "core", "inner")
HI = lax.Precision.HIGHEST
F32 = jnp.float32
BF16 = jnp.bfloat16


def nt(left, right, precision=HI):
    return lax.dot_general(
        left, right, (((1,), (1,)), ((), ())), precision=precision, preferred_element_type=F32
    )


def nn(left, right, precision=HI):
    return lax.dot_general(
        left, right, (((1,), (0,)), ((), ())), precision=precision, preferred_element_type=F32
    )


def tn(left, right):
    return nn(left.T, right)


def call(kernel, outs, *args, final=False, scalars=0):
    result = jax.ShapeDtypeStruct if final else pltpu.VMEM
    vectors = [pltpu.with_memory_space_constraint(a, pltpu.VMEM) for a in args[scalars:]]
    return pl.pallas_call(
        kernel,
        out_shape=[result(shape, kind) for shape, kind in outs],
        in_specs=[pl.BlockSpec(memory_space=pltpu.SMEM)] * scalars
        + [pl.BlockSpec(memory_space=pltpu.VMEM)] * len(vectors),
        compiler_params=pltpu.CompilerParams(vmem_limit_bytes=KERNEL_VMEM),
    )(*args[:scalars], *vectors)


def spread(value):
    return jnp.broadcast_to(value, (8, LANES))


def eliminate(groups, count):
    sub = lax.broadcasted_iota(jnp.int32, (8, LANES), 0)
    lane = lax.broadcasted_iota(jnp.int32, (8, LANES), 1)
    g = list(groups)
    for j in range(0, count, 2):
        q, s = divmod(j, 8)
        first = [spread(v[:, j:j + 1]) for v in g[q:]]
        second = [spread(v[:, j + 1:j + 2]) for v in g[q:]]
        row_a = spread(g[q][s:s + 1, :])
        row_b = spread(g[q][s + 1:s + 2, :])
        a = spread(first[0][s:s + 1, :])
        b = spread(first[0][s + 1:s + 2, :])
        d = spread(second[0][s + 1:s + 2, :])
        inverse = 1.0 / (a * d - b * b)
        left = (d * inverse) * row_a - (b * inverse) * row_b
        right = (a * inverse) * row_b - (b * inverse) * row_a
        for i in range(len(g) - q):
            change = first[i] * left + second[i] * right
            if i == 0:
                change = jnp.where(sub > s + 1, change, 0.0)
            g[q + i] = g[q + i] - change
    odd = sub % 2 == 1
    done = []
    for q, v in enumerate(g):
        above = pltpu.roll(v, 1, 0)
        at = lane == sub + (8 * q - 1)
        b = jnp.sum(jnp.where(at, v, 0.0), axis=1, keepdims=True)
        a = jnp.sum(jnp.where(at, above, 0.0), axis=1, keepdims=True)
        v = jnp.where(odd, v - (b / jnp.where(odd, a, 1.0)) * above, v)
        pivot = jnp.sum(jnp.where(lane == sub + 8 * q, v, 0.0), axis=1, keepdims=True)
        done.append(v * lax.rsqrt(pivot))
    return done


def eye_lanes(rows, start):
    row = lax.broadcasted_iota(jnp.int32, (rows, LANES), 0)
    lane = lax.broadcasted_iota(jnp.int32, (rows, LANES), 1)
    return jnp.where(lane == row + start, 1.0, 0.0)


def start_kernel(weights, rows, start, copies):
    value = nt(weights[...], rows[...], None)
    start[...] = value
    gram = nt(value, value)
    width = gram.shape[0]
    packed = jnp.concatenate([gram[8 * q:8 * q + 8, :] for q in range(width // 8)], axis=1)
    copies[...] = jnp.broadcast_to(packed[None], copies.shape)


def first_basis_kernel(parts, start, basis):
    packed = jnp.sum(parts[...], axis=0)
    width = start.shape[0]
    eye = eye_lanes(width, LANES // 2)
    groups = []
    for q in range(width // 8):
        piece = packed[:, width * q:width * (q + 1)]
        piece = jnp.concatenate([piece, jnp.zeros((8, LANES - width), F32)], axis=1)
        groups.append(piece + eye[8 * q:8 * q + 8, :])
    whole = jnp.concatenate(eliminate(groups, width), axis=0)
    inverse = whole[:, LANES // 2:LANES // 2 + width]
    basis[...] = nn(inverse, start[...])


def links_kernel(n_inner, place, bins, pairs, hots, links):
    column, group = place[0], place[1]
    odd = column % 2
    step = 2 * odd - 1
    others = (column, column - step, column + step)
    bin_of = lax.broadcasted_iota(jnp.int32, (BINS_COL, 1), 0)

    def hot(values, base):
        return jnp.where(values == bin_of + base, 1.0, 0.0)

    def bins_at(l, c):
        return bins[pl.ds(l * n_inner + c, 1), :]

    rows = jnp.concatenate(
        [hot(bins_at(group ^ r, column), column * BINS_COL) for r in (0, 2, 1, 3)], axis=1
    )
    left, right = pairs[0:1, :], pairs[1:2, :]
    base = column * BINS_COL
    left_mine, right_mine = hot(left, base), hot(right, base)
    for i, other in enumerate(others):
        base = other * BINS_COL
        count = nt(hot(left, base), right_mine, None) + nt(hot(right, base), left_mine, None)
        linked = jnp.where(count > 0.5, 1.0, 0.0)
        links[i] = nn(linked, rows, None)
        theirs = bins_at(group, jnp.clip(other, 0, n_inner - 1))
        hots[i] = hot(theirs, base)


def turn_kernel(r0, r1, r2, r3, turned, norms):
    span = r0.shape[0]
    for i, rows in enumerate((r0, r1, r2, r3)):
        at = slice(i * span, (i + 1) * span)
        value = rows[...].T
        turned[:, at] = value
        wide = value.astype(F32)
        norms[:, at] = jnp.sum(wide * wide, axis=0, keepdims=True)


def tile_kernel(scale, kind, part, other, hots, all_links, norms, degree, turned, *refs):
    high, low, out = refs[-3:]
    x = other[...]
    wide = x.astype(F32)
    own = jnp.sum(wide * wide, axis=1, keepdims=True)
    size = x.shape[0]
    hot = hots[kind, :, part * size:(part + 1) * size]
    mask = nn(hot.T, all_links[kind], None)
    products = nn(x, turned[...], None)
    distance = own + norms[...] - 2.0 * products
    value = mask * jnp.exp(distance * scale)
    top = value.astype(BF16)
    high[...] = top
    low[...] = (value - top.astype(F32)).astype(BF16)
    out[...] = degree[...] + jnp.sum(value, axis=0, keepdims=True)


def apply_kernel(*refs):
    vectors, tiles, (keep, send) = refs[:3], refs[3:-2], refs[-2:]
    width = vectors[0].shape[0]
    half = keep.shape[1]
    total = None
    count = len(tiles) // 2
    strip = jnp.concatenate([v[...] for v in vectors], axis=1)
    top = strip.astype(BF16)
    low = (strip - top.astype(F32)).astype(BF16)
    both = jnp.concatenate([top, low], axis=0)
    at = 0
    for i in range(count):
        high_tile, low_tile = tiles[2 * i][...], tiles[2 * i + 1][...]
        size = high_tile.shape[0]
        piece = nn(both[:, at:at + size], high_tile, None)
        piece = piece[:width] + piece[width:] + nn(top[:, at:at + size], low_tile, None)
        total = piece if total is None else total + piece
        at += size
    keep[...] = total[:, :half]
    send[...] = total[:, half:]


def gram_kernel(mine, got, inv_root, basis, image, image_next, packed):
    value = inv_root[...] * (mine[...] + got[...])
    image_next[...] = value
    first = image[...]
    packed[...] = jnp.concatenate(
        [nt(basis[...], first), nt(first, first), nt(first, value), nt(value, value)], axis=1
    )


def last_kernel(parts, q0, v1, v2, basis, coefficients):
    packed = jnp.sum(parts[...], axis=0)
    width = q0.shape[0]
    a_0, m_11, m_12, m_22 = [packed[:, width * i:width * (i + 1)] for i in range(4)]
    left_0 = jnp.concatenate([a_0, m_11], axis=1)
    cross = tn(left_0, left_0)
    top = jnp.concatenate([m_11, m_12], axis=1) - cross[:width]
    low = jnp.concatenate([m_12, m_22], axis=1) - cross[width:]
    gram = jnp.concatenate([top, low], axis=0)
    rows = 2 * width
    gram = jnp.concatenate([gram, jnp.zeros((rows, LANES - rows), F32)], axis=1)
    gram = gram + eye_lanes(rows, LANES // 2)
    groups = [gram[8 * q:8 * q + 8, :] for q in range(rows // 8)]
    whole = jnp.concatenate(eliminate(groups, rows), axis=0)
    inverse = whole[:, LANES // 2:LANES // 2 + rows]
    q = q0[...]
    rest = jnp.concatenate([v1[...], v2[...]], axis=0) - tn(left_0, q)
    basis[:width, :] = q
    basis[width:, :] = nn(inverse, rest)
    row = lax.broadcasted_iota(jnp.int32, (width, width), 0)
    col = lax.broadcasted_iota(jnp.int32, (width, width), 1)
    r_11 = jnp.where(col >= row, whole[:width, :width], 0.0)
    r_12 = whole[:width, width:rows]
    r_22 = jnp.where(col >= row, whole[width:, width:rows], 0.0)
    z_11 = inverse[:width, :width]
    coefficients[0] = a_0
    coefficients[1] = r_11
    coefficients[2] = nt(r_12 - nn(r_11, a_0), z_11)
    coefficients[3] = jnp.where(col >= row, nt(r_22, z_11), 0.0)


def routes(n_loop, n_inner):
    def build(loop_of, inner_of):
        pairs = []
        for l in range(n_loop):
            for c in range(n_inner):
                if 0 <= inner_of(c) < n_inner:
                    pairs.append((l * n_inner + c, loop_of(l) * n_inner + inner_of(c)))
        return pairs

    same = lambda v: v
    return {
        "core": build(lambda l: l ^ 1, same),
        "row": build(lambda l: l ^ 2, same),
        "near": build(same, lambda c: c ^ 1),
        "far": build(same, lambda c: c + 1 if c % 2 else c - 1),
        "relay": build(same, lambda c: c - 2 if c % 2 else c + 2),
    }


def steps(snapshots, bins, pairs, start_weights):
    row_count, features = snapshots.shape
    width = start_weights.shape[1]
    n_row = lax.axis_size("row")
    n_loop = n_row * lax.axis_size("core")
    n_inner = lax.axis_size("inner")
    column = lax.axis_index("inner")
    group = lax.axis_index(("row", "core"))
    route = routes(n_loop, n_inner)

    def move(value, name):
        return lax.ppermute(value, ALL, route[name])

    half = row_count // 2
    across = move(snapshots, "row")
    mate = move(snapshots, "core")
    near_a = move(snapshots[:half], "near")
    near_b = move(snapshots[half:], "near")
    far_a = move(near_a, "relay")
    far_b = move(near_b, "relay")
    across_mate = move(across, "core")
    group_rows = (snapshots, across, mate, across_mate)

    place = jnp.where(jnp.arange(2) == 0, column, group).astype(jnp.int32)
    hots, links = call(
        functools.partial(links_kernel, n_inner),
        [((3, BINS_COL, row_count), F32), ((3, BINS_COL, n_loop * row_count), F32)],
        place, bins.reshape(n_loop * n_inner, row_count), pairs.T,
        scalars=1,
    )

    n_all = n_loop * n_inner
    start, copies = call(
        start_kernel,
        [((width, row_count), F32), ((n_all, 8, width * width // 8), F32)],
        start_weights.T,
        snapshots,
    )
    parts = lax.all_to_all(copies, ALL, 0, 0)
    (basis_0,) = call(first_basis_kernel, [((width, row_count), F32)], parts, start)

    span = n_loop * row_count
    turned, norms = call(turn_kernel, [((features, span), BF16), ((1, span), F32)], *group_rows)
    degree = jnp.zeros((1, span), F32)
    tiles = []
    for kind, part, rows, after in (
        (0, 0, snapshots, ()),
        (1, 0, near_a, ()),
        (1, 1, near_b, (basis_0,)),
        (2, 0, far_a, ()),
        (2, 1, far_b, ()),
    ):
        size = rows.shape[0]
        high, low, degree = call(
            functools.partial(tile_kernel, -3.0 / features, kind, part),
            [((size, span), BF16), ((size, span), BF16), ((1, span), F32)],
            rows, hots, links, norms, degree, turned, *after,
        )
        tiles += [high, low]

    def group_sum(keep, send):
        keep = keep + move(send, "core")
        return keep[:, :row_count], move(keep[:, row_count:], "row")

    mine, got = group_sum(degree[:, :span // 2], degree[:, span // 2:])
    inv_root = lax.rsqrt(mine + got)

    def apply(vectors):
        scaled = inv_root * vectors
        keep, send = call(
            apply_kernel,
            [((width, span // 2), F32)] * 2,
            scaled, move(scaled, "near"), move(scaled, "far"), *tiles,
        )
        return group_sum(keep, send)

    mine, got = apply(basis_0)
    image_1 = inv_root * (mine + got)
    mine, got = apply(image_1)
    image_2, packed = call(
        gram_kernel,
        [((width, row_count), F32), ((width, 4 * width), F32)],
        mine, got, inv_root, basis_0, image_1,
    )
    packed = packed + move(packed, "core")
    copies = jnp.broadcast_to(packed[None], (n_row * n_inner,) + packed.shape)
    parts = lax.all_to_all(copies, ("row", "inner"), 0, 0)
    basis, coefficients = call(
        last_kernel,
        [((3 * width, row_count), F32), ((4, width, width), F32)],
        parts, basis_0, image_1, image_2,
        final=True,
    )
    return basis.T, coefficients


def solution(mesh):
    n_loop, n_inner = mesh.shape["loop"], mesh.shape["inner"]
    fine = Mesh(mesh.devices.reshape(n_loop // 2, 2, n_inner), ALL)
    in_specs = (P(ALL, None), P(), P(), P())
    out_specs = (P(ALL, None), P())
    return jax.shard_map(steps, mesh=fine, in_specs=in_specs, out_specs=out_specs, check_vma=False)
```

profile of v0, /device:TPU:0, one launch (start us, length us, event | category | flops | bytes accessed | tf_op | source)
XLA Modules:
  0.0 109.9 jit_solution(17723338405246986488)
XLA Ops:
  0.6 3.1 %collective-permute-start.2 = (bf16[256,1024]{1,0:T(8,128)(2,1)}, bf16[256,1024]{1,0:T(8,128)(2,1)S(1)}, u32[]{:S(2)}, u32[]{:S(2)}) collective-permute-start(bf16[256,1024]{1,0:T(8,128)(2,1)} %rows.1), channel_id=1, source_target_pairs={{0,16},{1,17},{2,18},{3,19},{4,20},{5,21},{6,22},{7,23},{8,24},{9,... | collective-permute-start | bytes 1572872 | tf_op jit(solution)/shard_map/ppermute | solution.py:261
  3.7 12.1 %collective-permute-done.2.r1 = bf16[256,1024]{1,0:T(8,128)(2,1)S(1)} collective-permute-done((bf16[256,1024]{1,0:T(8,128)(2,1)}, bf16[256,1024]{1,0:T(8,128)(2,1)S(1)}, u32[]{:S(2)}, u32[]{:S(2)}) %collective-permute-start.2) | collective-permute-done | bytes 524320 | tf_op jit(solution)/shard_map/ppermute | solution.py:261
  15.8 1.1 fusion.3
  16.9 1.8 %collective-permute-start.5 = (bf16[128,1024]{1,0:T(8,128)(2,1)S(1)}, bf16[128,1024]{1,0:T(8,128)(2,1)S(1)}, u32[]{:S(2)}, u32[]{:S(2)}) collective-permute-start(bf16[128,1024]{1,0:T(8,128)(2,1)S(1)} %get-tuple-element.62), channel_id=1, source_target_pairs={{0,1},{1,0},{2,3},{3,2},{4,5},{5,4},{6,7},{7,6},{8,9},{9,8},{10,11... | collective-permute-start | bytes 786440 | tf_op jit(solution)/shard_map/ppermute | solution.py:261
  19.0 7.2 %collective-permute-done.5.other = bf16[128,1024]{1,0:T(8,128)(2,1)S(1)} collective-permute-done((bf16[128,1024]{1,0:T(8,128)(2,1)S(1)}, bf16[128,1024]{1,0:T(8,128)(2,1)S(1)}, u32[]{:S(2)}, u32[]{:S(2)}) %collective-permute-start.5) | collective-permute-done | bytes 262176 | tf_op jit(solution)/shard_map/ppermute | solution.py:261
  26.1 3.7 %collective-permute-start.6 = (bf16[128,1024]{1,0:T(8,128)(2,1)S(1)}, bf16[128,1024]{1,0:T(8,128)(2,1)S(1)}, u32[]{:S(2)}, u32[]{:S(2)}) collective-permute-start(bf16[128,1024]{1,0:T(8,128)(2,1)S(1)} %collective-permute-done.5.other), channel_id=1, source_target_pairs={{0,2},{2,4},{3,1},{4,6},{5,3},{7,5},{8,10},{10,12},{11,9},{12,14},... | collective-permute-start | bytes 786440 | tf_op jit(solution)/shard_map/ppermute | solution.py:261
  29.9 1.4 %collective-permute-done.other = bf16[128,1024]{1,0:T(8,128)(2,1)S(1)} collective-permute-done((bf16[128,1024]{1,0:T(8,128)(2,1)S(1)}, bf16[128,1024]{1,0:T(8,128)(2,1)S(1)}, u32[]{:S(2)}, u32[]{:S(2)}) %collective-permute-start) | collective-permute-done | bytes 262176 | tf_op jit(solution)/shard_map/ppermute | solution.py:261
  31.3 3.7 %collective-permute-start.1 = (bf16[128,1024]{1,0:T(8,128)(2,1)S(1)}, bf16[128,1024]{1,0:T(8,128)(2,1)S(1)}, u32[]{:S(2)}, u32[]{:S(2)}) collective-permute-start(bf16[128,1024]{1,0:T(8,128)(2,1)S(1)} %collective-permute-done.other), channel_id=1, source_target_pairs={{0,2},{2,4},{3,1},{4,6},{5,3},{7,5},{8,10},{10,12},{11,9},{12,14},... | collective-permute-start | bytes 786440 | tf_op jit(solution)/shard_map/ppermute | solution.py:261
  35.0 1.0 copy-done
  36.1 0.8 copy-done.2
  36.9 1.1 %shard_map.63 = (f32[32,256]{1,0:T(8,128)S(1)}, f32[32,8,128]{2,1,0:T(8,128)}) custom-call(bf16[32,1024]{1,0:T(8,128)(2,1)S(1)} %bitcast.4, bf16[256,1024]{1,0:T(8,128)(2,1)S(1)} %copy-done), custom_call_target="tpu_custom_call" | custom-call | tf_op jit(solution)/shard_map/pallas_call | solution.py:38
  38.0 4.7 %all-to-all-start = ((f32[32,8,128]{2,1,0:T(8,128)}), f32[32,8,128]{2,1,0:T(8,128)S(1)}, u32[]{:S(2)}, u32[]{:S(2)}) async-start(f32[32,8,128]{2,1,0:T(8,128)} %get-tuple-element.37), calls=%async_computation | async-start | bytes 262144 | tf_op jit(solution)/shard_map/all_to_all | solution.py:288
  42.8 0.8 reshape.8.bins
  44.3 1.0 shard_map.59
  45.3 5.3 %all-to-all-done.parts = f32[32,8,128]{2,1,0:T(8,128)S(1)} async-done(((f32[32,8,128]{2,1,0:T(8,128)}), f32[32,8,128]{2,1,0:T(8,128)S(1)}, u32[]{:S(2)}, u32[]{:S(2)}) %all-to-all-start) | async-done | bytes 131104 | tf_op jit(solution)/shard_map/all_to_all | solution.py:288
  50.6 2.5 %shard_map.64.refs_0_.basis.q0 = f32[32,256]{1,0:T(8,128)S(1)} custom-call(f32[32,8,128]{2,1,0:T(8,128)S(1)} %all-to-all-done.parts, f32[32,256]{1,0:T(8,128)S(1)} %get-tuple-element.38.start), custom_call_target="tpu_custom_call" | custom-call | tf_op jit(solution)/shard_map/pallas_call | solution.py:38
  53.8 1.2 %shard_map.61 = (bf16[256,1024]{1,0:T(8,128)(2,1)S(1)}, bf16[256,1024]{1,0:T(8,128)(2,1)S(1)}, f32[1,1024]{1,0:T(1,128)S(1)}) custom-call(bf16[256,1024]{1,0:T(8,128)(2,1)S(1)} %copy-done.1, f32[3,8,256]{2,1,0:T(8,128)S(1)} %get-tuple-element.31.hots, f32[3,8,1024]{2,1,0:T(8,128)S(1)} %get-tuple-element.32.all_links, f32[1,1024]{1,0:T(1,128)S(1)} %get-tuple-element.33.norms, ...), custom_call_target="tpu_custom_call" | custom-call | tf_op jit(solution)/shard_map/pallas_call | solution.py:38
  57.8 1.0 collective-permute-done.7
  58.9 1.0 collective-permute-start.8
  59.9 2.6 %collective-permute-done.8 = f32[1,256]{1,0:T(1,128)S(1)} collective-permute-done((f32[1,256]{1,0:T(1,128)S(1)}, f32[1,256]{1,0:T(1,128)S(1)}, u32[]{:S(2)}, u32[]{:S(2)}) %collective-permute-start.8) | collective-permute-done | bytes 1056 | tf_op jit(solution)/shard_map/ppermute | solution.py:261
  63.2 3.6 %collective-permute-start.9 = (f32[32,256]{1,0:T(8,128)S(1)}, f32[32,256]{1,0:T(8,128)S(1)}, u32[]{:S(2)}, u32[]{:S(2)}) collective-permute-start(f32[32,256]{1,0:T(8,128)S(1)} %broadcast_multiply_fusion.1.refs_0_), channel_id=1, source_target_pairs={{0,1},{1,0},{2,3},{3,2},{4,5},{5,4},{6,7},{7,6},{8,9},{9,8},{10,11... | collective-permute-start | bytes 98312 | tf_op jit(solution)/shard_map/ppermute | solution.py:261
  66.8 1.9 %collective-permute-done.9.refs_1_ = f32[32,256]{1,0:T(8,128)S(1)} collective-permute-done((f32[32,256]{1,0:T(8,128)S(1)}, f32[32,256]{1,0:T(8,128)S(1)}, u32[]{:S(2)}, u32[]{:S(2)}) %collective-permute-start.9) | collective-permute-done | bytes 32800 | tf_op jit(solution)/shard_map/ppermute | solution.py:261
  69.4 1.2 %collective-permute-done.11 = f32[32,512]{1,0:T(8,128)S(1)} collective-permute-done((f32[32,512]{1,0:T(8,128)S(1)}, f32[32,512]{1,0:T(8,128)S(1)}, u32[]{:S(2)}, u32[]{:S(2)}) %collective-permute-start.11) | collective-permute-done | bytes 65568 | tf_op jit(solution)/shard_map/ppermute | solution.py:261
  71.3 3.3 %collective-permute-done.12 = f32[32,256]{1,0:T(8,128)S(1)} collective-permute-done((f32[32,256]{1,0:T(8,128)S(1)}, f32[32,256]{1,0:T(8,128)S(1)}, u32[]{:S(2)}, u32[]{:S(2)}) %collective-permute-start.12) | collective-permute-done | bytes 32800 | tf_op jit(solution)/shard_map/ppermute | solution.py:261
  75.3 5.1 %collective-permute-start.13 = (f32[32,256]{1,0:T(8,128)S(1)}, f32[32,256]{1,0:T(8,128)S(1)}, u32[]{:S(2)}, u32[]{:S(2)}) collective-permute-start(f32[32,256]{1,0:T(8,128)S(1)} %get-tuple-element.60.refs_0_), channel_id=1, source_target_pairs={{0,1},{1,0},{2,3},{3,2},{4,5},{5,4},{6,7},{7,6},{8,9},{9,8},{10,11... | collective-permute-start | bytes 98312 | tf_op jit(solution)/shard_map/ppermute | solution.py:261
  80.4 1.9 %collective-permute-done.13.refs_1_ = f32[32,256]{1,0:T(8,128)S(1)} collective-permute-done((f32[32,256]{1,0:T(8,128)S(1)}, f32[32,256]{1,0:T(8,128)S(1)}, u32[]{:S(2)}, u32[]{:S(2)}) %collective-permute-start.13) | collective-permute-done | bytes 32800 | tf_op jit(solution)/shard_map/ppermute | solution.py:261
  83.0 1.2 %collective-permute-done.15 = f32[32,512]{1,0:T(8,128)S(1)} collective-permute-done((f32[32,512]{1,0:T(8,128)S(1)}, f32[32,512]{1,0:T(8,128)S(1)}, u32[]{:S(2)}, u32[]{:S(2)}) %collective-permute-start.15) | collective-permute-done | bytes 65568 | tf_op jit(solution)/shard_map/ppermute | solution.py:261
  84.3 0.8 collective-permute-start.16
  85.1 3.2 %collective-permute-done.16.got = f32[32,256]{1,0:T(8,128)S(1)} collective-permute-done((f32[32,256]{1,0:T(8,128)S(1)}, f32[32,256]{1,0:T(8,128)S(1)}, u32[]{:S(2)}, u32[]{:S(2)}) %collective-permute-start.16) | collective-permute-done | bytes 32800 | tf_op jit(solution)/shard_map/ppermute | solution.py:261
  88.6 1.2 %collective-permute-done.17 = f32[32,128]{1,0:T(8,128)S(1)} collective-permute-done((f32[32,128]{1,0:T(8,128)S(1)}, f32[32,128]{1,0:T(8,128)S(1)}, u32[]{:S(2)}, u32[]{:S(2)}) %collective-permute-start.17) | collective-permute-done | bytes 16416 | tf_op jit(solution)/shard_map/ppermute | solution.py:261
  89.8 14.3 %all_to_all.10.parts = f32[16,32,128]{2,1,0:T(8,128)S(1)} all-to-all(f32[16,32,128]{2,1,0:T(8,128)S(1)} %broadcast_in_dim.20), channel_id=1, replica_groups=mesh['row'=2,'core'=2,'inner'=8] {'row','inner'}, dimensions={0} | all-to-all | bytes 524288 | tf_op jit(solution)/shard_map/all_to_all | solution.py:336
  104.0 5.8 %shard_map.71 = (f32[96,256]{1,0:T(8,128)}, f32[4,32,32]{2,1,0:T(8,128)}) custom-call(f32[16,32,128]{2,1,0:T(8,128)S(1)} %all_to_all.10.parts, f32[32,256]{1,0:T(8,128)S(1)} %shard_map.64.refs_0_.basis.q0, f32[32,256]{1,0:T(8,128)S(1)} %get-tuple-element.61.image.v1, f32[32,256]{1,0:T(8,128)S(1)} %get-tuple-element.57.v2), custom_call_target="tpu_custom_call" | custom-call | tf_op jit(solution)/shard_map/pallas_call | solution.py:38
  (44 shorter events, 8.3 us)
Async XLA Ops:
  0.6 52.5 %copy-start.1 = (bf16[256,1024]{1,0:T(8,128)(2,1)S(1)}, bf16[256,1024]{1,0:T(8,128)(2,1)}, u32[]{:S(2)}) copy-start(bf16[256,1024]{1,0:T(8,128)(2,1)} %rows.1) | copy-start | bytes 1572868
  0.6 15.2 %collective-permute-start.2 = (bf16[256,1024]{1,0:T(8,128)(2,1)}, bf16[256,1024]{1,0:T(8,128)(2,1)S(1)}, u32[]{:S(2)}, u32[]{:S(2)}) collective-permute-start(bf16[256,1024]{1,0:T(8,128)(2,1)} %rows.1), channel_id=1, source_target_pairs={{0,16},{1,17},{2,18},{3,19},{4,20},{5,21},{6,22},{7,23},{8,24},{9,... | collective-permute-start | bytes 1572872 | tf_op jit(solution)/shard_map/ppermute | solution.py:261
  3.7 49.4 %collective-permute-start.3 = (bf16[256,1024]{1,0:T(8,128)(2,1)}, bf16[256,1024]{1,0:T(8,128)(2,1)S(1)}, u32[]{:S(2)}, u32[]{:S(2)}) collective-permute-start(bf16[256,1024]{1,0:T(8,128)(2,1)} %rows.1), channel_id=1, source_target_pairs={{0,8},{1,9},{2,10},{3,11},{4,12},{5,13},{6,14},{7,15},{8,0},{9,1},... | collective-permute-start | bytes 1572872 | tf_op jit(solution)/shard_map/ppermute | solution.py:261
  15.8 37.3 %collective-permute-start.4 = (bf16[256,1024]{1,0:T(8,128)(2,1)S(1)}, bf16[256,1024]{1,0:T(8,128)(2,1)S(1)}, u32[]{:S(2)}, u32[]{:S(2)}) collective-permute-start(bf16[256,1024]{1,0:T(8,128)(2,1)S(1)} %collective-permute-done.2.r1), channel_id=1, source_target_pairs={{0,8},{1,9},{2,10},{3,11},{4,12},{5,13},{6,14},{7,15},{8,0},{9,1},... | collective-permute-start | bytes 1572872 | tf_op jit(solution)/shard_map/ppermute | solution.py:261
  16.9 9.2 %collective-permute-start.5 = (bf16[128,1024]{1,0:T(8,128)(2,1)S(1)}, bf16[128,1024]{1,0:T(8,128)(2,1)S(1)}, u32[]{:S(2)}, u32[]{:S(2)}) collective-permute-start(bf16[128,1024]{1,0:T(8,128)(2,1)S(1)} %get-tuple-element.62), channel_id=1, source_target_pairs={{0,1},{1,0},{2,3},{3,2},{4,5},{5,4},{6,7},{7,6},{8,9},{9,8},{10,11... | collective-permute-start | bytes 786440 | tf_op jit(solution)/shard_map/ppermute | solution.py:261
  18.7 12.6 %collective-permute-start = (bf16[128,1024]{1,0:T(8,128)(2,1)S(1)}, bf16[128,1024]{1,0:T(8,128)(2,1)S(1)}, u32[]{:S(2)}, u32[]{:S(2)}) collective-permute-start(bf16[128,1024]{1,0:T(8,128)(2,1)S(1)} %get-tuple-element.63), channel_id=1, source_target_pairs={{0,1},{1,0},{2,3},{3,2},{4,5},{5,4},{6,7},{7,6},{8,9},{9,8},{10,11... | collective-permute-start | bytes 786440 | tf_op jit(solution)/shard_map/ppermute | solution.py:261
  26.1 30.2 %collective-permute-start.6 = (bf16[128,1024]{1,0:T(8,128)(2,1)S(1)}, bf16[128,1024]{1,0:T(8,128)(2,1)S(1)}, u32[]{:S(2)}, u32[]{:S(2)}) collective-permute-start(bf16[128,1024]{1,0:T(8,128)(2,1)S(1)} %collective-permute-done.5.other), channel_id=1, source_target_pairs={{0,2},{2,4},{3,1},{4,6},{5,3},{7,5},{8,10},{10,12},{11,9},{12,14},... | collective-permute-start | bytes 786440 | tf_op jit(solution)/shard_map/ppermute | solution.py:261
  31.3 25.7 %collective-permute-start.1 = (bf16[128,1024]{1,0:T(8,128)(2,1)S(1)}, bf16[128,1024]{1,0:T(8,128)(2,1)S(1)}, u32[]{:S(2)}, u32[]{:S(2)}) collective-permute-start(bf16[128,1024]{1,0:T(8,128)(2,1)S(1)} %collective-permute-done.other), channel_id=1, source_target_pairs={{0,2},{2,4},{3,1},{4,6},{5,3},{7,5},{8,10},{10,12},{11,9},{12,14},... | collective-permute-start | bytes 786440 | tf_op jit(solution)/shard_map/ppermute | solution.py:261
  35.0 1.0 copy-start
  36.1 0.8 copy-start.2
  38.0 12.5 %all-to-all-start = ((f32[32,8,128]{2,1,0:T(8,128)}), f32[32,8,128]{2,1,0:T(8,128)S(1)}, u32[]{:S(2)}, u32[]{:S(2)}) async-start(f32[32,8,128]{2,1,0:T(8,128)} %get-tuple-element.37), calls=%async_computation | async-start | bytes 262144 | tf_op jit(solution)/shard_map/all_to_all | solution.py:288
  43.6 0.7 copy-start.3
  57.7 1.2 %collective-permute-start.7 = (f32[1,512]{1,0:T(1,128)S(1)}, f32[1,512]{1,0:T(1,128)S(1)}, u32[]{:S(2)}, u32[]{:S(2)}) collective-permute-start(f32[1,512]{1,0:T(1,128)S(1)} %slice.33), channel_id=1, source_target_pairs={{0,8},{1,9},{2,10},{3,11},{4,12},{5,13},{6,14},{7,15},{8,0},{9,1},... | collective-permute-start | bytes 6152 | tf_op jit(solution)/shard_map/ppermute | solution.py:261
  58.9 3.6 %collective-permute-start.8 = (f32[1,256]{1,0:T(1,128)S(1)}, f32[1,256]{1,0:T(1,128)S(1)}, u32[]{:S(2)}, u32[]{:S(2)}) collective-permute-start(f32[1,256]{1,0:T(1,128)S(1)} %slice.41), channel_id=1, source_target_pairs={{0,16},{1,17},{2,18},{3,19},{4,20},{5,21},{6,22},{7,23},{8,24},{9,... | collective-permute-start | bytes 3080 | tf_op jit(solution)/shard_map/ppermute | solution.py:261
  62.5 4.3 %collective-permute-start.10 = (f32[32,256]{1,0:T(8,128)S(1)}, f32[32,256]{1,0:T(8,128)S(1)}, u32[]{:S(2)}, u32[]{:S(2)}) collective-permute-start(f32[32,256]{1,0:T(8,128)S(1)} %broadcast_multiply_fusion.1.refs_0_), channel_id=1, source_target_pairs={{1,2},{2,1},{3,4},{4,3},{5,6},{6,5},{9,10},{10,9},{11,12},{12,11},... | collective-permute-start | bytes 98312 | tf_op jit(solution)/shard_map/ppermute | solution.py:261
  63.2 5.5 %collective-permute-start.9 = (f32[32,256]{1,0:T(8,128)S(1)}, f32[32,256]{1,0:T(8,128)S(1)}, u32[]{:S(2)}, u32[]{:S(2)}) collective-permute-start(f32[32,256]{1,0:T(8,128)S(1)} %broadcast_multiply_fusion.1.refs_0_), channel_id=1, source_target_pairs={{0,1},{1,0},{2,3},{3,2},{4,5},{5,4},{6,7},{7,6},{8,9},{9,8},{10,11... | collective-permute-start | bytes 98312 | tf_op jit(solution)/shard_map/ppermute | solution.py:261
  69.3 1.3 %collective-permute-start.11 = (f32[32,512]{1,0:T(8,128)S(1)}, f32[32,512]{1,0:T(8,128)S(1)}, u32[]{:S(2)}, u32[]{:S(2)}) collective-permute-start(f32[32,512]{1,0:T(8,128)S(1)} %get-tuple-element.53), channel_id=1, source_target_pairs={{0,8},{1,9},{2,10},{3,11},{4,12},{5,13},{6,14},{7,15},{8,0},{9,1},... | collective-permute-start | bytes 196616 | tf_op jit(solution)/shard_map/ppermute | solution.py:261
  70.6 4.0 %collective-permute-start.12 = (f32[32,256]{1,0:T(8,128)S(1)}, f32[32,256]{1,0:T(8,128)S(1)}, u32[]{:S(2)}, u32[]{:S(2)}) collective-permute-start(f32[32,256]{1,0:T(8,128)S(1)} %slice.43), channel_id=1, source_target_pairs={{0,16},{1,17},{2,18},{3,19},{4,20},{5,21},{6,22},{7,23},{8,24},{9,... | collective-permute-start | bytes 98312 | tf_op jit(solution)/shard_map/ppermute | solution.py:261
  74.6 5.8 %collective-permute-start.14 = (f32[32,256]{1,0:T(8,128)S(1)}, f32[32,256]{1,0:T(8,128)S(1)}, u32[]{:S(2)}, u32[]{:S(2)}) collective-permute-start(f32[32,256]{1,0:T(8,128)S(1)} %get-tuple-element.60.refs_0_), channel_id=1, source_target_pairs={{1,2},{2,1},{3,4},{4,3},{5,6},{6,5},{9,10},{10,9},{11,12},{12,11},... | collective-permute-start | bytes 98312 | tf_op jit(solution)/shard_map/ppermute | solution.py:261
  75.3 7.0 %collective-permute-start.13 = (f32[32,256]{1,0:T(8,128)S(1)}, f32[32,256]{1,0:T(8,128)S(1)}, u32[]{:S(2)}, u32[]{:S(2)}) collective-permute-start(f32[32,256]{1,0:T(8,128)S(1)} %get-tuple-element.60.refs_0_), channel_id=1, source_target_pairs={{0,1},{1,0},{2,3},{3,2},{4,5},{5,4},{6,7},{7,6},{8,9},{9,8},{10,11... | collective-permute-start | bytes 98312 | tf_op jit(solution)/shard_map/ppermute | solution.py:261
  82.9 1.3 %collective-permute-start.15 = (f32[32,512]{1,0:T(8,128)S(1)}, f32[32,512]{1,0:T(8,128)S(1)}, u32[]{:S(2)}, u32[]{:S(2)}) collective-permute-start(f32[32,512]{1,0:T(8,128)S(1)} %get-tuple-element.55), channel_id=1, source_target_pairs={{0,8},{1,9},{2,10},{3,11},{4,12},{5,13},{6,14},{7,15},{8,0},{9,1},... | collective-permute-start | bytes 196616 | tf_op jit(solution)/shard_map/ppermute | solution.py:261
  84.3 4.0 %collective-permute-start.16 = (f32[32,256]{1,0:T(8,128)S(1)}, f32[32,256]{1,0:T(8,128)S(1)}, u32[]{:S(2)}, u32[]{:S(2)}) collective-permute-start(f32[32,256]{1,0:T(8,128)S(1)} %get-tuple-element.64), channel_id=1, source_target_pairs={{0,16},{1,17},{2,18},{3,19},{4,20},{5,21},{6,22},{7,23},{8,24},{9,... | collective-permute-start | bytes 98312 | tf_op jit(solution)/shard_map/ppermute | solution.py:261
  88.5 1.2 %collective-permute-start.17 = (f32[32,128]{1,0:T(8,128)S(1)}, f32[32,128]{1,0:T(8,128)S(1)}, u32[]{:S(2)}, u32[]{:S(2)}) collective-permute-start(f32[32,128]{1,0:T(8,128)S(1)} %get-tuple-element.56), channel_id=1, source_target_pairs={{0,8},{1,9},{2,10},{3,11},{4,12},{5,13},{6,14},{7,15},{8,0},{9,1},... | collective-permute-start | bytes 49160 | tf_op jit(solution)/shard_map/ppermute | solution.py:261
where the time goes:
time: 110 us
  waiting for transfers between devices  43.6 us (40%)
  starting transfers between devices  30.1 us (27%)
  Pallas kernels  16.5 us (15%)
  blocking collectives  14.3 us (13%)
  local copies, waits for them, and re-layouts  4.44 us (4%)
    ppermute x18, waiting for transfers between devices, move(): return lax.ppermute(value, ALL, route[name])  38.3 us
    ppermute x18, starting transfers between devices, move(): return lax.ppermute(value, ALL, route[name])  25.4 us
    pallas_call x13, Pallas kernels, call(): pl.pallas_call(kernel, out_shape=[result(shape, kind) for shape, kind in...  16.5 us
    all_to_all x1, blocking collectives, steps(): parts = lax.all_to_all(copies, ('row', 'inner'), 0, 0)  14.3 us
    all_to_all x1, waiting for transfers between devices, steps(): parts = lax.all_to_all(copies, ALL, 0, 0)  5.3 us
    all_to_all x1, starting transfers between devices, steps(): parts = lax.all_to_all(copies, ALL, 0, 0)  4.72 us
    unnamed x8, local copies, waits for them, and re-layouts  2.56 us
  transfers between devices with their start and end apart: 19, of which 13 were waited for; matrix products, arithmetic and copies ran while one was open for 2% of the time, Pallas kernels for 8%

commit v1 on v0

--- a/solution.py
+++ b/solution.py
@@ -48,67 +48,68 @@
     return jnp.broadcast_to(value, (8, LANES))
 
 
-def eliminate(groups, count):
+def pivot_rows(row_a, row_b, a, b, d, lane, at):
+    row_a = jnp.where(lane == at, 1.0, jnp.where(lane == at + 1, 0.0, row_a))
+    row_b = jnp.where(lane == at, 0.0, jnp.where(lane == at + 1, 1.0, row_b))
+    inverse = 1.0 / (a * d - b * b)
+    a, b, d = a * inverse, b * inverse, d * inverse
+    return d * row_a - b * row_b, a * row_b - b * row_a
+
+
+def eliminate(groups):
     sub = lax.broadcasted_iota(jnp.int32, (8, LANES), 0)
     lane = lax.broadcasted_iota(jnp.int32, (8, LANES), 1)
     g = list(groups)
-    for j in range(0, count, 2):
+    for j in range(0, 8 * len(g), 4):
         q, s = divmod(j, 8)
-        first = [spread(v[:, j:j + 1]) for v in g[q:]]
-        second = [spread(v[:, j + 1:j + 2]) for v in g[q:]]
-        row_a = spread(g[q][s:s + 1, :])
-        row_b = spread(g[q][s + 1:s + 2, :])
-        a = spread(first[0][s:s + 1, :])
-        b = spread(first[0][s + 1:s + 2, :])
-        d = spread(second[0][s + 1:s + 2, :])
-        inverse = 1.0 / (a * d - b * b)
-        left = (d * inverse) * row_a - (b * inverse) * row_b
-        right = (a * inverse) * row_b - (b * inverse) * row_a
+        cols = [[spread(v[:, j + k:j + k + 1]) for v in g[q:]] for k in range(4)]
+        rows = [spread(g[q][s + k:s + k + 1, :]) for k in range(4)]
+        m = [[spread(cols[k][0][s + i:s + i + 1, :]) for k in range(4)] for i in range(4)]
+        first_pair = jnp.logical_or(lane == j, lane == j + 1)
+        last_pair = jnp.logical_or(lane == j + 2, lane == j + 3)
+        w0, w1 = pivot_rows(rows[0], rows[1], m[0][0], m[0][1], m[1][1], lane, j)
+        inverse = 1.0 / (m[0][0] * m[1][1] - m[0][1] * m[0][1])
+        u = [
+            ((m[1][1] * m[0][k] - m[0][1] * m[1][k]) * inverse,
+             (m[0][0] * m[1][k] - m[0][1] * m[0][k]) * inverse)
+            for k in (2, 3)
+        ]
+        third = jnp.where(first_pair, 0.0, rows[2]) - (m[2][0] * w0 + m[2][1] * w1)
+        fourth = jnp.where(first_pair, 0.0, rows[3]) - (m[3][0] * w0 + m[3][1] * w1)
+        a = m[2][2] - (m[2][0] * u[0][0] + m[2][1] * u[0][1])
+        b = m[2][3] - (m[2][0] * u[1][0] + m[2][1] * u[1][1])
+        d = m[3][3] - (m[3][0] * u[1][0] + m[3][1] * u[1][1])
+        w2, w3 = pivot_rows(third, fourth, a, b, d, lane, j + 2)
+        clear_0, clear_1 = jnp.where(last_pair, 0.0, w0), jnp.where(last_pair, 0.0, w1)
+        pair = jnp.logical_or(first_pair, last_pair)
         for i in range(len(g) - q):
-            change = first[i] * left + second[i] * right
+            c0, c1 = cols[0][i], cols[1][i]
+            c2 = cols[2][i] - (c0 * u[0][0] + c1 * u[0][1])
+            c3 = cols[3][i] - (c0 * u[1][0] + c1 * u[1][1])
+            old = g[q + i]
+            new = jnp.where(pair, 0.0, old) - (c0 * clear_0 + c1 * clear_1) - (c2 * w2 + c3 * w3)
             if i == 0:
-                change = jnp.where(sub > s + 1, change, 0.0)
-            g[q + i] = g[q + i] - change
+                new = jnp.where(sub > s + 3, new, old)
+                new = jnp.where(sub == s + 2, third, jnp.where(sub == s + 3, fourth, new))
+            g[q + i] = new
     odd = sub % 2 == 1
     done = []
     for q, v in enumerate(g):
+        row = sub + 8 * q
         above = pltpu.roll(v, 1, 0)
-        at = lane == sub + (8 * q - 1)
+        at = lane == row - 1
         b = jnp.sum(jnp.where(at, v, 0.0), axis=1, keepdims=True)
         a = jnp.sum(jnp.where(at, above, 0.0), axis=1, keepdims=True)
-        v = jnp.where(odd, v - (b / jnp.where(odd, a, 1.0)) * above, v)
-        pivot = jnp.sum(jnp.where(lane == sub + 8 * q, v, 0.0), axis=1, keepdims=True)
+        above = jnp.where(at, 1.0, above)
+        split = jnp.where(at, 0.0, v) - (b / jnp.where(odd, a, 1.0)) * above
+        v = jnp.where(odd, split, v)
+        pivot = jnp.sum(jnp.where(lane == row, v, 0.0), axis=1, keepdims=True)
         done.append(v * lax.rsqrt(pivot))
     return done
 
 
-def eye_lanes(rows, start):
-    row = lax.broadcasted_iota(jnp.int32, (rows, LANES), 0)
-    lane = lax.broadcasted_iota(jnp.int32, (rows, LANES), 1)
-    return jnp.where(lane == row + start, 1.0, 0.0)
-
-
-def start_kernel(weights, rows, start, copies):
-    value = nt(weights[...], rows[...], None)
-    start[...] = value
-    gram = nt(value, value)
-    width = gram.shape[0]
-    packed = jnp.concatenate([gram[8 * q:8 * q + 8, :] for q in range(width // 8)], axis=1)
-    copies[...] = jnp.broadcast_to(packed[None], copies.shape)
-
-
-def first_basis_kernel(parts, start, basis):
-    packed = jnp.sum(parts[...], axis=0)
-    width = start.shape[0]
-    eye = eye_lanes(width, LANES // 2)
-    groups = []
-    for q in range(width // 8):
-        piece = packed[:, width * q:width * (q + 1)]
-        piece = jnp.concatenate([piece, jnp.zeros((8, LANES - width), F32)], axis=1)
-        groups.append(piece + eye[8 * q:8 * q + 8, :])
-    whole = jnp.concatenate(eliminate(groups, width), axis=0)
-    inverse = whole[:, LANES // 2:LANES // 2 + width]
-    basis[...] = nn(inverse, start[...])
+def start_kernel(weights, rows, start):
+    start[...] = nt(weights[...], rows[...], None)
 
 
 def links_kernel(n_inner, place, bins, pairs, hots, links):
@@ -149,8 +150,7 @@
         norms[:, at] = jnp.sum(wide * wide, axis=0, keepdims=True)
 
 
-def tile_kernel(scale, kind, part, other, hots, all_links, norms, degree, turned, *refs):
-    high, low, out = refs[-3:]
+def tile_kernel(scale, kind, part, other, hots, all_links, norms, degree, turned, high, low, out):
     x = other[...]
     wide = x.astype(F32)
     own = jnp.sum(wide * wide, axis=1, keepdims=True)
@@ -188,44 +188,62 @@
     send[...] = total[:, half:]
 
 
-def gram_kernel(mine, got, inv_root, basis, image, image_next, packed):
+def gram_kernel(mine, got, inv_root, start, image, image_next, packed):
     value = inv_root[...] * (mine[...] + got[...])
     image_next[...] = value
-    first = image[...]
-    packed[...] = jnp.concatenate(
-        [nt(basis[...], first), nt(first, first), nt(first, value), nt(value, value)], axis=1
-    )
-
-
-def last_kernel(parts, q0, v1, v2, basis, coefficients):
+    first, begin = image[...], start[...]
+    width = first.shape[0]
+    packed[:width, :] = jnp.concatenate(
+        [nt(begin, first), nt(first, first), nt(first, value), nt(value, value)], axis=1
+    )
+    gram = nt(begin, begin)
+    packed[width:, :] = jnp.concatenate(
+        [gram[8 * i:8 * i + 8, :] for i in range(width // 8)], axis=1
+    )
+
+
+def spread_kernel(mine, got, copies):
+    copies[...] = jnp.broadcast_to((mine[...] + got[...])[None], copies.shape)
+
+
+def last_kernel(parts, v0, v1, v2, basis, coefficients):
     packed = jnp.sum(parts[...], axis=0)
-    width = q0.shape[0]
-    a_0, m_11, m_12, m_22 = [packed[:, width * i:width * (i + 1)] for i in range(4)]
-    left_0 = jnp.concatenate([a_0, m_11], axis=1)
-    cross = tn(left_0, left_0)
-    top = jnp.concatenate([m_11, m_12], axis=1) - cross[:width]
-    low = jnp.concatenate([m_12, m_22], axis=1) - cross[width:]
-    gram = jnp.concatenate([top, low], axis=0)
-    rows = 2 * width
-    gram = jnp.concatenate([gram, jnp.zeros((rows, LANES - rows), F32)], axis=1)
-    gram = gram + eye_lanes(rows, LANES // 2)
-    groups = [gram[8 * q:8 * q + 8, :] for q in range(rows // 8)]
-    whole = jnp.concatenate(eliminate(groups, rows), axis=0)
-    inverse = whole[:, LANES // 2:LANES // 2 + rows]
-    q = q0[...]
-    rest = jnp.concatenate([v1[...], v2[...]], axis=0) - tn(left_0, q)
-    basis[:width, :] = q
-    basis[width:, :] = nn(inverse, rest)
-    row = lax.broadcasted_iota(jnp.int32, (width, width), 0)
-    col = lax.broadcasted_iota(jnp.int32, (width, width), 1)
-    r_11 = jnp.where(col >= row, whole[:width, :width], 0.0)
-    r_12 = whole[:width, width:rows]
-    r_22 = jnp.where(col >= row, whole[width:, width:rows], 0.0)
-    z_11 = inverse[:width, :width]
-    coefficients[0] = a_0
-    coefficients[1] = r_11
-    coefficients[2] = nt(r_12 - nn(r_11, a_0), z_11)
-    coefficients[3] = jnp.where(col >= row, nt(r_22, z_11), 0.0)
+    width = v0.shape[0]
+    m_01, m_11, m_12, m_22 = [packed[:width, width * i:width * (i + 1)] for i in range(4)]
+    m_00 = jnp.concatenate(
+        [packed[width:, width * i:width * (i + 1)] for i in range(width // 8)], axis=0
+    )
+    blank = jnp.zeros((width, LANES - 3 * width), F32)
+    gram = jnp.concatenate(
+        [
+            jnp.concatenate([m_00, m_01, m_11, blank], axis=1),
+            jnp.concatenate([m_01.T, m_11, m_12, blank], axis=1),
+            jnp.concatenate([m_11, m_12.T, m_22, blank], axis=1),
+        ],
+        axis=0,
+    )
+    rows = 3 * width
+    groups = [gram[8 * i:8 * i + 8, :] for i in range(rows // 8)]
+    whole = jnp.concatenate(eliminate(groups), axis=0)[:, :rows]
+    row = lax.broadcasted_iota(jnp.int32, (rows, rows), 0)
+    col = lax.broadcasted_iota(jnp.int32, (rows, rows), 1)
+    upper = jnp.where(col >= row, whole, 0.0)
+    pivot = jnp.sum(jnp.where(col == row, whole, 0.0), axis=1, keepdims=True)
+    inverse = jnp.where(col < row, whole, jnp.where(col == row, 1.0 / pivot, 0.0))
+    basis[...] = nn(inverse, jnp.concatenate([v0[...], v1[...], v2[...]], axis=0))
+
+    def block(value, i, j):
+        return value[width * i:width * (i + 1), width * j:width * (j + 1)]
+
+    z_00, z_11 = block(inverse, 0, 0), block(inverse, 1, 1)
+    r_01, r_11 = block(upper, 0, 1), block(upper, 1, 1)
+    first = nt(jnp.concatenate([r_01, r_11], axis=0), z_00)
+    mixed = block(upper, 1, 2) - nn(r_11, tn(z_00, r_01))
+    second = nt(jnp.concatenate([mixed, block(upper, 2, 2)], axis=0), z_11)
+    coefficients[0] = first[:width]
+    coefficients[1] = first[width:]
+    coefficients[2] = second[:width]
+    coefficients[3] = second[width:]
 
 
 def routes(n_loop, n_inner):
@@ -278,32 +296,20 @@
         scalars=1,
     )
 
-    n_all = n_loop * n_inner
-    start, copies = call(
-        start_kernel,
-        [((width, row_count), F32), ((n_all, 8, width * width // 8), F32)],
-        start_weights.T,
-        snapshots,
-    )
-    parts = lax.all_to_all(copies, ALL, 0, 0)
-    (basis_0,) = call(first_basis_kernel, [((width, row_count), F32)], parts, start)
+    (start,) = call(start_kernel, [((width, row_count), F32)], start_weights.T, snapshots)
 
     span = n_loop * row_count
     turned, norms = call(turn_kernel, [((features, span), BF16), ((1, span), F32)], *group_rows)
     degree = jnp.zeros((1, span), F32)
     tiles = []
-    for kind, part, rows, after in (
-        (0, 0, snapshots, ()),
-        (1, 0, near_a, ()),
-        (1, 1, near_b, (basis_0,)),
-        (2, 0, far_a, ()),
-        (2, 1, far_b, ()),
+    for kind, part, rows in (
+        (0, 0, snapshots), (1, 0, near_a), (1, 1, near_b), (2, 0, far_a), (2, 1, far_b)
     ):
         size = rows.shape[0]
         high, low, degree = call(
             functools.partial(tile_kernel, -3.0 / features, kind, part),
             [((size, span), BF16), ((size, span), BF16), ((1, span), F32)],
-            rows, hots, links, norms, degree, turned, *after,
+            rows, hots, links, norms, degree, turned,
         )
         tiles += [high, low]
 
@@ -323,21 +329,24 @@
         )
         return group_sum(keep, send)
 
-    mine, got = apply(basis_0)
+    mine, got = apply(start)
     image_1 = inv_root * (mine + got)
     mine, got = apply(image_1)
     image_2, packed = call(
         gram_kernel,
-        [((width, row_count), F32), ((width, 4 * width), F32)],
-        mine, got, inv_root, basis_0, image_1,
-    )
-    packed = packed + move(packed, "core")
-    copies = jnp.broadcast_to(packed[None], (n_row * n_inner,) + packed.shape)
+        [((width, row_count), F32), ((width + 8, 4 * width), F32)],
+        mine, got, inv_root, start, image_1,
+    )
+    (copies,) = call(
+        spread_kernel,
+        [((n_row * n_inner,) + packed.shape, F32)],
+        packed, move(packed, "core"),
+    )
     parts = lax.all_to_all(copies, ("row", "inner"), 0, 0)
     basis, coefficients = call(
         last_kernel,
         [((3 * width, row_count), F32), ((4, width, width), F32)],
-        parts, basis_0, image_1, image_2,
+        parts, start, image_1, image_2,
         final=True,
     )
     return basis.T, coefficients

time: 110 us -> 98.8 us (0.90)
  waiting for transfers between devices: 43.6 us -> 35.4 us
  blocking collectives: 14.3 us -> 20.4 us
  starting transfers between devices: 30.1 us -> 25.2 us
  Pallas kernels: 16.5 us -> 12.9 us
    all_to_all x1, blocking collectives: 14.3 us -> 20.4 us  [steps(): parts = lax.all_to_all(copies, ('row', 'inner'), 0, 0)]
    all_to_all x1 -> x0, waiting for transfers between devices: 5.3 us -> none  [steps(): parts = lax.all_to_all(copies, ALL, 0, 0)]
    all_to_all x1 -> x0, starting transfers between devices: 4.72 us -> none  [steps(): parts = lax.all_to_all(copies, ALL, 0, 0)]
    pallas_call x13, Pallas kernels: 16.5 us -> 12.9 us  [call(): pl.pallas_call(kernel, out_shape=[result(shape, kind) for shape, kind in...]
    ppermute x18, waiting for transfers between devices: 38.3 us -> 35.4 us  [move(): return lax.ppermute(value, ALL, route[name])]
  transfers between devices with their start and end apart: 19 -> 18, of which waited for: 13 -> 12; matrix products, arithmetic and copies ran while one was open for 2% -> 2% of each run, Pallas kernels for 8% -> 5%
where the time goes in v1:
time: 98.8 us; the launch traced here: 98.4 us
  waiting for transfers between devices  35.4 us (36%)
  starting transfers between devices  25.2 us (26%)
  blocking collectives  20.4 us (21%)
  Pallas kernels  12.9 us (13%)
  local copies, waits for them, and re-layouts  3.58 us (4%)
    ppermute x18, waiting for transfers between devices, move(): return lax.ppermute(value, ALL, route[name])  35.4 us
    ppermute x18, starting transfers between devices, move(): return lax.ppermute(value, ALL, route[name])  25.2 us
    all_to_all x1, blocking collectives, steps(): parts = lax.all_to_all(copies, ('row', 'inner'), 0, 0)  20.4 us
    pallas_call x13, Pallas kernels, call(): pl.pallas_call(kernel, out_shape=[result(shape, kind) for shape, kind in...  12.9 us
  transfers between devices with their start and end apart: 18, of which 12 were waited for; matrix products, arithmetic and copies ran while one was open for 2% of the time, Pallas kernels for 5%

profile of v1, /device:TPU:0, one launch (start us, length us, event | category | flops | bytes accessed | tf_op | source)
XLA Modules:
  0.0 98.4 jit_solution(5833765103576083168)
XLA Ops:
  0.6 3.1 %collective-permute-start.2 = (bf16[256,1024]{1,0:T(8,128)(2,1)}, bf16[256,1024]{1,0:T(8,128)(2,1)S(1)}, u32[]{:S(2)}, u32[]{:S(2)}) collective-permute-start(bf16[256,1024]{1,0:T(8,128)(2,1)} %rows.1), channel_id=1, source_target_pairs={{0,16},{1,17},{2,18},{3,19},{4,20},{5,21},{6,22},{7,23},{8,24},{9,... | collective-permute-start | bytes 1572872 | tf_op jit(solution)/shard_map/ppermute | solution.py:279
  3.7 12.1 %collective-permute-done.2.r1 = bf16[256,1024]{1,0:T(8,128)(2,1)S(1)} collective-permute-done((bf16[256,1024]{1,0:T(8,128)(2,1)}, bf16[256,1024]{1,0:T(8,128)(2,1)S(1)}, u32[]{:S(2)}, u32[]{:S(2)}) %collective-permute-start.2) | collective-permute-done | bytes 524320 | tf_op jit(solution)/shard_map/ppermute | solution.py:279
  15.8 1.1 %fusion.3 = (bf16[128,1024]{1,0:T(8,128)(2,1)S(1)}, bf16[128,1024]{1,0:T(8,128)(2,1)S(1)}) fusion(bf16[256,1024]{1,0:T(8,128)(2,1)} %rows.1), kind=kLoop, calls=%fused_computation.8 | loop fusion | bytes 1048576 | tf_op jit(solution)/shard_map/slice | solution.py:284
  16.9 1.8 %collective-permute-start.5 = (bf16[128,1024]{1,0:T(8,128)(2,1)S(1)}, bf16[128,1024]{1,0:T(8,128)(2,1)S(1)}, u32[]{:S(2)}, u32[]{:S(2)}) collective-permute-start(bf16[128,1024]{1,0:T(8,128)(2,1)S(1)} %get-tuple-element.58), channel_id=1, source_target_pairs={{0,1},{1,0},{2,3},{3,2},{4,5},{5,4},{6,7},{7,6},{8,9},{9,8},{10,11... | collective-permute-start | bytes 786440 | tf_op jit(solution)/shard_map/ppermute | solution.py:279
  19.0 7.2 %collective-permute-done.5.other = bf16[128,1024]{1,0:T(8,128)(2,1)S(1)} collective-permute-done((bf16[128,1024]{1,0:T(8,128)(2,1)S(1)}, bf16[128,1024]{1,0:T(8,128)(2,1)S(1)}, u32[]{:S(2)}, u32[]{:S(2)}) %collective-permute-start.5) | collective-permute-done | bytes 262176 | tf_op jit(solution)/shard_map/ppermute | solution.py:279
  26.1 3.7 %collective-permute-start.6 = (bf16[128,1024]{1,0:T(8,128)(2,1)S(1)}, bf16[128,1024]{1,0:T(8,128)(2,1)S(1)}, u32[]{:S(2)}, u32[]{:S(2)}) collective-permute-start(bf16[128,1024]{1,0:T(8,128)(2,1)S(1)} %collective-permute-done.5.other), channel_id=1, source_target_pairs={{0,2},{2,4},{3,1},{4,6},{5,3},{7,5},{8,10},{10,12},{11,9},{12,14},... | collective-permute-start | bytes 786440 | tf_op jit(solution)/shard_map/ppermute | solution.py:279
  29.9 1.4 %collective-permute-done.other = bf16[128,1024]{1,0:T(8,128)(2,1)S(1)} collective-permute-done((bf16[128,1024]{1,0:T(8,128)(2,1)S(1)}, bf16[128,1024]{1,0:T(8,128)(2,1)S(1)}, u32[]{:S(2)}, u32[]{:S(2)}) %collective-permute-start) | collective-permute-done | bytes 262176 | tf_op jit(solution)/shard_map/ppermute | solution.py:279
  31.3 3.7 %collective-permute-start.1 = (bf16[128,1024]{1,0:T(8,128)(2,1)S(1)}, bf16[128,1024]{1,0:T(8,128)(2,1)S(1)}, u32[]{:S(2)}, u32[]{:S(2)}) collective-permute-start(bf16[128,1024]{1,0:T(8,128)(2,1)S(1)} %collective-permute-done.other), channel_id=1, source_target_pairs={{0,2},{2,4},{3,1},{4,6},{5,3},{7,5},{8,10},{10,12},{11,9},{12,14},... | collective-permute-start | bytes 786440 | tf_op jit(solution)/shard_map/ppermute | solution.py:279
  35.0 0.8 reshape.7.bins
  35.8 0.7 copy-done.3
  36.5 1.0 %shard_map.59 = (f32[3,8,256]{2,1,0:T(8,128)S(1)}, f32[3,8,1024]{2,1,0:T(8,128)S(1)}) custom-call(s32[2]{0:T(128)S(1)} %compare_select_fusion.place, s32[32,256]{1,0:T(8,128)S(1)} %reshape.7.bins, s32[2,256]{1,0:T(2,128)S(1)} %bitcast.7), custom_call_target="tpu_custom_call" | custom-call | tf_op jit(solution)/shard_map/pallas_call | solution.py:38
  37.6 1.0 %copy-done = bf16[256,1024]{1,0:T(8,128)(2,1)S(1)} copy-done((bf16[256,1024]{1,0:T(8,128)(2,1)S(1)}, bf16[256,1024]{1,0:T(8,128)(2,1)}, u32[]{:S(2)}) %copy-start) | copy-done | bytes 524312
  38.6 0.7 shard_map.60
  39.3 1.2 %shard_map.61 = (bf16[256,1024]{1,0:T(8,128)(2,1)S(1)}, bf16[256,1024]{1,0:T(8,128)(2,1)S(1)}, f32[1,1024]{1,0:T(1,128)S(1)}) custom-call(bf16[256,1024]{1,0:T(8,128)(2,1)S(1)} %copy-done.1, f32[3,8,256]{2,1,0:T(8,128)S(1)} %get-tuple-element.29.hots, f32[3,8,1024]{2,1,0:T(8,128)S(1)} %get-tuple-element.30.all_links, f32[1,1024]{1,0:T(1,128)S(1)} %get-tuple-element.31.norms, ...), custom_call_target="tpu_custom_call" | custom-call | tf_op jit(solution)/shard_map/pallas_call | solution.py:38
  40.5 0.7 shard_map.62
  41.2 0.7 shard_map.63
  43.3 1.1 %collective-permute-done.7 = f32[1,512]{1,0:T(1,128)S(1)} collective-permute-done((f32[1,512]{1,0:T(1,128)S(1)}, f32[1,512]{1,0:T(1,128)S(1)}, u32[]{:S(2)}, u32[]{:S(2)}) %collective-permute-start.7) | collective-permute-done | bytes 2080 | tf_op jit(solution)/shard_map/ppermute | solution.py:279
  44.5 1.5 %collective-permute-start.8 = (f32[1,256]{1,0:T(1,128)S(1)}, f32[1,256]{1,0:T(1,128)S(1)}, u32[]{:S(2)}, u32[]{:S(2)}) collective-permute-start(f32[1,256]{1,0:T(1,128)S(1)} %slice.41), channel_id=1, source_target_pairs={{0,16},{1,17},{2,18},{3,19},{4,20},{5,21},{6,22},{7,23},{8,24},{9,... | collective-permute-start | bytes 3080 | tf_op jit(solution)/shard_map/ppermute | solution.py:279
  46.2 1.8 %collective-permute-done.8 = f32[1,256]{1,0:T(1,128)S(1)} collective-permute-done((f32[1,256]{1,0:T(1,128)S(1)}, f32[1,256]{1,0:T(1,128)S(1)}, u32[]{:S(2)}, u32[]{:S(2)}) %collective-permute-start.8) | collective-permute-done | bytes 1056 | tf_op jit(solution)/shard_map/ppermute | solution.py:279
  48.7 4.4 %collective-permute-start.9 = (f32[32,256]{1,0:T(8,128)S(1)}, f32[32,256]{1,0:T(8,128)S(1)}, u32[]{:S(2)}, u32[]{:S(2)}) collective-permute-start(f32[32,256]{1,0:T(8,128)S(1)} %broadcast_multiply_fusion.1.refs_0_), channel_id=1, source_target_pairs={{0,1},{1,0},{2,3},{3,2},{4,5},{5,4},{6,7},{7,6},{8,9},{9,8},{10,11... | collective-permute-start | bytes 98312 | tf_op jit(solution)/shard_map/ppermute | solution.py:279
  53.1 1.9 %collective-permute-done.9.refs_1_ = f32[32,256]{1,0:T(8,128)S(1)} collective-permute-done((f32[32,256]{1,0:T(8,128)S(1)}, f32[32,256]{1,0:T(8,128)S(1)}, u32[]{:S(2)}, u32[]{:S(2)}) %collective-permute-start.9) | collective-permute-done | bytes 32800 | tf_op jit(solution)/shard_map/ppermute | solution.py:279
  55.7 1.2 %collective-permute-done.11 = f32[32,512]{1,0:T(8,128)S(1)} collective-permute-done((f32[32,512]{1,0:T(8,128)S(1)}, f32[32,512]{1,0:T(8,128)S(1)}, u32[]{:S(2)}, u32[]{:S(2)}) %collective-permute-start.11) | collective-permute-done | bytes 65568 | tf_op jit(solution)/shard_map/ppermute | solution.py:279
  56.9 1.6 %collective-permute-start.12 = (f32[32,256]{1,0:T(8,128)S(1)}, f32[32,256]{1,0:T(8,128)S(1)}, u32[]{:S(2)}, u32[]{:S(2)}) collective-permute-start(f32[32,256]{1,0:T(8,128)S(1)} %slice.43), channel_id=1, source_target_pairs={{0,16},{1,17},{2,18},{3,19},{4,20},{5,21},{6,22},{7,23},{8,24},{9,... | collective-permute-start | bytes 98312 | tf_op jit(solution)/shard_map/ppermute | solution.py:279
  58.5 2.4 %collective-permute-done.12 = f32[32,256]{1,0:T(8,128)S(1)} collective-permute-done((f32[32,256]{1,0:T(8,128)S(1)}, f32[32,256]{1,0:T(8,128)S(1)}, u32[]{:S(2)}, u32[]{:S(2)}) %collective-permute-start.12) | collective-permute-done | bytes 32800 | tf_op jit(solution)/shard_map/ppermute | solution.py:279
  60.9 2.1 %collective-permute-start.13 = (f32[32,256]{1,0:T(8,128)S(1)}, f32[32,256]{1,0:T(8,128)S(1)}, u32[]{:S(2)}, u32[]{:S(2)}) collective-permute-start(f32[32,256]{1,0:T(8,128)S(1)} %get-tuple-element.56.refs_0_), channel_id=1, source_target_pairs={{0,1},{1,0},{2,3},{3,2},{4,5},{5,4},{6,7},{7,6},{8,9},{9,8},{10,11... | collective-permute-start | bytes 98312 | tf_op jit(solution)/shard_map/ppermute | solution.py:279
  63.7 1.2 %collective-permute-done.13.refs_1_ = f32[32,256]{1,0:T(8,128)S(1)} collective-permute-done((f32[32,256]{1,0:T(8,128)S(1)}, f32[32,256]{1,0:T(8,128)S(1)}, u32[]{:S(2)}, u32[]{:S(2)}) %collective-permute-start.13) | collective-permute-done | bytes 32800 | tf_op jit(solution)/shard_map/ppermute | solution.py:279
  65.6 1.2 %collective-permute-done.15 = f32[32,512]{1,0:T(8,128)S(1)} collective-permute-done((f32[32,512]{1,0:T(8,128)S(1)}, f32[32,512]{1,0:T(8,128)S(1)}, u32[]{:S(2)}, u32[]{:S(2)}) %collective-permute-start.15) | collective-permute-done | bytes 65568 | tf_op jit(solution)/shard_map/ppermute | solution.py:279
  66.9 1.6 %collective-permute-start.16 = (f32[32,256]{1,0:T(8,128)S(1)}, f32[32,256]{1,0:T(8,128)S(1)}, u32[]{:S(2)}, u32[]{:S(2)}) collective-permute-start(f32[32,256]{1,0:T(8,128)S(1)} %get-tuple-element.60), channel_id=1, source_target_pairs={{0,16},{1,17},{2,18},{3,19},{4,20},{5,21},{6,22},{7,23},{8,24},{9,... | collective-permute-start | bytes 98312 | tf_op jit(solution)/shard_map/ppermute | solution.py:279
  68.4 2.4 %collective-permute-done.16.got = f32[32,256]{1,0:T(8,128)S(1)} collective-permute-done((f32[32,256]{1,0:T(8,128)S(1)}, f32[32,256]{1,0:T(8,128)S(1)}, u32[]{:S(2)}, u32[]{:S(2)}) %collective-permute-start.16) | collective-permute-done | bytes 32800 | tf_op jit(solution)/shard_map/ppermute | solution.py:279
  71.3 1.2 %collective-permute-done.17.got = f32[40,128]{1,0:T(8,128)S(1)} collective-permute-done((f32[40,128]{1,0:T(8,128)S(1)}, f32[40,128]{1,0:T(8,128)S(1)}, u32[]{:S(2)}, u32[]{:S(2)}) %collective-permute-start.17) | collective-permute-done | bytes 20512 | tf_op jit(solution)/shard_map/ppermute | solution.py:279
  72.5 20.4 %all_to_all.5.parts = f32[16,40,128]{2,1,0:T(8,128)S(1)} all-to-all(f32[16,40,128]{2,1,0:T(8,128)S(1)} %shard_map.70), channel_id=1, replica_groups=mesh['row'=2,'core'=2,'inner'=8] {'row','inner'}, dimensions={0} | all-to-all | bytes 655360 | tf_op jit(solution)/shard_map/all_to_all | solution.py:345
  92.9 5.5 %shard_map.71 = (f32[96,256]{1,0:T(8,128)}, f32[4,32,32]{2,1,0:T(8,128)}) custom-call(f32[16,40,128]{2,1,0:T(8,128)S(1)} %all_to_all.5.parts, f32[32,256]{1,0:T(8,128)S(1)} %shard_map.66.start.v0, f32[32,256]{1,0:T(8,128)S(1)} %get-tuple-element.57.image.v1, f32[32,256]{1,0:T(8,128)S(1)} %get-tuple-element.53.v2), custom_call_target="tpu_custom_call" | custom-call | tf_op jit(solution)/shard_map/pallas_call | solution.py:38
  (40 shorter events, 5.1 us)
Async XLA Ops:
  0.6 38.6 %copy-start.1 = (bf16[256,1024]{1,0:T(8,128)(2,1)S(1)}, bf16[256,1024]{1,0:T(8,128)(2,1)}, u32[]{:S(2)}) copy-start(bf16[256,1024]{1,0:T(8,128)(2,1)} %rows.1) | copy-start | bytes 1572868
  0.6 15.2 %collective-permute-start.2 = (bf16[256,1024]{1,0:T(8,128)(2,1)}, bf16[256,1024]{1,0:T(8,128)(2,1)S(1)}, u32[]{:S(2)}, u32[]{:S(2)}) collective-permute-start(bf16[256,1024]{1,0:T(8,128)(2,1)} %rows.1), channel_id=1, source_target_pairs={{0,16},{1,17},{2,18},{3,19},{4,20},{5,21},{6,22},{7,23},{8,24},{9,... | collective-permute-start | bytes 1572872 | tf_op jit(solution)/shard_map/ppermute | solution.py:279
  3.7 33.8 %collective-permute-start.3 = (bf16[256,1024]{1,0:T(8,128)(2,1)}, bf16[256,1024]{1,0:T(8,128)(2,1)S(1)}, u32[]{:S(2)}, u32[]{:S(2)}) collective-permute-start(bf16[256,1024]{1,0:T(8,128)(2,1)} %rows.1), channel_id=1, source_target_pairs={{0,8},{1,9},{2,10},{3,11},{4,12},{5,13},{6,14},{7,15},{8,0},{9,1},... | collective-permute-start | bytes 1572872 | tf_op jit(solution)/shard_map/ppermute | solution.py:279
  15.8 21.7 %collective-permute-start.4 = (bf16[256,1024]{1,0:T(8,128)(2,1)S(1)}, bf16[256,1024]{1,0:T(8,128)(2,1)S(1)}, u32[]{:S(2)}, u32[]{:S(2)}) collective-permute-start(bf16[256,1024]{1,0:T(8,128)(2,1)S(1)} %collective-permute-done.2.r1), channel_id=1, source_target_pairs={{0,8},{1,9},{2,10},{3,11},{4,12},{5,13},{6,14},{7,15},{8,0},{9,1},... | collective-permute-start | bytes 1572872 | tf_op jit(solution)/shard_map/ppermute | solution.py:279
  16.9 9.2 %collective-permute-start.5 = (bf16[128,1024]{1,0:T(8,128)(2,1)S(1)}, bf16[128,1024]{1,0:T(8,128)(2,1)S(1)}, u32[]{:S(2)}, u32[]{:S(2)}) collective-permute-start(bf16[128,1024]{1,0:T(8,128)(2,1)S(1)} %get-tuple-element.58), channel_id=1, source_target_pairs={{0,1},{1,0},{2,3},{3,2},{4,5},{5,4},{6,7},{7,6},{8,9},{9,8},{10,11... | collective-permute-start | bytes 786440 | tf_op jit(solution)/shard_map/ppermute | solution.py:279
  18.7 12.6 %collective-permute-start = (bf16[128,1024]{1,0:T(8,128)(2,1)S(1)}, bf16[128,1024]{1,0:T(8,128)(2,1)S(1)}, u32[]{:S(2)}, u32[]{:S(2)}) collective-permute-start(bf16[128,1024]{1,0:T(8,128)(2,1)S(1)} %get-tuple-element.59), channel_id=1, source_target_pairs={{0,1},{1,0},{2,3},{3,2},{4,5},{5,4},{6,7},{7,6},{8,9},{9,8},{10,11... | collective-permute-start | bytes 786440 | tf_op jit(solution)/shard_map/ppermute | solution.py:279
  26.1 15.7 %collective-permute-start.6 = (bf16[128,1024]{1,0:T(8,128)(2,1)S(1)}, bf16[128,1024]{1,0:T(8,128)(2,1)S(1)}, u32[]{:S(2)}, u32[]{:S(2)}) collective-permute-start(bf16[128,1024]{1,0:T(8,128)(2,1)S(1)} %collective-permute-done.5.other), channel_id=1, source_target_pairs={{0,2},{2,4},{3,1},{4,6},{5,3},{7,5},{8,10},{10,12},{11,9},{12,14},... | collective-permute-start | bytes 786440 | tf_op jit(solution)/shard_map/ppermute | solution.py:279
  31.3 11.2 %collective-permute-start.1 = (bf16[128,1024]{1,0:T(8,128)(2,1)S(1)}, bf16[128,1024]{1,0:T(8,128)(2,1)S(1)}, u32[]{:S(2)}, u32[]{:S(2)}) collective-permute-start(bf16[128,1024]{1,0:T(8,128)(2,1)S(1)} %collective-permute-done.other), channel_id=1, source_target_pairs={{0,2},{2,4},{3,1},{4,6},{5,3},{7,5},{8,10},{10,12},{11,9},{12,14},... | collective-permute-start | bytes 786440 | tf_op jit(solution)/shard_map/ppermute | solution.py:279
  35.8 0.7 copy-start.3
  37.5 1.0 %copy-start = (bf16[256,1024]{1,0:T(8,128)(2,1)S(1)}, bf16[256,1024]{1,0:T(8,128)(2,1)}, u32[]{:S(2)}) copy-start(bf16[256,1024]{1,0:T(8,128)(2,1)} %rows.1) | copy-start | bytes 1572868
  41.9 4.1 %copy-start.2 = (bf16[1024,32]{0,1:T(8,128)(2,1)S(1)}, bf16[1024,32]{0,1:T(8,128)(2,1)}, u32[]{:S(2)}) copy-start(bf16[1024,32]{0,1:T(8,128)(2,1)} %param.7) | copy-start | bytes 196612
  43.2 1.2 %collective-permute-start.7 = (f32[1,512]{1,0:T(1,128)S(1)}, f32[1,512]{1,0:T(1,128)S(1)}, u32[]{:S(2)}, u32[]{:S(2)}) collective-permute-start(f32[1,512]{1,0:T(1,128)S(1)} %slice.33), channel_id=1, source_target_pairs={{0,8},{1,9},{2,10},{3,11},{4,12},{5,13},{6,14},{7,15},{8,0},{9,1},... | collective-permute-start | bytes 6152 | tf_op jit(solution)/shard_map/ppermute | solution.py:279
  44.5 3.6 %collective-permute-start.8 = (f32[1,256]{1,0:T(1,128)S(1)}, f32[1,256]{1,0:T(1,128)S(1)}, u32[]{:S(2)}, u32[]{:S(2)}) collective-permute-start(f32[1,256]{1,0:T(1,128)S(1)} %slice.41), channel_id=1, source_target_pairs={{0,16},{1,17},{2,18},{3,19},{4,20},{5,21},{6,22},{7,23},{8,24},{9,... | collective-permute-start | bytes 3080 | tf_op jit(solution)/shard_map/ppermute | solution.py:279
  48.1 5.0 %collective-permute-start.10 = (f32[32,256]{1,0:T(8,128)S(1)}, f32[32,256]{1,0:T(8,128)S(1)}, u32[]{:S(2)}, u32[]{:S(2)}) collective-permute-start(f32[32,256]{1,0:T(8,128)S(1)} %broadcast_multiply_fusion.1.refs_0_), channel_id=1, source_target_pairs={{1,2},{2,1},{3,4},{4,3},{5,6},{6,5},{9,10},{10,9},{11,12},{12,11},... | collective-permute-start | bytes 98312 | tf_op jit(solution)/shard_map/ppermute | solution.py:279
  48.7 6.2 %collective-permute-start.9 = (f32[32,256]{1,0:T(8,128)S(1)}, f32[32,256]{1,0:T(8,128)S(1)}, u32[]{:S(2)}, u32[]{:S(2)}) collective-permute-start(f32[32,256]{1,0:T(8,128)S(1)} %broadcast_multiply_fusion.1.refs_0_), channel_id=1, source_target_pairs={{0,1},{1,0},{2,3},{3,2},{4,5},{5,4},{6,7},{7,6},{8,9},{9,8},{10,11... | collective-permute-start | bytes 98312 | tf_op jit(solution)/shard_map/ppermute | solution.py:279
  55.6 1.3 %collective-permute-start.11 = (f32[32,512]{1,0:T(8,128)S(1)}, f32[32,512]{1,0:T(8,128)S(1)}, u32[]{:S(2)}, u32[]{:S(2)}) collective-permute-start(f32[32,512]{1,0:T(8,128)S(1)} %get-tuple-element.49), channel_id=1, source_target_pairs={{0,8},{1,9},{2,10},{3,11},{4,12},{5,13},{6,14},{7,15},{8,0},{9,1},... | collective-permute-start | bytes 196616 | tf_op jit(solution)/shard_map/ppermute | solution.py:279
  56.9 4.0 %collective-permute-start.12 = (f32[32,256]{1,0:T(8,128)S(1)}, f32[32,256]{1,0:T(8,128)S(1)}, u32[]{:S(2)}, u32[]{:S(2)}) collective-permute-start(f32[32,256]{1,0:T(8,128)S(1)} %slice.43), channel_id=1, source_target_pairs={{0,16},{1,17},{2,18},{3,19},{4,20},{5,21},{6,22},{7,23},{8,24},{9,... | collective-permute-start | bytes 98312 | tf_op jit(solution)/shard_map/ppermute | solution.py:279
  60.9 4.0 %collective-permute-start.13 = (f32[32,256]{1,0:T(8,128)S(1)}, f32[32,256]{1,0:T(8,128)S(1)}, u32[]{:S(2)}, u32[]{:S(2)}) collective-permute-start(f32[32,256]{1,0:T(8,128)S(1)} %get-tuple-element.56.refs_0_), channel_id=1, source_target_pairs={{0,1},{1,0},{2,3},{3,2},{4,5},{5,4},{6,7},{7,6},{8,9},{9,8},{10,11... | collective-permute-start | bytes 98312 | tf_op jit(solution)/shard_map/ppermute | solution.py:279
  63.0 1.9 %collective-permute-start.14 = (f32[32,256]{1,0:T(8,128)S(1)}, f32[32,256]{1,0:T(8,128)S(1)}, u32[]{:S(2)}, u32[]{:S(2)}) collective-permute-start(f32[32,256]{1,0:T(8,128)S(1)} %get-tuple-element.56.refs_0_), channel_id=1, source_target_pairs={{1,2},{2,1},{3,4},{4,3},{5,6},{6,5},{9,10},{10,9},{11,12},{12,11},... | collective-permute-start | bytes 98312 | tf_op jit(solution)/shard_map/ppermute | solution.py:279
  65.5 1.3 %collective-permute-start.15 = (f32[32,512]{1,0:T(8,128)S(1)}, f32[32,512]{1,0:T(8,128)S(1)}, u32[]{:S(2)}, u32[]{:S(2)}) collective-permute-start(f32[32,512]{1,0:T(8,128)S(1)} %get-tuple-element.51), channel_id=1, source_target_pairs={{0,8},{1,9},{2,10},{3,11},{4,12},{5,13},{6,14},{7,15},{8,0},{9,1},... | collective-permute-start | bytes 196616 | tf_op jit(solution)/shard_map/ppermute | solution.py:279
  66.9 4.0 %collective-permute-start.16 = (f32[32,256]{1,0:T(8,128)S(1)}, f32[32,256]{1,0:T(8,128)S(1)}, u32[]{:S(2)}, u32[]{:S(2)}) collective-permute-start(f32[32,256]{1,0:T(8,128)S(1)} %get-tuple-element.60), channel_id=1, source_target_pairs={{0,16},{1,17},{2,18},{3,19},{4,20},{5,21},{6,22},{7,23},{8,24},{9,... | collective-permute-start | bytes 98312 | tf_op jit(solution)/shard_map/ppermute | solution.py:279
  71.2 1.2 %collective-permute-start.17 = (f32[40,128]{1,0:T(8,128)S(1)}, f32[40,128]{1,0:T(8,128)S(1)}, u32[]{:S(2)}, u32[]{:S(2)}) collective-permute-start(f32[40,128]{1,0:T(8,128)S(1)} %get-tuple-element.52.mine), channel_id=1, source_target_pairs={{0,8},{1,9},{2,10},{3,11},{4,12},{5,13},{6,14},{7,15},{8,0},{9,1},... | collective-permute-start | bytes 61448 | tf_op jit(solution)/shard_map/ppermute | solution.py:279

commit v2 on v1

--- a/solution.py
+++ b/solution.py
@@ -108,10 +108,6 @@
     return done
 
 
-def start_kernel(weights, rows, start):
-    start[...] = nt(weights[...], rows[...], None)
-
-
 def links_kernel(n_inner, place, bins, pairs, hots, links):
     column, group = place[0], place[1]
     odd = column % 2
@@ -126,7 +122,7 @@
         return bins[pl.ds(l * n_inner + c, 1), :]
 
     rows = jnp.concatenate(
-        [hot(bins_at(group ^ r, column), column * BINS_COL) for r in (0, 2, 1, 3)], axis=1
+        [hot(bins_at(group ^ r, column), column * BINS_COL) for r in range(4)], axis=1
     )
     left, right = pairs[0:1, :], pairs[1:2, :]
     base = column * BINS_COL
@@ -140,30 +136,56 @@
         hots[i] = hot(theirs, base)
 
 
-def turn_kernel(r0, r1, r2, r3, turned, norms):
+def turn_kernel(weights, r0, r1, turned, norms, start):
     span = r0.shape[0]
-    for i, rows in enumerate((r0, r1, r2, r3)):
+    for i, rows in enumerate((r0, r1)):
         at = slice(i * span, (i + 1) * span)
         value = rows[...].T
         turned[:, at] = value
         wide = value.astype(F32)
         norms[:, at] = jnp.sum(wide * wide, axis=0, keepdims=True)
-
-
-def tile_kernel(scale, kind, part, other, hots, all_links, norms, degree, turned, high, low, out):
+        start[:, at] = nn(weights[...], value, None)
+
+
+def tile_kernel(scale, kind, part, other, hots, all_links, *refs):
+    groups, (high, low, out) = refs[:4], refs[-3:]
+    first = len(refs) == 7
     x = other[...]
     wide = x.astype(F32)
     own = jnp.sum(wide * wide, axis=1, keepdims=True)
     size = x.shape[0]
-    hot = hots[kind, :, part * size:(part + 1) * size]
-    mask = nn(hot.T, all_links[kind], None)
-    products = nn(x, turned[...], None)
-    distance = own + norms[...] - 2.0 * products
-    value = mask * jnp.exp(distance * scale)
-    top = value.astype(BF16)
-    high[...] = top
-    low[...] = (value - top.astype(F32)).astype(BF16)
-    out[...] = degree[...] + jnp.sum(value, axis=0, keepdims=True)
+    hot = hots[kind, :, part * size:(part + 1) * size].T
+    span = groups[0].shape[1]
+    for i in range(2):
+        turned, norms = groups[2 * i:2 * i + 2]
+        at = slice(i * span, (i + 1) * span)
+        mask = nn(hot, all_links[kind, :, at], None)
+        distance = own + norms[...] - 2.0 * nn(x, turned[...], None)
+        value = mask * jnp.exp(distance * scale)
+        top = value.astype(BF16)
+        high[:, at] = top
+        low[:, at] = (value - top.astype(F32)).astype(BF16)
+        total = jnp.sum(value, axis=0, keepdims=True)
+        out[:, at] = total if first else refs[4][:, at] + total
+
+
+def send_back_kernel(degree, got, start_a, start_b, *refs):
+    tiles, (inv_root, own, near, far) = refs[:-4], refs[-4:]
+    width, size = own.shape
+    other = jnp.concatenate([got[:, size * i:size * (i + 1)] for i in (2, 3, 0, 1)], axis=1)
+    scale = lax.rsqrt(degree[...] + other)
+    inv_root[...] = scale[:, :size]
+    vectors = (jnp.concatenate([start_a[...], start_b[...]], axis=1) * scale).T
+    top = vectors.astype(BF16)
+    low = (vectors - top.astype(F32)).astype(BF16)
+    both = jnp.concatenate([top, low], axis=1)
+    pieces = []
+    for i in range(len(tiles) // 2):
+        piece = nn(tiles[2 * i][...], both, None)
+        pieces.append(piece[:, :width] + piece[:, width:] + nn(tiles[2 * i + 1][...], top, None))
+    own[...] = pieces[0].T
+    near[...] = jnp.concatenate(pieces[1:3], axis=0).T
+    far[...] = jnp.concatenate(pieces[3:5], axis=0).T
 
 
 def apply_kernel(*refs):
@@ -184,8 +206,9 @@
         piece = piece[:width] + piece[width:] + nn(top[:, at:at + size], low_tile, None)
         total = piece if total is None else total + piece
         at += size
-    keep[...] = total[:, :half]
-    send[...] = total[:, half:]
+    size = half // 2
+    keep[:, :size], keep[:, size:] = total[:, :size], total[:, half:half + size]
+    send[:, :size], send[:, size:] = total[:, size:half], total[:, half + size:]
 
 
 def gram_kernel(mine, got, inv_root, start, image, image_next, packed):
@@ -286,7 +309,6 @@
     far_a = move(near_a, "relay")
     far_b = move(near_b, "relay")
     across_mate = move(across, "core")
-    group_rows = (snapshots, across, mate, across_mate)
 
     place = jnp.where(jnp.arange(2) == 0, column, group).astype(jnp.int32)
     hots, links = call(
@@ -296,42 +318,47 @@
         scalars=1,
     )
 
-    (start,) = call(start_kernel, [((width, row_count), F32)], start_weights.T, snapshots)
-
     span = n_loop * row_count
-    turned, norms = call(turn_kernel, [((features, span), BF16), ((1, span), F32)], *group_rows)
-    degree = jnp.zeros((1, span), F32)
+    turn_outs = [((features, span // 2), BF16), ((1, span // 2), F32), ((width, span // 2), F32)]
+    turned_a, norms_a, start_a = call(
+        turn_kernel, turn_outs, start_weights.T, snapshots, mate
+    )
+    turned_b, norms_b, start_b = call(turn_kernel, turn_outs, start_weights.T, across, across_mate)
     tiles = []
+    degree = ()
     for kind, part, rows in (
         (0, 0, snapshots), (1, 0, near_a), (1, 1, near_b), (2, 0, far_a), (2, 1, far_b)
     ):
         size = rows.shape[0]
-        high, low, degree = call(
+        high, low, *degree = call(
             functools.partial(tile_kernel, -3.0 / features, kind, part),
             [((size, span), BF16), ((size, span), BF16), ((1, span), F32)],
-            rows, hots, links, norms, degree, turned,
+            rows, hots, links, turned_a, norms_a, turned_b, norms_b, *degree,
         )
         tiles += [high, low]
-
-    def group_sum(keep, send):
-        keep = keep + move(send, "core")
-        return keep[:, :row_count], move(keep[:, row_count:], "row")
-
-    mine, got = group_sum(degree[:, :span // 2], degree[:, span // 2:])
-    inv_root = lax.rsqrt(mine + got)
-
-    def apply(vectors):
-        scaled = inv_root * vectors
-        keep, send = call(
-            apply_kernel,
-            [((width, span // 2), F32)] * 2,
-            scaled, move(scaled, "near"), move(scaled, "far"), *tiles,
-        )
-        return group_sum(keep, send)
-
-    mine, got = apply(start)
-    image_1 = inv_root * (mine + got)
-    mine, got = apply(image_1)
+    (degree,) = degree
+
+    got = move(degree, "core")
+    degree = degree + jnp.concatenate(
+        [got[:, row_count * i:row_count * (i + 1)] for i in (1, 0, 3, 2)], axis=1
+    )
+    block = ((width, row_count), F32)
+    inv_root, own, near, far = call(
+        send_back_kernel,
+        [((1, row_count), F32), block, block, block],
+        degree, move(degree, "row"), start_a, start_b, *tiles,
+    )
+    start = start_a[:, :row_count]
+    image_1 = inv_root * (own + move(near, "near") + move(far, "far"))
+
+    scaled = inv_root * image_1
+    keep, send = call(
+        apply_kernel,
+        [((width, span // 2), F32)] * 2,
+        scaled, move(scaled, "near"), move(scaled, "far"), *tiles,
+    )
+    keep = keep + move(send, "core")
+    mine, got = keep[:, :row_count], move(keep[:, row_count:], "row")
     image_2, packed = call(
         gram_kernel,
         [((width, row_count), F32), ((width + 8, 4 * width), F32)],

time: 98.8 us -> 93.7 us (0.948)
  waiting for transfers between devices: 35.4 us -> 31.9 us
  local copies, waits for them, and re-layouts: 3.58 us -> 1.78 us
  starting transfers between devices: 25.2 us -> 23.9 us
    ppermute x18 -> x16, waiting for transfers between devices: 35.4 us -> 31.9 us  [move(): return lax.ppermute(value, ALL, route[name])]
    ppermute x18 -> x16, starting transfers between devices: 25.2 us -> 23.9 us  [move(): return lax.ppermute(value, ALL, route[name])]
    unnamed x8, local copies, waits for them, and re-layouts: 1.73 us -> 0.68 us
  transfers between devices with their start and end apart: 18 -> 16, of which waited for: 12 -> 10; matrix products, arithmetic and copies ran while one was open for 2% -> 1% of each run, Pallas kernels for 5% -> 6%
where the time goes in v2:
time: 93.7 us; the launch traced here: 93.4 us
  waiting for transfers between devices  31.9 us (34%)
  starting transfers between devices  23.9 us (26%)
  blocking collectives  21.2 us (23%)
  Pallas kernels  13.7 us (15%)
  local copies, waits for them, and re-layouts  1.78 us (2%)
    ppermute x16, waiting for transfers between devices, move(): return lax.ppermute(value, ALL, route[name])  31.9 us
    ppermute x16, starting transfers between devices, move(): return lax.ppermute(value, ALL, route[name])  23.9 us
    all_to_all x1, blocking collectives, steps(): parts = lax.all_to_all(copies, ('row', 'inner'), 0, 0)  21.2 us
    pallas_call x13, Pallas kernels, call(): pl.pallas_call(kernel, out_shape=[result(shape, kind) for shape, kind in...  13.7 us
  transfers between devices with their start and end apart: 16, of which 10 were waited for; matrix products, arithmetic and copies ran while one was open for 1% of the time, Pallas kernels for 6%

profile of v2, /device:TPU:0, one launch (start us, length us, event | category | flops | bytes accessed | tf_op | source)
XLA Modules:
  0.0 93.4 jit_solution(9651812759113339036)
XLA Ops:
  0.6 3.1 %collective-permute-start.3 = (bf16[256,1024]{1,0:T(8,128)(2,1)}, bf16[256,1024]{1,0:T(8,128)(2,1)S(1)}, u32[]{:S(2)}, u32[]{:S(2)}) collective-permute-start(bf16[256,1024]{1,0:T(8,128)(2,1)} %other.1), channel_id=1, source_target_pairs={{0,16},{1,17},{2,18},{3,19},{4,20},{5,21},{6,22},{7,23},{8,24},{9,... | collective-permute-start | bytes 1572872 | tf_op jit(solution)/shard_map/ppermute | solution.py:302
  3.7 12.1 %collective-permute-done.3.r0 = bf16[256,1024]{1,0:T(8,128)(2,1)S(1)} collective-permute-done((bf16[256,1024]{1,0:T(8,128)(2,1)}, bf16[256,1024]{1,0:T(8,128)(2,1)S(1)}, u32[]{:S(2)}, u32[]{:S(2)}) %collective-permute-start.3) | collective-permute-done | bytes 524320 | tf_op jit(solution)/shard_map/ppermute | solution.py:302
  15.8 1.1 %fusion = (bf16[128,1024]{1,0:T(8,128)(2,1)S(1)}, bf16[128,1024]{1,0:T(8,128)(2,1)S(1)}) fusion(bf16[256,1024]{1,0:T(8,128)(2,1)} %other.1), kind=kLoop, calls=%fused_computation.4 | loop fusion | bytes 1048576 | tf_op jit(solution)/shard_map/slice | solution.py:307
  16.9 1.8 %collective-permute-start.5 = (bf16[128,1024]{1,0:T(8,128)(2,1)S(1)}, bf16[128,1024]{1,0:T(8,128)(2,1)S(1)}, u32[]{:S(2)}, u32[]{:S(2)}) collective-permute-start(bf16[128,1024]{1,0:T(8,128)(2,1)S(1)} %get-tuple-element.70), channel_id=1, source_target_pairs={{0,1},{1,0},{2,3},{3,2},{4,5},{5,4},{6,7},{7,6},{8,9},{9,8},{10,11... | collective-permute-start | bytes 786440 | tf_op jit(solution)/shard_map/ppermute | solution.py:302
  19.0 7.2 %collective-permute-done.5.other = bf16[128,1024]{1,0:T(8,128)(2,1)S(1)} collective-permute-done((bf16[128,1024]{1,0:T(8,128)(2,1)S(1)}, bf16[128,1024]{1,0:T(8,128)(2,1)S(1)}, u32[]{:S(2)}, u32[]{:S(2)}) %collective-permute-start.5) | collective-permute-done | bytes 262176 | tf_op jit(solution)/shard_map/ppermute | solution.py:302
  26.2 3.7 %collective-permute-start.6 = (bf16[128,1024]{1,0:T(8,128)(2,1)S(1)}, bf16[128,1024]{1,0:T(8,128)(2,1)S(1)}, u32[]{:S(2)}, u32[]{:S(2)}) collective-permute-start(bf16[128,1024]{1,0:T(8,128)(2,1)S(1)} %collective-permute-done.5.other), channel_id=1, source_target_pairs={{0,2},{2,4},{3,1},{4,6},{5,3},{7,5},{8,10},{10,12},{11,9},{12,14},... | collective-permute-start | bytes 786440 | tf_op jit(solution)/shard_map/ppermute | solution.py:302
  29.9 1.4 %collective-permute-done.other = bf16[128,1024]{1,0:T(8,128)(2,1)S(1)} collective-permute-done((bf16[128,1024]{1,0:T(8,128)(2,1)S(1)}, bf16[128,1024]{1,0:T(8,128)(2,1)S(1)}, u32[]{:S(2)}, u32[]{:S(2)}) %collective-permute-start) | collective-permute-done | bytes 262176 | tf_op jit(solution)/shard_map/ppermute | solution.py:302
  31.3 3.7 %collective-permute-start.1 = (bf16[128,1024]{1,0:T(8,128)(2,1)S(1)}, bf16[128,1024]{1,0:T(8,128)(2,1)S(1)}, u32[]{:S(2)}, u32[]{:S(2)}) collective-permute-start(bf16[128,1024]{1,0:T(8,128)(2,1)S(1)} %collective-permute-done.other), channel_id=1, source_target_pairs={{0,2},{2,4},{3,1},{4,6},{5,3},{7,5},{8,10},{10,12},{11,9},{12,14},... | collective-permute-start | bytes 786440 | tf_op jit(solution)/shard_map/ppermute | solution.py:302
  35.1 0.7 copy-done.2
  35.8 1.0 %shard_map.59 = (f32[3,8,256]{2,1,0:T(8,128)S(1)}, f32[3,8,1024]{2,1,0:T(8,128)S(1)}) custom-call(s32[2]{0:T(128)S(1)} %compare_select_fusion.place, s32[32,256]{1,0:T(8,128)S(1)} %reshape.7.bins, s32[2,256]{1,0:T(2,128)S(1)} %bitcast.7), custom_call_target="tpu_custom_call" | custom-call | tf_op jit(solution)/shard_map/pallas_call | solution.py:38
  37.8 1.2 %shard_map.62 = (bf16[256,1024]{1,0:T(8,128)(2,1)S(1)}, bf16[256,1024]{1,0:T(8,128)(2,1)S(1)}, f32[1,1024]{1,0:T(1,128)S(1)}) custom-call(bf16[256,1024]{1,0:T(8,128)(2,1)S(1)} %copy-done, f32[3,8,256]{2,1,0:T(8,128)S(1)} %get-tuple-element.35.hots, f32[3,8,1024]{2,1,0:T(8,128)S(1)} %get-tuple-element.36.all_links, ...), custom_call_target="tpu_custom_call" | custom-call | tf_op jit(solution)/shard_map/pallas_call | solution.py:38
  39.0 0.7 shard_map.63
  39.6 0.7 shard_map.64
  40.3 0.7 shard_map.65
  41.0 0.7 shard_map.66
  41.8 1.2 %collective-permute-done.7 = f32[1,1024]{1,0:T(1,128)S(1)} collective-permute-done((f32[1,1024]{1,0:T(1,128)S(1)}, f32[1,1024]{1,0:T(1,128)S(1)}, u32[]{:S(2)}, u32[]{:S(2)}) %collective-permute-start.7) | collective-permute-done | bytes 4128 | tf_op jit(solution)/shard_map/ppermute | solution.py:302
  42.9 1.6 %collective-permute-start.8 = (f32[1,1024]{1,0:T(1,128)S(1)}, f32[1,1024]{1,0:T(1,128)S(1)}, u32[]{:S(2)}, u32[]{:S(2)}) collective-permute-start(f32[1,1024]{1,0:T(1,128)S(1)} %maximum_add_fusion.degree), channel_id=1, source_target_pairs={{0,16},{1,17},{2,18},{3,19},{4,20},{5,21},{6,22},{7,23},{8,24},{9,... | collective-permute-start | bytes 12296 | tf_op jit(solution)/shard_map/ppermute | solution.py:302
  44.5 2.1 %collective-permute-done.8.got = f32[1,1024]{1,0:T(1,128)S(1)} collective-permute-done((f32[1,1024]{1,0:T(1,128)S(1)}, f32[1,1024]{1,0:T(1,128)S(1)}, u32[]{:S(2)}, u32[]{:S(2)}) %collective-permute-start.8) | collective-permute-done | bytes 4128 | tf_op jit(solution)/shard_map/ppermute | solution.py:302
  46.6 1.4 %shard_map.67 = (f32[1,256]{1,0:T(1,128)S(1)}, f32[32,256]{1,0:T(8,128)S(1)}, f32[32,256]{1,0:T(8,128)S(1)}, f32[32,256]{1,0:T(8,128)S(1)}) custom-call(f32[1,1024]{1,0:T(1,128)S(1)} %maximum_add_fusion.degree, f32[1,1024]{1,0:T(1,128)S(1)} %collective-permute-done.8.got, f32[32,512]{1,0:T(8,128)S(1)} %get-tuple-element.46.start_a, ...), custom_call_target="tpu_custom_call" | custom-call | tf_op jit(solution)/shard_map/pallas_call | solution.py:38
  48.0 0.7 collective-permute-start.10
  48.6 4.6 %collective-permute-start.9 = (f32[32,256]{1,0:T(8,128)S(1)}, f32[32,256]{1,0:T(8,128)S(1)}, u32[]{:S(2)}, u32[]{:S(2)}) collective-permute-start(f32[32,256]{1,0:T(8,128)S(1)} %get-tuple-element.60), channel_id=1, source_target_pairs={{0,1},{1,0},{2,3},{3,2},{4,5},{5,4},{6,7},{7,6},{8,9},{9,8},{10,11... | collective-permute-start | bytes 98312 | tf_op jit(solution)/shard_map/ppermute | solution.py:302
  53.3 1.9 %collective-permute-done.9 = f32[32,256]{1,0:T(8,128)S(1)} collective-permute-done((f32[32,256]{1,0:T(8,128)S(1)}, f32[32,256]{1,0:T(8,128)S(1)}, u32[]{:S(2)}, u32[]{:S(2)}) %collective-permute-start.9) | collective-permute-done | bytes 32800 | tf_op jit(solution)/shard_map/ppermute | solution.py:302
  55.2 2.1 %collective-permute-start.11 = (f32[32,256]{1,0:T(8,128)S(1)}, f32[32,256]{1,0:T(8,128)S(1)}, u32[]{:S(2)}, u32[]{:S(2)}) collective-permute-start(f32[32,256]{1,0:T(8,128)S(1)} %get-tuple-element.68.refs_0_), channel_id=1, source_target_pairs={{0,1},{1,0},{2,3},{3,2},{4,5},{5,4},{6,7},{7,6},{8,9},{9,8},{10,11... | collective-permute-start | bytes 98312 | tf_op jit(solution)/shard_map/ppermute | solution.py:302
  57.2 0.7 collective-permute-start.12
  57.9 1.2 %collective-permute-done.11.refs_1_ = f32[32,256]{1,0:T(8,128)S(1)} collective-permute-done((f32[32,256]{1,0:T(8,128)S(1)}, f32[32,256]{1,0:T(8,128)S(1)}, u32[]{:S(2)}, u32[]{:S(2)}) %collective-permute-start.11) | collective-permute-done | bytes 32800 | tf_op jit(solution)/shard_map/ppermute | solution.py:302
  59.1 0.6 shard_map.68
  59.8 1.2 %collective-permute-done.13 = f32[32,512]{1,0:T(8,128)S(1)} collective-permute-done((f32[32,512]{1,0:T(8,128)S(1)}, f32[32,512]{1,0:T(8,128)S(1)}, u32[]{:S(2)}, u32[]{:S(2)}) %collective-permute-start.13) | collective-permute-done | bytes 65568 | tf_op jit(solution)/shard_map/ppermute | solution.py:302
  61.1 1.6 %collective-permute-start.14 = (f32[32,256]{1,0:T(8,128)S(1)}, f32[32,256]{1,0:T(8,128)S(1)}, u32[]{:S(2)}, u32[]{:S(2)}) collective-permute-start(f32[32,256]{1,0:T(8,128)S(1)} %get-tuple-element.72), channel_id=1, source_target_pairs={{0,16},{1,17},{2,18},{3,19},{4,20},{5,21},{6,22},{7,23},{8,24},{9,... | collective-permute-start | bytes 98312 | tf_op jit(solution)/shard_map/ppermute | solution.py:302
  62.7 2.4 %collective-permute-done.14.got = f32[32,256]{1,0:T(8,128)S(1)} collective-permute-done((f32[32,256]{1,0:T(8,128)S(1)}, f32[32,256]{1,0:T(8,128)S(1)}, u32[]{:S(2)}, u32[]{:S(2)}) %collective-permute-start.14) | collective-permute-done | bytes 32800 | tf_op jit(solution)/shard_map/ppermute | solution.py:302
  65.5 1.2 %collective-permute-done.15.got = f32[40,128]{1,0:T(8,128)S(1)} collective-permute-done((f32[40,128]{1,0:T(8,128)S(1)}, f32[40,128]{1,0:T(8,128)S(1)}, u32[]{:S(2)}, u32[]{:S(2)}) %collective-permute-start.15) | collective-permute-done | bytes 20512 | tf_op jit(solution)/shard_map/ppermute | solution.py:302
  66.7 21.2 %all_to_all.5.parts = f32[16,40,128]{2,1,0:T(8,128)S(1)} all-to-all(f32[16,40,128]{2,1,0:T(8,128)S(1)} %shard_map.70), channel_id=1, replica_groups=mesh['row'=2,'core'=2,'inner'=8] {'row','inner'}, dimensions={0} | all-to-all | bytes 655360 | tf_op jit(solution)/shard_map/all_to_all | solution.py:372
  87.9 5.5 %shard_map.71 = (f32[96,256]{1,0:T(8,128)}, f32[4,32,32]{2,1,0:T(8,128)}) custom-call(f32[16,40,128]{2,1,0:T(8,128)S(1)} %all_to_all.5.parts, f32[32,256]{1,0:T(8,128)S(1)} %slice.35.start.v0, f32[32,256]{1,0:T(8,128)S(1)} %get-tuple-element.69.image.v1, f32[32,256]{1,0:T(8,128)S(1)} %get-tuple-element.65.v2), custom_call_target="tpu_custom_call" | custom-call | tf_op jit(solution)/shard_map/pallas_call | solution.py:38
  (31 shorter events, 1.9 us)
Async XLA Ops:
  0.6 36.2 %copy-start = (bf16[256,1024]{1,0:T(8,128)(2,1)S(1)}, bf16[256,1024]{1,0:T(8,128)(2,1)}, u32[]{:S(2)}) copy-start(bf16[256,1024]{1,0:T(8,128)(2,1)} %other.1) | copy-start | bytes 1572868
  0.6 15.2 %collective-permute-start.3 = (bf16[256,1024]{1,0:T(8,128)(2,1)}, bf16[256,1024]{1,0:T(8,128)(2,1)S(1)}, u32[]{:S(2)}, u32[]{:S(2)}) collective-permute-start(bf16[256,1024]{1,0:T(8,128)(2,1)} %other.1), channel_id=1, source_target_pairs={{0,16},{1,17},{2,18},{3,19},{4,20},{5,21},{6,22},{7,23},{8,24},{9,... | collective-permute-start | bytes 1572872 | tf_op jit(solution)/shard_map/ppermute | solution.py:302
  3.7 33.1 %collective-permute-start.2 = (bf16[256,1024]{1,0:T(8,128)(2,1)}, bf16[256,1024]{1,0:T(8,128)(2,1)S(1)}, u32[]{:S(2)}, u32[]{:S(2)}) collective-permute-start(bf16[256,1024]{1,0:T(8,128)(2,1)} %other.1), channel_id=1, source_target_pairs={{0,8},{1,9},{2,10},{3,11},{4,12},{5,13},{6,14},{7,15},{8,0},{9,1},... | collective-permute-start | bytes 1572872 | tf_op jit(solution)/shard_map/ppermute | solution.py:302
  15.8 21.5 %collective-permute-start.4 = (bf16[256,1024]{1,0:T(8,128)(2,1)S(1)}, bf16[256,1024]{1,0:T(8,128)(2,1)S(1)}, u32[]{:S(2)}, u32[]{:S(2)}) collective-permute-start(bf16[256,1024]{1,0:T(8,128)(2,1)S(1)} %collective-permute-done.3.r0), channel_id=1, source_target_pairs={{0,8},{1,9},{2,10},{3,11},{4,12},{5,13},{6,14},{7,15},{8,0},{9,1},... | collective-permute-start | bytes 1572872 | tf_op jit(solution)/shard_map/ppermute | solution.py:302
  15.8 19.2 %copy-start.3 = (s32[8192]{0:T(1024)S(1)}, s32[8192]{0:T(1024)}, u32[]{:S(2)}) copy-start(s32[8192]{0:T(1024)} %param.5) | copy-start | bytes 98308
  16.9 19.9 %copy-start.1 = (bf16[1024,32]{0,1:T(8,128)(2,1)S(1)}, bf16[1024,32]{0,1:T(8,128)(2,1)}, u32[]{:S(2)}) copy-start(bf16[1024,32]{0,1:T(8,128)(2,1)} %param.7) | copy-start | bytes 196612
  16.9 9.2 %collective-permute-start.5 = (bf16[128,1024]{1,0:T(8,128)(2,1)S(1)}, bf16[128,1024]{1,0:T(8,128)(2,1)S(1)}, u32[]{:S(2)}, u32[]{:S(2)}) collective-permute-start(bf16[128,1024]{1,0:T(8,128)(2,1)S(1)} %get-tuple-element.70), channel_id=1, source_target_pairs={{0,1},{1,0},{2,3},{3,2},{4,5},{5,4},{6,7},{7,6},{8,9},{9,8},{10,11... | collective-permute-start | bytes 786440 | tf_op jit(solution)/shard_map/ppermute | solution.py:302
  18.7 12.6 %collective-permute-start = (bf16[128,1024]{1,0:T(8,128)(2,1)S(1)}, bf16[128,1024]{1,0:T(8,128)(2,1)S(1)}, u32[]{:S(2)}, u32[]{:S(2)}) collective-permute-start(bf16[128,1024]{1,0:T(8,128)(2,1)S(1)} %get-tuple-element.71), channel_id=1, source_target_pairs={{0,1},{1,0},{2,3},{3,2},{4,5},{5,4},{6,7},{7,6},{8,9},{9,8},{10,11... | collective-permute-start | bytes 786440 | tf_op jit(solution)/shard_map/ppermute | solution.py:302
  26.2 14.2 %collective-permute-start.6 = (bf16[128,1024]{1,0:T(8,128)(2,1)S(1)}, bf16[128,1024]{1,0:T(8,128)(2,1)S(1)}, u32[]{:S(2)}, u32[]{:S(2)}) collective-permute-start(bf16[128,1024]{1,0:T(8,128)(2,1)S(1)} %collective-permute-done.5.other), channel_id=1, source_target_pairs={{0,2},{2,4},{3,1},{4,6},{5,3},{7,5},{8,10},{10,12},{11,9},{12,14},... | collective-permute-start | bytes 786440 | tf_op jit(solution)/shard_map/ppermute | solution.py:302
  31.3 9.7 %collective-permute-start.1 = (bf16[128,1024]{1,0:T(8,128)(2,1)S(1)}, bf16[128,1024]{1,0:T(8,128)(2,1)S(1)}, u32[]{:S(2)}, u32[]{:S(2)}) collective-permute-start(bf16[128,1024]{1,0:T(8,128)(2,1)S(1)} %collective-permute-done.other), channel_id=1, source_target_pairs={{0,2},{2,4},{3,1},{4,6},{5,3},{7,5},{8,10},{10,12},{11,9},{12,14},... | collective-permute-start | bytes 786440 | tf_op jit(solution)/shard_map/ppermute | solution.py:302
  35.1 0.7 copy-start.2
  41.7 1.2 %collective-permute-start.7 = (f32[1,1024]{1,0:T(1,128)S(1)}, f32[1,1024]{1,0:T(1,128)S(1)}, u32[]{:S(2)}, u32[]{:S(2)}) collective-permute-start(f32[1,1024]{1,0:T(1,128)S(1)} %get-tuple-element.45), channel_id=1, source_target_pairs={{0,8},{1,9},{2,10},{3,11},{4,12},{5,13},{6,14},{7,15},{8,0},{9,1},... | collective-permute-start | bytes 12296 | tf_op jit(solution)/shard_map/ppermute | solution.py:302
  42.9 3.7 %collective-permute-start.8 = (f32[1,1024]{1,0:T(1,128)S(1)}, f32[1,1024]{1,0:T(1,128)S(1)}, u32[]{:S(2)}, u32[]{:S(2)}) collective-permute-start(f32[1,1024]{1,0:T(1,128)S(1)} %maximum_add_fusion.degree), channel_id=1, source_target_pairs={{0,16},{1,17},{2,18},{3,19},{4,20},{5,21},{6,22},{7,23},{8,24},{9,... | collective-permute-start | bytes 12296 | tf_op jit(solution)/shard_map/ppermute | solution.py:302
  48.0 5.3 %collective-permute-start.10 = (f32[32,256]{1,0:T(8,128)S(1)}, f32[32,256]{1,0:T(8,128)S(1)}, u32[]{:S(2)}, u32[]{:S(2)}) collective-permute-start(f32[32,256]{1,0:T(8,128)S(1)} %get-tuple-element.61), channel_id=1, source_target_pairs={{1,2},{2,1},{3,4},{4,3},{5,6},{6,5},{9,10},{10,9},{11,12},{12,11},... | collective-permute-start | bytes 98312 | tf_op jit(solution)/shard_map/ppermute | solution.py:302
  48.6 6.5 %collective-permute-start.9 = (f32[32,256]{1,0:T(8,128)S(1)}, f32[32,256]{1,0:T(8,128)S(1)}, u32[]{:S(2)}, u32[]{:S(2)}) collective-permute-start(f32[32,256]{1,0:T(8,128)S(1)} %get-tuple-element.60), channel_id=1, source_target_pairs={{0,1},{1,0},{2,3},{3,2},{4,5},{5,4},{6,7},{7,6},{8,9},{9,8},{10,11... | collective-permute-start | bytes 98312 | tf_op jit(solution)/shard_map/ppermute | solution.py:302
  55.2 4.0 %collective-permute-start.11 = (f32[32,256]{1,0:T(8,128)S(1)}, f32[32,256]{1,0:T(8,128)S(1)}, u32[]{:S(2)}, u32[]{:S(2)}) collective-permute-start(f32[32,256]{1,0:T(8,128)S(1)} %get-tuple-element.68.refs_0_), channel_id=1, source_target_pairs={{0,1},{1,0},{2,3},{3,2},{4,5},{5,4},{6,7},{7,6},{8,9},{9,8},{10,11... | collective-permute-start | bytes 98312 | tf_op jit(solution)/shard_map/ppermute | solution.py:302
  57.2 1.9 %collective-permute-start.12 = (f32[32,256]{1,0:T(8,128)S(1)}, f32[32,256]{1,0:T(8,128)S(1)}, u32[]{:S(2)}, u32[]{:S(2)}) collective-permute-start(f32[32,256]{1,0:T(8,128)S(1)} %get-tuple-element.68.refs_0_), channel_id=1, source_target_pairs={{1,2},{2,1},{3,4},{4,3},{5,6},{6,5},{9,10},{10,9},{11,12},{12,11},... | collective-permute-start | bytes 98312 | tf_op jit(solution)/shard_map/ppermute | solution.py:302
  59.8 1.3 %collective-permute-start.13 = (f32[32,512]{1,0:T(8,128)S(1)}, f32[32,512]{1,0:T(8,128)S(1)}, u32[]{:S(2)}, u32[]{:S(2)}) collective-permute-start(f32[32,512]{1,0:T(8,128)S(1)} %get-tuple-element.63), channel_id=1, source_target_pairs={{0,8},{1,9},{2,10},{3,11},{4,12},{5,13},{6,14},{7,15},{8,0},{9,1},... | collective-permute-start | bytes 196616 | tf_op jit(solution)/shard_map/ppermute | solution.py:302
  61.1 4.0 %collective-permute-start.14 = (f32[32,256]{1,0:T(8,128)S(1)}, f32[32,256]{1,0:T(8,128)S(1)}, u32[]{:S(2)}, u32[]{:S(2)}) collective-permute-start(f32[32,256]{1,0:T(8,128)S(1)} %get-tuple-element.72), channel_id=1, source_target_pairs={{0,16},{1,17},{2,18},{3,19},{4,20},{5,21},{6,22},{7,23},{8,24},{9,... | collective-permute-start | bytes 98312 | tf_op jit(solution)/shard_map/ppermute | solution.py:302
  65.4 1.2 %collective-permute-start.15 = (f32[40,128]{1,0:T(8,128)S(1)}, f32[40,128]{1,0:T(8,128)S(1)}, u32[]{:S(2)}, u32[]{:S(2)}) collective-permute-start(f32[40,128]{1,0:T(8,128)S(1)} %get-tuple-element.64.mine), channel_id=1, source_target_pairs={{0,8},{1,9},{2,10},{3,11},{4,12},{5,13},{6,14},{7,15},{8,0},{9,1},... | collective-permute-start | bytes 61448 | tf_op jit(solution)/shard_map/ppermute | solution.py:302

commit v3 on v2

--- a/solution.py
+++ b/solution.py
@@ -211,18 +211,37 @@
     send[:, :size], send[:, size:] = total[:, size:half], total[:, half + size:]
 
 
+def fold(upper, lower):
+    width = upper.shape[0]
+    row = lax.broadcasted_iota(jnp.int32, upper.shape, 0)
+    col = lax.broadcasted_iota(jnp.int32, upper.shape, 1)
+    both = jnp.where(col >= row, upper, lower)
+    flat = jnp.concatenate([both[8 * i:8 * i + 8, :] for i in range(width // 8)], axis=1)
+    return flat, jnp.sum(jnp.where(col == row, lower, 0.0), axis=0, keepdims=True)
+
+
+def unfold(flat, diagonal):
+    width = diagonal.shape[1]
+    both = jnp.concatenate([flat[:, width * i:width * (i + 1)] for i in range(width // 8)], axis=0)
+    turned = both.T
+    row = lax.broadcasted_iota(jnp.int32, both.shape, 0)
+    col = lax.broadcasted_iota(jnp.int32, both.shape, 1)
+    upper = jnp.where(col >= row, both, turned)
+    return upper, jnp.where(col < row, both, jnp.where(col == row, diagonal, turned))
+
+
 def gram_kernel(mine, got, inv_root, start, image, image_next, packed):
     value = inv_root[...] * (mine[...] + got[...])
     image_next[...] = value
     first, begin = image[...], start[...]
     width = first.shape[0]
-    packed[:width, :] = jnp.concatenate(
-        [nt(begin, first), nt(first, first), nt(first, value), nt(value, value)], axis=1
-    )
-    gram = nt(begin, begin)
-    packed[width:, :] = jnp.concatenate(
-        [gram[8 * i:8 * i + 8, :] for i in range(width // 8)], axis=1
-    )
+    half = width // 2
+    packed[:8, :], row_a = fold(nt(begin, begin), nt(begin, first))
+    packed[8:16, :], row_b = fold(nt(first, first), nt(first, value))
+    last = nt(value, value)
+    block = jnp.concatenate([last[:half, :], last[half:, half:]], axis=1)
+    rows = jnp.concatenate([row_a, row_b, jnp.zeros((6, width), F32)], axis=0)
+    packed[16:, :] = jnp.concatenate([block[:8, :], block[8:, :], rows], axis=1)
 
 
 def spread_kernel(mine, got, copies):
@@ -232,16 +251,22 @@
 def last_kernel(parts, v0, v1, v2, basis, coefficients):
     packed = jnp.sum(parts[...], axis=0)
     width = v0.shape[0]
-    m_01, m_11, m_12, m_22 = [packed[:width, width * i:width * (i + 1)] for i in range(4)]
-    m_00 = jnp.concatenate(
-        [packed[width:, width * i:width * (i + 1)] for i in range(width // 8)], axis=0
+    half = width // 2
+    span = width + half
+    rows = packed[16:, 2 * span:2 * span + width]
+    m_00, m_01 = unfold(packed[:8, :], rows[0:1, :])
+    m_11, m_12 = unfold(packed[8:16, :], rows[1:2, :])
+    block = jnp.concatenate([packed[16:, :span], packed[16:, span:2 * span]], axis=0)
+    corner = block[:, half:width].T
+    m_22 = jnp.concatenate(
+        [block[:, :width], jnp.concatenate([corner, block[:, width:]], axis=1)], axis=0
     )
     blank = jnp.zeros((width, LANES - 3 * width), F32)
     gram = jnp.concatenate(
         [
             jnp.concatenate([m_00, m_01, m_11, blank], axis=1),
-            jnp.concatenate([m_01.T, m_11, m_12, blank], axis=1),
-            jnp.concatenate([m_11, m_12.T, m_22, blank], axis=1),
+            jnp.concatenate([m_01, m_11, m_12, blank], axis=1),
+            jnp.concatenate([m_11, m_12, m_22, blank], axis=1),
         ],
         axis=0,
     )
@@ -361,7 +386,7 @@
     mine, got = keep[:, :row_count], move(keep[:, row_count:], "row")
     image_2, packed = call(
         gram_kernel,
-        [((width, row_count), F32), ((width + 8, 4 * width), F32)],
+        [((width, row_count), F32), ((24, LANES), F32)],
         mine, got, inv_root, start, image_1,
     )
     (copies,) = call(

time: 93.7 us -> 90.9 us (0.970)
  blocking collectives: 21.2 us -> 18.2 us
    all_to_all x1, blocking collectives: 21.2 us -> 18.2 us  [steps(): parts = lax.all_to_all(copies, ('row', 'inner'), 0, 0)]
where the time goes in v3:
time: 90.9 us; the launch traced here: 90.6 us
  waiting for transfers between devices  31.9 us (35%)
  starting transfers between devices  23.9 us (26%)
  blocking collectives  18.2 us (20%)
  Pallas kernels  13.9 us (15%)
  local copies, waits for them, and re-layouts  1.78 us (2%)
    ppermute x16, waiting for transfers between devices, move(): return lax.ppermute(value, ALL, route[name])  31.9 us
    ppermute x16, starting transfers between devices, move(): return lax.ppermute(value, ALL, route[name])  23.9 us
    all_to_all x1, blocking collectives, steps(): parts = lax.all_to_all(copies, ('row', 'inner'), 0, 0)  18.2 us
    pallas_call x13, Pallas kernels, call(): pl.pallas_call(kernel, out_shape=[result(shape, kind) for shape, kind in...  13.9 us
  transfers between devices with their start and end apart: 16, of which 10 were waited for; matrix products, arithmetic and copies ran while one was open for 1% of the time, Pallas kernels for 6%

profile of v3, /device:TPU:0, one launch (start us, length us, event | category | flops | bytes accessed | tf_op | source)
XLA Modules:
  0.0 90.6 jit_solution(10992763614542233791)
XLA Ops:
  0.6 3.1 %collective-permute-start.3 = (bf16[256,1024]{1,0:T(8,128)(2,1)}, bf16[256,1024]{1,0:T(8,128)(2,1)S(1)}, u32[]{:S(2)}, u32[]{:S(2)}) collective-permute-start(bf16[256,1024]{1,0:T(8,128)(2,1)} %other.1), channel_id=1, source_target_pairs={{0,16},{1,17},{2,18},{3,19},{4,20},{5,21},{6,22},{7,23},{8,24},{9,... | collective-permute-start | bytes 1572872 | tf_op jit(solution)/shard_map/ppermute | solution.py:327
  3.7 12.1 %collective-permute-done.3.r0 = bf16[256,1024]{1,0:T(8,128)(2,1)S(1)} collective-permute-done((bf16[256,1024]{1,0:T(8,128)(2,1)}, bf16[256,1024]{1,0:T(8,128)(2,1)S(1)}, u32[]{:S(2)}, u32[]{:S(2)}) %collective-permute-start.3) | collective-permute-done | bytes 524320 | tf_op jit(solution)/shard_map/ppermute | solution.py:327
  15.8 1.1 %fusion = (bf16[128,1024]{1,0:T(8,128)(2,1)S(1)}, bf16[128,1024]{1,0:T(8,128)(2,1)S(1)}) fusion(bf16[256,1024]{1,0:T(8,128)(2,1)} %other.1), kind=kLoop, calls=%fused_computation.4 | loop fusion | bytes 1048576 | tf_op jit(solution)/shard_map/slice | solution.py:332
  16.9 1.8 %collective-permute-start.5 = (bf16[128,1024]{1,0:T(8,128)(2,1)S(1)}, bf16[128,1024]{1,0:T(8,128)(2,1)S(1)}, u32[]{:S(2)}, u32[]{:S(2)}) collective-permute-start(bf16[128,1024]{1,0:T(8,128)(2,1)S(1)} %get-tuple-element.70), channel_id=1, source_target_pairs={{0,1},{1,0},{2,3},{3,2},{4,5},{5,4},{6,7},{7,6},{8,9},{9,8},{10,11... | collective-permute-start | bytes 786440 | tf_op jit(solution)/shard_map/ppermute | solution.py:327
  19.0 7.2 %collective-permute-done.5.other = bf16[128,1024]{1,0:T(8,128)(2,1)S(1)} collective-permute-done((bf16[128,1024]{1,0:T(8,128)(2,1)S(1)}, bf16[128,1024]{1,0:T(8,128)(2,1)S(1)}, u32[]{:S(2)}, u32[]{:S(2)}) %collective-permute-start.5) | collective-permute-done | bytes 262176 | tf_op jit(solution)/shard_map/ppermute | solution.py:327
  26.2 3.7 %collective-permute-start.6 = (bf16[128,1024]{1,0:T(8,128)(2,1)S(1)}, bf16[128,1024]{1,0:T(8,128)(2,1)S(1)}, u32[]{:S(2)}, u32[]{:S(2)}) collective-permute-start(bf16[128,1024]{1,0:T(8,128)(2,1)S(1)} %collective-permute-done.5.other), channel_id=1, source_target_pairs={{0,2},{2,4},{3,1},{4,6},{5,3},{7,5},{8,10},{10,12},{11,9},{12,14},... | collective-permute-start | bytes 786440 | tf_op jit(solution)/shard_map/ppermute | solution.py:327
  29.9 1.4 %collective-permute-done.other = bf16[128,1024]{1,0:T(8,128)(2,1)S(1)} collective-permute-done((bf16[128,1024]{1,0:T(8,128)(2,1)S(1)}, bf16[128,1024]{1,0:T(8,128)(2,1)S(1)}, u32[]{:S(2)}, u32[]{:S(2)}) %collective-permute-start) | collective-permute-done | bytes 262176 | tf_op jit(solution)/shard_map/ppermute | solution.py:327
  31.3 3.7 %collective-permute-start.1 = (bf16[128,1024]{1,0:T(8,128)(2,1)S(1)}, bf16[128,1024]{1,0:T(8,128)(2,1)S(1)}, u32[]{:S(2)}, u32[]{:S(2)}) collective-permute-start(bf16[128,1024]{1,0:T(8,128)(2,1)S(1)} %collective-permute-done.other), channel_id=1, source_target_pairs={{0,2},{2,4},{3,1},{4,6},{5,3},{7,5},{8,10},{10,12},{11,9},{12,14},... | collective-permute-start | bytes 786440 | tf_op jit(solution)/shard_map/ppermute | solution.py:327
  35.1 0.7 copy-done.2
  35.8 1.0 %shard_map.59 = (f32[3,8,256]{2,1,0:T(8,128)S(1)}, f32[3,8,1024]{2,1,0:T(8,128)S(1)}) custom-call(s32[2]{0:T(128)S(1)} %compare_select_fusion.place, s32[32,256]{1,0:T(8,128)S(1)} %reshape.7.bins, s32[2,256]{1,0:T(2,128)S(1)} %bitcast.7), custom_call_target="tpu_custom_call" | custom-call | tf_op jit(solution)/shard_map/pallas_call | solution.py:38
  37.8 1.2 %shard_map.62 = (bf16[256,1024]{1,0:T(8,128)(2,1)S(1)}, bf16[256,1024]{1,0:T(8,128)(2,1)S(1)}, f32[1,1024]{1,0:T(1,128)S(1)}) custom-call(bf16[256,1024]{1,0:T(8,128)(2,1)S(1)} %copy-done, f32[3,8,256]{2,1,0:T(8,128)S(1)} %get-tuple-element.35.hots, f32[3,8,1024]{2,1,0:T(8,128)S(1)} %get-tuple-element.36.all_links, ...), custom_call_target="tpu_custom_call" | custom-call | tf_op jit(solution)/shard_map/pallas_call | solution.py:38
  39.0 0.7 shard_map.63
  39.6 0.7 shard_map.64
  40.3 0.7 shard_map.65
  41.0 0.7 shard_map.66
  41.8 1.2 %collective-permute-done.7 = f32[1,1024]{1,0:T(1,128)S(1)} collective-permute-done((f32[1,1024]{1,0:T(1,128)S(1)}, f32[1,1024]{1,0:T(1,128)S(1)}, u32[]{:S(2)}, u32[]{:S(2)}) %collective-permute-start.7) | collective-permute-done | bytes 4128 | tf_op jit(solution)/shard_map/ppermute | solution.py:327
  42.9 1.6 %collective-permute-start.8 = (f32[1,1024]{1,0:T(1,128)S(1)}, f32[1,1024]{1,0:T(1,128)S(1)}, u32[]{:S(2)}, u32[]{:S(2)}) collective-permute-start(f32[1,1024]{1,0:T(1,128)S(1)} %maximum_add_fusion.degree), channel_id=1, source_target_pairs={{0,16},{1,17},{2,18},{3,19},{4,20},{5,21},{6,22},{7,23},{8,24},{9,... | collective-permute-start | bytes 12296 | tf_op jit(solution)/shard_map/ppermute | solution.py:327
  44.5 2.1 %collective-permute-done.8.got = f32[1,1024]{1,0:T(1,128)S(1)} collective-permute-done((f32[1,1024]{1,0:T(1,128)S(1)}, f32[1,1024]{1,0:T(1,128)S(1)}, u32[]{:S(2)}, u32[]{:S(2)}) %collective-permute-start.8) | collective-permute-done | bytes 4128 | tf_op jit(solution)/shard_map/ppermute | solution.py:327
  46.6 1.4 %shard_map.67 = (f32[1,256]{1,0:T(1,128)S(1)}, f32[32,256]{1,0:T(8,128)S(1)}, f32[32,256]{1,0:T(8,128)S(1)}, f32[32,256]{1,0:T(8,128)S(1)}) custom-call(f32[1,1024]{1,0:T(1,128)S(1)} %maximum_add_fusion.degree, f32[1,1024]{1,0:T(1,128)S(1)} %collective-permute-done.8.got, f32[32,512]{1,0:T(8,128)S(1)} %get-tuple-element.46.start_a, ...), custom_call_target="tpu_custom_call" | custom-call | tf_op jit(solution)/shard_map/pallas_call | solution.py:38
  48.0 0.7 collective-permute-start.10
  48.6 4.6 %collective-permute-start.9 = (f32[32,256]{1,0:T(8,128)S(1)}, f32[32,256]{1,0:T(8,128)S(1)}, u32[]{:S(2)}, u32[]{:S(2)}) collective-permute-start(f32[32,256]{1,0:T(8,128)S(1)} %get-tuple-element.60), channel_id=1, source_target_pairs={{0,1},{1,0},{2,3},{3,2},{4,5},{5,4},{6,7},{7,6},{8,9},{9,8},{10,11... | collective-permute-start | bytes 98312 | tf_op jit(solution)/shard_map/ppermute | solution.py:327
  53.3 1.9 %collective-permute-done.9 = f32[32,256]{1,0:T(8,128)S(1)} collective-permute-done((f32[32,256]{1,0:T(8,128)S(1)}, f32[32,256]{1,0:T(8,128)S(1)}, u32[]{:S(2)}, u32[]{:S(2)}) %collective-permute-start.9) | collective-permute-done | bytes 32800 | tf_op jit(solution)/shard_map/ppermute | solution.py:327
  55.2 2.1 %collective-permute-start.11 = (f32[32,256]{1,0:T(8,128)S(1)}, f32[32,256]{1,0:T(8,128)S(1)}, u32[]{:S(2)}, u32[]{:S(2)}) collective-permute-start(f32[32,256]{1,0:T(8,128)S(1)} %get-tuple-element.68.refs_0_), channel_id=1, source_target_pairs={{0,1},{1,0},{2,3},{3,2},{4,5},{5,4},{6,7},{7,6},{8,9},{9,8},{10,11... | collective-permute-start | bytes 98312 | tf_op jit(solution)/shard_map/ppermute | solution.py:327
  57.2 0.7 collective-permute-start.12
  57.9 1.2 %collective-permute-done.11.refs_1_ = f32[32,256]{1,0:T(8,128)S(1)} collective-permute-done((f32[32,256]{1,0:T(8,128)S(1)}, f32[32,256]{1,0:T(8,128)S(1)}, u32[]{:S(2)}, u32[]{:S(2)}) %collective-permute-start.11) | collective-permute-done | bytes 32800 | tf_op jit(solution)/shard_map/ppermute | solution.py:327
  59.1 0.6 shard_map.68
  59.8 1.2 %collective-permute-done.13 = f32[32,512]{1,0:T(8,128)S(1)} collective-permute-done((f32[32,512]{1,0:T(8,128)S(1)}, f32[32,512]{1,0:T(8,128)S(1)}, u32[]{:S(2)}, u32[]{:S(2)}) %collective-permute-start.13) | collective-permute-done | bytes 65568 | tf_op jit(solution)/shard_map/ppermute | solution.py:327
  61.1 1.6 %collective-permute-start.14 = (f32[32,256]{1,0:T(8,128)S(1)}, f32[32,256]{1,0:T(8,128)S(1)}, u32[]{:S(2)}, u32[]{:S(2)}) collective-permute-start(f32[32,256]{1,0:T(8,128)S(1)} %get-tuple-element.72), channel_id=1, source_target_pairs={{0,16},{1,17},{2,18},{3,19},{4,20},{5,21},{6,22},{7,23},{8,24},{9,... | collective-permute-start | bytes 98312 | tf_op jit(solution)/shard_map/ppermute | solution.py:327
  62.7 2.4 %collective-permute-done.14.got = f32[32,256]{1,0:T(8,128)S(1)} collective-permute-done((f32[32,256]{1,0:T(8,128)S(1)}, f32[32,256]{1,0:T(8,128)S(1)}, u32[]{:S(2)}, u32[]{:S(2)}) %collective-permute-start.14) | collective-permute-done | bytes 32800 | tf_op jit(solution)/shard_map/ppermute | solution.py:327
  65.5 1.2 %collective-permute-done.15.got = f32[24,128]{1,0:T(8,128)S(1)} collective-permute-done((f32[24,128]{1,0:T(8,128)S(1)}, f32[24,128]{1,0:T(8,128)S(1)}, u32[]{:S(2)}, u32[]{:S(2)}) %collective-permute-start.15) | collective-permute-done | bytes 12320 | tf_op jit(solution)/shard_map/ppermute | solution.py:327
  66.7 18.2 %all_to_all.5.parts = f32[16,24,128]{2,1,0:T(8,128)S(1)} all-to-all(f32[16,24,128]{2,1,0:T(8,128)S(1)} %shard_map.70), channel_id=1, replica_groups=mesh['row'=2,'core'=2,'inner'=8] {'row','inner'}, dimensions={0} | all-to-all | bytes 393216 | tf_op jit(solution)/shard_map/all_to_all | solution.py:397
  85.0 5.6 %shard_map.71 = (f32[96,256]{1,0:T(8,128)}, f32[4,32,32]{2,1,0:T(8,128)}) custom-call(f32[16,24,128]{2,1,0:T(8,128)S(1)} %all_to_all.5.parts, f32[32,256]{1,0:T(8,128)S(1)} %slice.35.start.v0, f32[32,256]{1,0:T(8,128)S(1)} %get-tuple-element.69.image.v1, f32[32,256]{1,0:T(8,128)S(1)} %get-tuple-element.65.v2), custom_call_target="tpu_custom_call" | custom-call | tf_op jit(solution)/shard_map/pallas_call | solution.py:38
  (31 shorter events, 2.0 us)
Async XLA Ops:
  0.6 36.2 %copy-start = (bf16[256,1024]{1,0:T(8,128)(2,1)S(1)}, bf16[256,1024]{1,0:T(8,128)(2,1)}, u32[]{:S(2)}) copy-start(bf16[256,1024]{1,0:T(8,128)(2,1)} %other.1) | copy-start | bytes 1572868
  0.6 15.2 %collective-permute-start.3 = (bf16[256,1024]{1,0:T(8,128)(2,1)}, bf16[256,1024]{1,0:T(8,128)(2,1)S(1)}, u32[]{:S(2)}, u32[]{:S(2)}) collective-permute-start(bf16[256,1024]{1,0:T(8,128)(2,1)} %other.1), channel_id=1, source_target_pairs={{0,16},{1,17},{2,18},{3,19},{4,20},{5,21},{6,22},{7,23},{8,24},{9,... | collective-permute-start | bytes 1572872 | tf_op jit(solution)/shard_map/ppermute | solution.py:327
  3.7 33.1 %collective-permute-start.2 = (bf16[256,1024]{1,0:T(8,128)(2,1)}, bf16[256,1024]{1,0:T(8,128)(2,1)S(1)}, u32[]{:S(2)}, u32[]{:S(2)}) collective-permute-start(bf16[256,1024]{1,0:T(8,128)(2,1)} %other.1), channel_id=1, source_target_pairs={{0,8},{1,9},{2,10},{3,11},{4,12},{5,13},{6,14},{7,15},{8,0},{9,1},... | collective-permute-start | bytes 1572872 | tf_op jit(solution)/shard_map/ppermute | solution.py:327
  15.8 21.5 %collective-permute-start.4 = (bf16[256,1024]{1,0:T(8,128)(2,1)S(1)}, bf16[256,1024]{1,0:T(8,128)(2,1)S(1)}, u32[]{:S(2)}, u32[]{:S(2)}) collective-permute-start(bf16[256,1024]{1,0:T(8,128)(2,1)S(1)} %collective-permute-done.3.r0), channel_id=1, source_target_pairs={{0,8},{1,9},{2,10},{3,11},{4,12},{5,13},{6,14},{7,15},{8,0},{9,1},... | collective-permute-start | bytes 1572872 | tf_op jit(solution)/shard_map/ppermute | solution.py:327
  15.8 19.2 %copy-start.3 = (s32[8192]{0:T(1024)S(1)}, s32[8192]{0:T(1024)}, u32[]{:S(2)}) copy-start(s32[8192]{0:T(1024)} %param.5) | copy-start | bytes 98308
  16.9 19.9 %copy-start.1 = (bf16[1024,32]{0,1:T(8,128)(2,1)S(1)}, bf16[1024,32]{0,1:T(8,128)(2,1)}, u32[]{:S(2)}) copy-start(bf16[1024,32]{0,1:T(8,128)(2,1)} %param.7) | copy-start | bytes 196612
  16.9 9.2 %collective-permute-start.5 = (bf16[128,1024]{1,0:T(8,128)(2,1)S(1)}, bf16[128,1024]{1,0:T(8,128)(2,1)S(1)}, u32[]{:S(2)}, u32[]{:S(2)}) collective-permute-start(bf16[128,1024]{1,0:T(8,128)(2,1)S(1)} %get-tuple-element.70), channel_id=1, source_target_pairs={{0,1},{1,0},{2,3},{3,2},{4,5},{5,4},{6,7},{7,6},{8,9},{9,8},{10,11... | collective-permute-start | bytes 786440 | tf_op jit(solution)/shard_map/ppermute | solution.py:327
  18.7 12.6 %collective-permute-start = (bf16[128,1024]{1,0:T(8,128)(2,1)S(1)}, bf16[128,1024]{1,0:T(8,128)(2,1)S(1)}, u32[]{:S(2)}, u32[]{:S(2)}) collective-permute-start(bf16[128,1024]{1,0:T(8,128)(2,1)S(1)} %get-tuple-element.71), channel_id=1, source_target_pairs={{0,1},{1,0},{2,3},{3,2},{4,5},{5,4},{6,7},{7,6},{8,9},{9,8},{10,11... | collective-permute-start | bytes 786440 | tf_op jit(solution)/shard_map/ppermute | solution.py:327
  26.2 14.2 %collective-permute-start.6 = (bf16[128,1024]{1,0:T(8,128)(2,1)S(1)}, bf16[128,1024]{1,0:T(8,128)(2,1)S(1)}, u32[]{:S(2)}, u32[]{:S(2)}) collective-permute-start(bf16[128,1024]{1,0:T(8,128)(2,1)S(1)} %collective-permute-done.5.other), channel_id=1, source_target_pairs={{0,2},{2,4},{3,1},{4,6},{5,3},{7,5},{8,10},{10,12},{11,9},{12,14},... | collective-permute-start | bytes 786440 | tf_op jit(solution)/shard_map/ppermute | solution.py:327
  31.3 9.7 %collective-permute-start.1 = (bf16[128,1024]{1,0:T(8,128)(2,1)S(1)}, bf16[128,1024]{1,0:T(8,128)(2,1)S(1)}, u32[]{:S(2)}, u32[]{:S(2)}) collective-permute-start(bf16[128,1024]{1,0:T(8,128)(2,1)S(1)} %collective-permute-done.other), channel_id=1, source_target_pairs={{0,2},{2,4},{3,1},{4,6},{5,3},{7,5},{8,10},{10,12},{11,9},{12,14},... | collective-permute-start | bytes 786440 | tf_op jit(solution)/shard_map/ppermute | solution.py:327
  35.1 0.7 copy-start.2
  41.7 1.2 %collective-permute-start.7 = (f32[1,1024]{1,0:T(1,128)S(1)}, f32[1,1024]{1,0:T(1,128)S(1)}, u32[]{:S(2)}, u32[]{:S(2)}) collective-permute-start(f32[1,1024]{1,0:T(1,128)S(1)} %get-tuple-element.45), channel_id=1, source_target_pairs={{0,8},{1,9},{2,10},{3,11},{4,12},{5,13},{6,14},{7,15},{8,0},{9,1},... | collective-permute-start | bytes 12296 | tf_op jit(solution)/shard_map/ppermute | solution.py:327
  42.9 3.7 %collective-permute-start.8 = (f32[1,1024]{1,0:T(1,128)S(1)}, f32[1,1024]{1,0:T(1,128)S(1)}, u32[]{:S(2)}, u32[]{:S(2)}) collective-permute-start(f32[1,1024]{1,0:T(1,128)S(1)} %maximum_add_fusion.degree), channel_id=1, source_target_pairs={{0,16},{1,17},{2,18},{3,19},{4,20},{5,21},{6,22},{7,23},{8,24},{9,... | collective-permute-start | bytes 12296 | tf_op jit(solution)/shard_map/ppermute | solution.py:327
  48.0 5.3 %collective-permute-start.10 = (f32[32,256]{1,0:T(8,128)S(1)}, f32[32,256]{1,0:T(8,128)S(1)}, u32[]{:S(2)}, u32[]{:S(2)}) collective-permute-start(f32[32,256]{1,0:T(8,128)S(1)} %get-tuple-element.61), channel_id=1, source_target_pairs={{1,2},{2,1},{3,4},{4,3},{5,6},{6,5},{9,10},{10,9},{11,12},{12,11},... | collective-permute-start | bytes 98312 | tf_op jit(solution)/shard_map/ppermute | solution.py:327
  48.6 6.5 %collective-permute-start.9 = (f32[32,256]{1,0:T(8,128)S(1)}, f32[32,256]{1,0:T(8,128)S(1)}, u32[]{:S(2)}, u32[]{:S(2)}) collective-permute-start(f32[32,256]{1,0:T(8,128)S(1)} %get-tuple-element.60), channel_id=1, source_target_pairs={{0,1},{1,0},{2,3},{3,2},{4,5},{5,4},{6,7},{7,6},{8,9},{9,8},{10,11... | collective-permute-start | bytes 98312 | tf_op jit(solution)/shard_map/ppermute | solution.py:327
  55.2 4.0 %collective-permute-start.11 = (f32[32,256]{1,0:T(8,128)S(1)}, f32[32,256]{1,0:T(8,128)S(1)}, u32[]{:S(2)}, u32[]{:S(2)}) collective-permute-start(f32[32,256]{1,0:T(8,128)S(1)} %get-tuple-element.68.refs_0_), channel_id=1, source_target_pairs={{0,1},{1,0},{2,3},{3,2},{4,5},{5,4},{6,7},{7,6},{8,9},{9,8},{10,11... | collective-permute-start | bytes 98312 | tf_op jit(solution)/shard_map/ppermute | solution.py:327
  57.2 1.9 %collective-permute-start.12 = (f32[32,256]{1,0:T(8,128)S(1)}, f32[32,256]{1,0:T(8,128)S(1)}, u32[]{:S(2)}, u32[]{:S(2)}) collective-permute-start(f32[32,256]{1,0:T(8,128)S(1)} %get-tuple-element.68.refs_0_), channel_id=1, source_target_pairs={{1,2},{2,1},{3,4},{4,3},{5,6},{6,5},{9,10},{10,9},{11,12},{12,11},... | collective-permute-start | bytes 98312 | tf_op jit(solution)/shard_map/ppermute | solution.py:327
  59.8 1.3 %collective-permute-start.13 = (f32[32,512]{1,0:T(8,128)S(1)}, f32[32,512]{1,0:T(8,128)S(1)}, u32[]{:S(2)}, u32[]{:S(2)}) collective-permute-start(f32[32,512]{1,0:T(8,128)S(1)} %get-tuple-element.63), channel_id=1, source_target_pairs={{0,8},{1,9},{2,10},{3,11},{4,12},{5,13},{6,14},{7,15},{8,0},{9,1},... | collective-permute-start | bytes 196616 | tf_op jit(solution)/shard_map/ppermute | solution.py:327
  61.1 4.0 %collective-permute-start.14 = (f32[32,256]{1,0:T(8,128)S(1)}, f32[32,256]{1,0:T(8,128)S(1)}, u32[]{:S(2)}, u32[]{:S(2)}) collective-permute-start(f32[32,256]{1,0:T(8,128)S(1)} %get-tuple-element.72), channel_id=1, source_target_pairs={{0,16},{1,17},{2,18},{3,19},{4,20},{5,21},{6,22},{7,23},{8,24},{9,... | collective-permute-start | bytes 98312 | tf_op jit(solution)/shard_map/ppermute | solution.py:327
  65.5 1.2 %collective-permute-start.15 = (f32[24,128]{1,0:T(8,128)S(1)}, f32[24,128]{1,0:T(8,128)S(1)}, u32[]{:S(2)}, u32[]{:S(2)}) collective-permute-start(f32[24,128]{1,0:T(8,128)S(1)} %get-tuple-element.64.mine), channel_id=1, source_target_pairs={{0,8},{1,9},{2,10},{3,11},{4,12},{5,13},{6,14},{7,15},{8,0},{9,1},... | collective-permute-start | bytes 36872 | tf_op jit(solution)/shard_map/ppermute | solution.py:327

commit v4 on v3

--- a/solution.py
+++ b/solution.py
@@ -147,26 +147,30 @@
         start[:, at] = nn(weights[...], value, None)
 
 
-def tile_kernel(scale, kind, part, other, hots, all_links, *refs):
-    groups, (high, low, out) = refs[:4], refs[-3:]
-    first = len(refs) == 7
-    x = other[...]
-    wide = x.astype(F32)
-    own = jnp.sum(wide * wide, axis=1, keepdims=True)
-    size = x.shape[0]
-    hot = hots[kind, :, part * size:(part + 1) * size].T
+def tile_kernel(scale, places, hots, all_links, *refs):
+    count = len(places)
+    groups, others, outs = refs[:4], refs[4:4 + count], refs[-2 * count - 1:]
+    degree = refs[4 + count:-2 * count - 1]
     span = groups[0].shape[1]
-    for i in range(2):
-        turned, norms = groups[2 * i:2 * i + 2]
-        at = slice(i * span, (i + 1) * span)
-        mask = nn(hot, all_links[kind, :, at], None)
-        distance = own + norms[...] - 2.0 * nn(x, turned[...], None)
-        value = mask * jnp.exp(distance * scale)
-        top = value.astype(BF16)
-        high[:, at] = top
-        low[:, at] = (value - top.astype(F32)).astype(BF16)
-        total = jnp.sum(value, axis=0, keepdims=True)
-        out[:, at] = total if first else refs[4][:, at] + total
+    totals = [degree[0][:, span * i:span * (i + 1)] if degree else 0.0 for i in range(2)]
+    for k, (kind, part) in enumerate(places):
+        x = others[k][...]
+        wide = x.astype(F32)
+        own = jnp.sum(wide * wide, axis=1, keepdims=True)
+        size = x.shape[0]
+        hot = hots[kind, :, part * size:(part + 1) * size].T
+        high, low = outs[2 * k:2 * k + 2]
+        for i in range(2):
+            turned, norms = groups[2 * i:2 * i + 2]
+            at = slice(i * span, (i + 1) * span)
+            mask = nn(hot, all_links[kind, :, at], None)
+            distance = own + norms[...] - 2.0 * nn(x, turned[...], None)
+            value = mask * jnp.exp(distance * scale)
+            top = value.astype(BF16)
+            high[:, at] = top
+            low[:, at] = (value - top.astype(F32)).astype(BF16)
+            totals[i] = totals[i] + jnp.sum(value, axis=0, keepdims=True)
+    outs[-1][...] = jnp.concatenate(totals, axis=1)
 
 
 def send_back_kernel(degree, got, start_a, start_b, *refs):
@@ -330,9 +334,9 @@
     across = move(snapshots, "row")
     mate = move(snapshots, "core")
     near_a = move(snapshots[:half], "near")
+    far_b = move(snapshots[half:], "far")
     near_b = move(snapshots[half:], "near")
     far_a = move(near_a, "relay")
-    far_b = move(near_b, "relay")
     across_mate = move(across, "core")
 
     place = jnp.where(jnp.arange(2) == 0, column, group).astype(jnp.int32)
@@ -349,19 +353,25 @@
         turn_kernel, turn_outs, start_weights.T, snapshots, mate
     )
     turned_b, norms_b, start_b = call(turn_kernel, turn_outs, start_weights.T, across, across_mate)
-    tiles = []
+    made = {}
     degree = ()
-    for kind, part, rows in (
-        (0, 0, snapshots), (1, 0, near_a), (1, 1, near_b), (2, 0, far_a), (2, 1, far_b)
+    for blocks in (
+        (((0, 0), snapshots), ((1, 0), near_a)),
+        (((2, 0), far_a),),
+        (((1, 1), near_b), ((2, 1), far_b)),
     ):
-        size = rows.shape[0]
-        high, low, *degree = call(
-            functools.partial(tile_kernel, -3.0 / features, kind, part),
-            [((size, span), BF16), ((size, span), BF16), ((1, span), F32)],
-            rows, hots, links, turned_a, norms_a, turned_b, norms_b, *degree,
+        places = tuple(place for place, rows in blocks)
+        outs = [((rows.shape[0], span), BF16) for place, rows in blocks for _ in range(2)]
+        *out, total = call(
+            functools.partial(tile_kernel, -3.0 / features, places),
+            outs + [((1, span), F32)],
+            hots, links, turned_a, norms_a, turned_b, norms_b,
+            *(rows for place, rows in blocks), *degree,
         )
-        tiles += [high, low]
+        degree = (total,)
+        made.update((place, out[2 * i:2 * i + 2]) for i, place in enumerate(places))
     (degree,) = degree
+    tiles = sum((made[place] for place in sorted(made)), [])
 
     got = move(degree, "core")
     degree = degree + jnp.concatenate(

time: 90.9 us -> 92 us (1.012)
  waiting for transfers between devices: 31.9 us -> 35.6 us
  starting transfers between devices: 23.9 us -> 22.5 us
    ppermute x16, waiting for transfers between devices: 31.9 us -> 35.6 us  [move(): return lax.ppermute(value, ALL, route[name])]
    ppermute x16, starting transfers between devices: 23.9 us -> 22.5 us  [move(): return lax.ppermute(value, ALL, route[name])]
    pallas_call x13 -> x11, Pallas kernels: 13.9 us -> 13.5 us  [call(): pl.pallas_call(kernel, out_shape=[result(shape, kind) for shape, kind in...]
  transfers between devices with their start and end apart: 16 -> 16, of which waited for: 10 -> 11; matrix products, arithmetic and copies ran while one was open for 1% -> 1% of each run, Pallas kernels for 6% -> 5%
where the time goes in v4:
time: 92 us; the launch traced here: 91.7 us
  waiting for transfers between devices  35.6 us (39%)
  starting transfers between devices  22.5 us (24%)
  blocking collectives  17.5 us (19%)
  Pallas kernels  13.5 us (15%)
  local copies, waits for them, and re-layouts  1.78 us (2%)
    ppermute x16, waiting for transfers between devices, move(): return lax.ppermute(value, ALL, route[name])  35.6 us
    ppermute x16, starting transfers between devices, move(): return lax.ppermute(value, ALL, route[name])  22.5 us
    all_to_all x1, blocking collectives, steps(): parts = lax.all_to_all(copies, ('row', 'inner'), 0, 0)  17.5 us
    pallas_call x11, Pallas kernels, call(): pl.pallas_call(kernel, out_shape=[result(shape, kind) for shape, kind in...  13.5 us
  transfers between devices with their start and end apart: 16, of which 11 were waited for; matrix products, arithmetic and copies ran while one was open for 1% of the time, Pallas kernels for 5%

profile of v4, /device:TPU:0, one launch (start us, length us, event | category | flops | bytes accessed | tf_op | source)
XLA Modules:
  0.0 91.7 jit_solution(7179674806444647046)
XLA Ops:
  0.6 3.1 %collective-permute-start.1 = (bf16[256,1024]{1,0:T(8,128)(2,1)}, bf16[256,1024]{1,0:T(8,128)(2,1)S(1)}, u32[]{:S(2)}, u32[]{:S(2)}) collective-permute-start(bf16[256,1024]{1,0:T(8,128)(2,1)} %refs_4_.1), channel_id=1, source_target_pairs={{0,16},{1,17},{2,18},{3,19},{4,20},{5,21},{6,22},{7,23},{8,24},{9,... | collective-permute-start | bytes 1572872 | tf_op jit(solution)/shard_map/ppermute | solution.py:331
  3.7 12.1 %collective-permute-done.1.r0 = bf16[256,1024]{1,0:T(8,128)(2,1)S(1)} collective-permute-done((bf16[256,1024]{1,0:T(8,128)(2,1)}, bf16[256,1024]{1,0:T(8,128)(2,1)S(1)}, u32[]{:S(2)}, u32[]{:S(2)}) %collective-permute-start.1) | collective-permute-done | bytes 524320 | tf_op jit(solution)/shard_map/ppermute | solution.py:331
  15.8 1.1 %fusion = (bf16[128,1024]{1,0:T(8,128)(2,1)S(1)}, bf16[128,1024]{1,0:T(8,128)(2,1)S(1)}) fusion(bf16[256,1024]{1,0:T(8,128)(2,1)} %refs_4_.1), kind=kLoop, calls=%fused_computation.4 | loop fusion | bytes 1048576 | tf_op jit(solution)/shard_map/slice | solution.py:336
  16.9 1.8 %collective-permute-start.5 = (bf16[128,1024]{1,0:T(8,128)(2,1)S(1)}, bf16[128,1024]{1,0:T(8,128)(2,1)S(1)}, u32[]{:S(2)}, u32[]{:S(2)}) collective-permute-start(bf16[128,1024]{1,0:T(8,128)(2,1)S(1)} %get-tuple-element.66), channel_id=1, source_target_pairs={{0,1},{1,0},{2,3},{3,2},{4,5},{5,4},{6,7},{7,6},{8,9},{9,8},{10,11... | collective-permute-start | bytes 786440 | tf_op jit(solution)/shard_map/ppermute | solution.py:331
  18.7 7.0 %collective-permute-done.5.refs_5_ = bf16[128,1024]{1,0:T(8,128)(2,1)S(1)} collective-permute-done((bf16[128,1024]{1,0:T(8,128)(2,1)S(1)}, bf16[128,1024]{1,0:T(8,128)(2,1)S(1)}, u32[]{:S(2)}, u32[]{:S(2)}) %collective-permute-start.5) | collective-permute-done | bytes 262176 | tf_op jit(solution)/shard_map/ppermute | solution.py:331
  25.7 3.7 %collective-permute-start.6 = (bf16[128,1024]{1,0:T(8,128)(2,1)S(1)}, bf16[128,1024]{1,0:T(8,128)(2,1)S(1)}, u32[]{:S(2)}, u32[]{:S(2)}) collective-permute-start(bf16[128,1024]{1,0:T(8,128)(2,1)S(1)} %collective-permute-done.5.refs_5_), channel_id=1, source_target_pairs={{0,2},{2,4},{3,1},{4,6},{5,3},{7,5},{8,10},{10,12},{11,9},{12,14},... | collective-permute-start | bytes 786440 | tf_op jit(solution)/shard_map/ppermute | solution.py:331
  29.5 0.7 collective-permute-start.4
  30.3 0.7 copy-done.2
  30.9 1.0 %shard_map.59 = (f32[3,8,256]{2,1,0:T(8,128)S(1)}, f32[3,8,1024]{2,1,0:T(8,128)S(1)}) custom-call(s32[2]{0:T(128)S(1)} %compare_select_fusion.place, s32[32,256]{1,0:T(8,128)S(1)} %reshape.7.bins, s32[2,256]{1,0:T(2,128)S(1)} %bitcast.7), custom_call_target="tpu_custom_call" | custom-call | tf_op jit(solution)/shard_map/pallas_call | solution.py:38
  32.0 0.5 shard_map.60
  32.4 0.5 shard_map.61
  32.9 1.6 %shard_map.62 = (bf16[256,1024]{1,0:T(8,128)(2,1)S(1)}, bf16[256,1024]{1,0:T(8,128)(2,1)S(1)}, bf16[128,1024]{1,0:T(8,128)(2,1)S(1)}, bf16[128,1024]{1,0:T(8,128)(2,1)S(1)}, f32[1,1024]{1,0:T(1,128)S(1)}) custom-call(f32[3,8,256]{2,1,0:T(8,128)S(1)} %get-tuple-element.33.hots, f32[3,8,1024]{2,1,0:T(8,128)S(1)} %get-tuple-element.34.all_links, ...), custom_call_target="tpu_custom_call" | custom-call | tf_op jit(solution)/shard_map/pallas_call | solution.py:38
  34.8 0.7 shard_map.63
  35.4 5.1 %collective-permute-done.3.refs_4_ = bf16[128,1024]{1,0:T(8,128)(2,1)S(1)} collective-permute-done((bf16[128,1024]{1,0:T(8,128)(2,1)S(1)}, bf16[128,1024]{1,0:T(8,128)(2,1)S(1)}, u32[]{:S(2)}, u32[]{:S(2)}) %collective-permute-start.3) | collective-permute-done | bytes 262176 | tf_op jit(solution)/shard_map/ppermute | solution.py:331
  40.5 1.2 %shard_map.64 = (bf16[128,1024]{1,0:T(8,128)(2,1)S(1)}, bf16[128,1024]{1,0:T(8,128)(2,1)S(1)}, bf16[128,1024]{1,0:T(8,128)(2,1)S(1)}, bf16[128,1024]{1,0:T(8,128)(2,1)S(1)}, f32[1,1024]{1,0:T(1,128)S(1)}) custom-call(f32[3,8,256]{2,1,0:T(8,128)S(1)} %get-tuple-element.33.hots, f32[3,8,1024]{2,1,0:T(8,128)S(1)} %get-tuple-element.34.all_links, ...), custom_call_target="tpu_custom_call" | custom-call | tf_op jit(solution)/shard_map/pallas_call | solution.py:38
  41.7 1.2 %collective-permute-done.7 = f32[1,1024]{1,0:T(1,128)S(1)} collective-permute-done((f32[1,1024]{1,0:T(1,128)S(1)}, f32[1,1024]{1,0:T(1,128)S(1)}, u32[]{:S(2)}, u32[]{:S(2)}) %collective-permute-start.7) | collective-permute-done | bytes 4128 | tf_op jit(solution)/shard_map/ppermute | solution.py:331
  42.9 1.6 %collective-permute-start.8 = (f32[1,1024]{1,0:T(1,128)S(1)}, f32[1,1024]{1,0:T(1,128)S(1)}, u32[]{:S(2)}, u32[]{:S(2)}) collective-permute-start(f32[1,1024]{1,0:T(1,128)S(1)} %maximum_add_fusion.degree), channel_id=1, source_target_pairs={{0,16},{1,17},{2,18},{3,19},{4,20},{5,21},{6,22},{7,23},{8,24},{9,... | collective-permute-start | bytes 12296 | tf_op jit(solution)/shard_map/ppermute | solution.py:331
  44.5 2.1 %collective-permute-done.8.got = f32[1,1024]{1,0:T(1,128)S(1)} collective-permute-done((f32[1,1024]{1,0:T(1,128)S(1)}, f32[1,1024]{1,0:T(1,128)S(1)}, u32[]{:S(2)}, u32[]{:S(2)}) %collective-permute-start.8) | collective-permute-done | bytes 4128 | tf_op jit(solution)/shard_map/ppermute | solution.py:331
  46.6 1.4 %shard_map.65 = (f32[1,256]{1,0:T(1,128)S(1)}, f32[32,256]{1,0:T(8,128)S(1)}, f32[32,256]{1,0:T(8,128)S(1)}, f32[32,256]{1,0:T(8,128)S(1)}) custom-call(f32[1,1024]{1,0:T(1,128)S(1)} %maximum_add_fusion.degree, f32[1,1024]{1,0:T(1,128)S(1)} %collective-permute-done.8.got, f32[32,512]{1,0:T(8,128)S(1)} %get-tuple-element.42.start_a, ...), custom_call_target="tpu_custom_call" | custom-call | tf_op jit(solution)/shard_map/pallas_call | solution.py:38
  48.0 0.7 collective-permute-start.10
  48.6 6.5 %collective-permute-start.9 = (f32[32,256]{1,0:T(8,128)S(1)}, f32[32,256]{1,0:T(8,128)S(1)}, u32[]{:S(2)}, u32[]{:S(2)}) collective-permute-start(f32[32,256]{1,0:T(8,128)S(1)} %get-tuple-element.56), channel_id=1, source_target_pairs={{0,1},{1,0},{2,3},{3,2},{4,5},{5,4},{6,7},{7,6},{8,9},{9,8},{10,11... | collective-permute-start | bytes 98312 | tf_op jit(solution)/shard_map/ppermute | solution.py:331
  55.2 1.9 %collective-permute-done.9 = f32[32,256]{1,0:T(8,128)S(1)} collective-permute-done((f32[32,256]{1,0:T(8,128)S(1)}, f32[32,256]{1,0:T(8,128)S(1)}, u32[]{:S(2)}, u32[]{:S(2)}) %collective-permute-start.9) | collective-permute-done | bytes 32800 | tf_op jit(solution)/shard_map/ppermute | solution.py:331
  57.1 2.1 %collective-permute-start.11 = (f32[32,256]{1,0:T(8,128)S(1)}, f32[32,256]{1,0:T(8,128)S(1)}, u32[]{:S(2)}, u32[]{:S(2)}) collective-permute-start(f32[32,256]{1,0:T(8,128)S(1)} %get-tuple-element.64.refs_0_), channel_id=1, source_target_pairs={{0,1},{1,0},{2,3},{3,2},{4,5},{5,4},{6,7},{7,6},{8,9},{9,8},{10,11... | collective-permute-start | bytes 98312 | tf_op jit(solution)/shard_map/ppermute | solution.py:331
  59.1 0.7 collective-permute-start.12
  59.8 1.2 %collective-permute-done.11.refs_1_ = f32[32,256]{1,0:T(8,128)S(1)} collective-permute-done((f32[32,256]{1,0:T(8,128)S(1)}, f32[32,256]{1,0:T(8,128)S(1)}, u32[]{:S(2)}, u32[]{:S(2)}) %collective-permute-start.11) | collective-permute-done | bytes 32800 | tf_op jit(solution)/shard_map/ppermute | solution.py:331
  61.0 0.6 shard_map.66
  61.7 1.2 %collective-permute-done.13 = f32[32,512]{1,0:T(8,128)S(1)} collective-permute-done((f32[32,512]{1,0:T(8,128)S(1)}, f32[32,512]{1,0:T(8,128)S(1)}, u32[]{:S(2)}, u32[]{:S(2)}) %collective-permute-start.13) | collective-permute-done | bytes 65568 | tf_op jit(solution)/shard_map/ppermute | solution.py:331
  63.0 1.6 %collective-permute-start.14 = (f32[32,256]{1,0:T(8,128)S(1)}, f32[32,256]{1,0:T(8,128)S(1)}, u32[]{:S(2)}, u32[]{:S(2)}) collective-permute-start(f32[32,256]{1,0:T(8,128)S(1)} %get-tuple-element.68), channel_id=1, source_target_pairs={{0,16},{1,17},{2,18},{3,19},{4,20},{5,21},{6,22},{7,23},{8,24},{9,... | collective-permute-start | bytes 98312 | tf_op jit(solution)/shard_map/ppermute | solution.py:331
  64.6 2.4 %collective-permute-done.14.got = f32[32,256]{1,0:T(8,128)S(1)} collective-permute-done((f32[32,256]{1,0:T(8,128)S(1)}, f32[32,256]{1,0:T(8,128)S(1)}, u32[]{:S(2)}, u32[]{:S(2)}) %collective-permute-start.14) | collective-permute-done | bytes 32800 | tf_op jit(solution)/shard_map/ppermute | solution.py:331
  67.4 1.2 %collective-permute-done.15.got = f32[24,128]{1,0:T(8,128)S(1)} collective-permute-done((f32[24,128]{1,0:T(8,128)S(1)}, f32[24,128]{1,0:T(8,128)S(1)}, u32[]{:S(2)}, u32[]{:S(2)}) %collective-permute-start.15) | collective-permute-done | bytes 12320 | tf_op jit(solution)/shard_map/ppermute | solution.py:331
  68.6 17.5 %all_to_all.5.parts = f32[16,24,128]{2,1,0:T(8,128)S(1)} all-to-all(f32[16,24,128]{2,1,0:T(8,128)S(1)} %shard_map.68), channel_id=1, replica_groups=mesh['row'=2,'core'=2,'inner'=8] {'row','inner'}, dimensions={0} | all-to-all | bytes 393216 | tf_op jit(solution)/shard_map/all_to_all | solution.py:407
  86.1 5.6 %shard_map.69 = (f32[96,256]{1,0:T(8,128)}, f32[4,32,32]{2,1,0:T(8,128)}) custom-call(f32[16,24,128]{2,1,0:T(8,128)S(1)} %all_to_all.5.parts, f32[32,256]{1,0:T(8,128)S(1)} %slice.36.start.v0, f32[32,256]{1,0:T(8,128)S(1)} %get-tuple-element.65.image.v1, f32[32,256]{1,0:T(8,128)S(1)} %get-tuple-element.61.v2), custom_call_target="tpu_custom_call" | custom-call | tf_op jit(solution)/shard_map/pallas_call | solution.py:38
  (29 shorter events, 0.9 us)
Async XLA Ops:
  0.6 31.3 %copy-start = (bf16[256,1024]{1,0:T(8,128)(2,1)S(1)}, bf16[256,1024]{1,0:T(8,128)(2,1)}, u32[]{:S(2)}) copy-start(bf16[256,1024]{1,0:T(8,128)(2,1)} %refs_4_.1) | copy-start | bytes 1572868
  0.6 15.2 %collective-permute-start.1 = (bf16[256,1024]{1,0:T(8,128)(2,1)}, bf16[256,1024]{1,0:T(8,128)(2,1)S(1)}, u32[]{:S(2)}, u32[]{:S(2)}) collective-permute-start(bf16[256,1024]{1,0:T(8,128)(2,1)} %refs_4_.1), channel_id=1, source_target_pairs={{0,16},{1,17},{2,18},{3,19},{4,20},{5,21},{6,22},{7,23},{8,24},{9,... | collective-permute-start | bytes 1572872 | tf_op jit(solution)/shard_map/ppermute | solution.py:331
  3.7 28.2 %collective-permute-start = (bf16[256,1024]{1,0:T(8,128)(2,1)}, bf16[256,1024]{1,0:T(8,128)(2,1)S(1)}, u32[]{:S(2)}, u32[]{:S(2)}) collective-permute-start(bf16[256,1024]{1,0:T(8,128)(2,1)} %refs_4_.1), channel_id=1, source_target_pairs={{0,8},{1,9},{2,10},{3,11},{4,12},{5,13},{6,14},{7,15},{8,0},{9,1},... | collective-permute-start | bytes 1572872 | tf_op jit(solution)/shard_map/ppermute | solution.py:331
  15.8 16.6 %collective-permute-start.2 = (bf16[256,1024]{1,0:T(8,128)(2,1)S(1)}, bf16[256,1024]{1,0:T(8,128)(2,1)S(1)}, u32[]{:S(2)}, u32[]{:S(2)}) collective-permute-start(bf16[256,1024]{1,0:T(8,128)(2,1)S(1)} %collective-permute-done.1.r0), channel_id=1, source_target_pairs={{0,8},{1,9},{2,10},{3,11},{4,12},{5,13},{6,14},{7,15},{8,0},{9,1},... | collective-permute-start | bytes 1572872 | tf_op jit(solution)/shard_map/ppermute | solution.py:331
  15.8 14.4 %copy-start.3 = (s32[8192]{0:T(1024)S(1)}, s32[8192]{0:T(1024)}, u32[]{:S(2)}) copy-start(s32[8192]{0:T(1024)} %param.5) | copy-start | bytes 98308
  16.9 15.0 %copy-start.1 = (bf16[1024,32]{0,1:T(8,128)(2,1)S(1)}, bf16[1024,32]{0,1:T(8,128)(2,1)}, u32[]{:S(2)}) copy-start(bf16[1024,32]{0,1:T(8,128)(2,1)} %param.7) | copy-start | bytes 196612
  16.9 8.8 %collective-permute-start.5 = (bf16[128,1024]{1,0:T(8,128)(2,1)S(1)}, bf16[128,1024]{1,0:T(8,128)(2,1)S(1)}, u32[]{:S(2)}, u32[]{:S(2)}) collective-permute-start(bf16[128,1024]{1,0:T(8,128)(2,1)S(1)} %get-tuple-element.66), channel_id=1, source_target_pairs={{0,1},{1,0},{2,3},{3,2},{4,5},{5,4},{6,7},{7,6},{8,9},{9,8},{10,11... | collective-permute-start | bytes 786440 | tf_op jit(solution)/shard_map/ppermute | solution.py:331
  25.7 9.1 %collective-permute-start.6 = (bf16[128,1024]{1,0:T(8,128)(2,1)S(1)}, bf16[128,1024]{1,0:T(8,128)(2,1)S(1)}, u32[]{:S(2)}, u32[]{:S(2)}) collective-permute-start(bf16[128,1024]{1,0:T(8,128)(2,1)S(1)} %collective-permute-done.5.refs_5_), channel_id=1, source_target_pairs={{0,2},{2,4},{3,1},{4,6},{5,3},{7,5},{8,10},{10,12},{11,9},{12,14},... | collective-permute-start | bytes 786440 | tf_op jit(solution)/shard_map/ppermute | solution.py:331
  29.4 11.1 %collective-permute-start.3 = (bf16[128,1024]{1,0:T(8,128)(2,1)S(1)}, bf16[128,1024]{1,0:T(8,128)(2,1)S(1)}, u32[]{:S(2)}, u32[]{:S(2)}) collective-permute-start(bf16[128,1024]{1,0:T(8,128)(2,1)S(1)} %get-tuple-element.67), channel_id=1, source_target_pairs={{0,1},{1,0},{2,3},{3,2},{4,5},{5,4},{6,7},{7,6},{8,9},{9,8},{10,11... | collective-permute-start | bytes 786440 | tf_op jit(solution)/shard_map/ppermute | solution.py:331
  29.5 11.0 %collective-permute-start.4 = (bf16[128,1024]{1,0:T(8,128)(2,1)S(1)}, bf16[128,1024]{1,0:T(8,128)(2,1)S(1)}, u32[]{:S(2)}, u32[]{:S(2)}) collective-permute-start(bf16[128,1024]{1,0:T(8,128)(2,1)S(1)} %get-tuple-element.67), channel_id=1, source_target_pairs={{1,2},{2,1},{3,4},{4,3},{5,6},{6,5},{9,10},{10,9},{11,12},{12,11},... | collective-permute-start | bytes 786440 | tf_op jit(solution)/shard_map/ppermute | solution.py:331
  30.2 0.7 copy-start.2
  41.7 1.2 %collective-permute-start.7 = (f32[1,1024]{1,0:T(1,128)S(1)}, f32[1,1024]{1,0:T(1,128)S(1)}, u32[]{:S(2)}, u32[]{:S(2)}) collective-permute-start(f32[1,1024]{1,0:T(1,128)S(1)} %get-tuple-element.41), channel_id=1, source_target_pairs={{0,8},{1,9},{2,10},{3,11},{4,12},{5,13},{6,14},{7,15},{8,0},{9,1},... | collective-permute-start | bytes 12296 | tf_op jit(solution)/shard_map/ppermute | solution.py:331
  42.9 3.7 %collective-permute-start.8 = (f32[1,1024]{1,0:T(1,128)S(1)}, f32[1,1024]{1,0:T(1,128)S(1)}, u32[]{:S(2)}, u32[]{:S(2)}) collective-permute-start(f32[1,1024]{1,0:T(1,128)S(1)} %maximum_add_fusion.degree), channel_id=1, source_target_pairs={{0,16},{1,17},{2,18},{3,19},{4,20},{5,21},{6,22},{7,23},{8,24},{9,... | collective-permute-start | bytes 12296 | tf_op jit(solution)/shard_map/ppermute | solution.py:331
  48.0 7.2 %collective-permute-start.10 = (f32[32,256]{1,0:T(8,128)S(1)}, f32[32,256]{1,0:T(8,128)S(1)}, u32[]{:S(2)}, u32[]{:S(2)}) collective-permute-start(f32[32,256]{1,0:T(8,128)S(1)} %get-tuple-element.57), channel_id=1, source_target_pairs={{1,2},{2,1},{3,4},{4,3},{5,6},{6,5},{9,10},{10,9},{11,12},{12,11},... | collective-permute-start | bytes 98312 | tf_op jit(solution)/shard_map/ppermute | solution.py:331
  48.6 8.4 %collective-permute-start.9 = (f32[32,256]{1,0:T(8,128)S(1)}, f32[32,256]{1,0:T(8,128)S(1)}, u32[]{:S(2)}, u32[]{:S(2)}) collective-permute-start(f32[32,256]{1,0:T(8,128)S(1)} %get-tuple-element.56), channel_id=1, source_target_pairs={{0,1},{1,0},{2,3},{3,2},{4,5},{5,4},{6,7},{7,6},{8,9},{9,8},{10,11... | collective-permute-start | bytes 98312 | tf_op jit(solution)/shard_map/ppermute | solution.py:331
  57.1 4.0 %collective-permute-start.11 = (f32[32,256]{1,0:T(8,128)S(1)}, f32[32,256]{1,0:T(8,128)S(1)}, u32[]{:S(2)}, u32[]{:S(2)}) collective-permute-start(f32[32,256]{1,0:T(8,128)S(1)} %get-tuple-element.64.refs_0_), channel_id=1, source_target_pairs={{0,1},{1,0},{2,3},{3,2},{4,5},{5,4},{6,7},{7,6},{8,9},{9,8},{10,11... | collective-permute-start | bytes 98312 | tf_op jit(solution)/shard_map/ppermute | solution.py:331
  59.1 1.9 %collective-permute-start.12 = (f32[32,256]{1,0:T(8,128)S(1)}, f32[32,256]{1,0:T(8,128)S(1)}, u32[]{:S(2)}, u32[]{:S(2)}) collective-permute-start(f32[32,256]{1,0:T(8,128)S(1)} %get-tuple-element.64.refs_0_), channel_id=1, source_target_pairs={{1,2},{2,1},{3,4},{4,3},{5,6},{6,5},{9,10},{10,9},{11,12},{12,11},... | collective-permute-start | bytes 98312 | tf_op jit(solution)/shard_map/ppermute | solution.py:331
  61.7 1.3 %collective-permute-start.13 = (f32[32,512]{1,0:T(8,128)S(1)}, f32[32,512]{1,0:T(8,128)S(1)}, u32[]{:S(2)}, u32[]{:S(2)}) collective-permute-start(f32[32,512]{1,0:T(8,128)S(1)} %get-tuple-element.59), channel_id=1, source_target_pairs={{0,8},{1,9},{2,10},{3,11},{4,12},{5,13},{6,14},{7,15},{8,0},{9,1},... | collective-permute-start | bytes 196616 | tf_op jit(solution)/shard_map/ppermute | solution.py:331
  63.0 4.0 %collective-permute-start.14 = (f32[32,256]{1,0:T(8,128)S(1)}, f32[32,256]{1,0:T(8,128)S(1)}, u32[]{:S(2)}, u32[]{:S(2)}) collective-permute-start(f32[32,256]{1,0:T(8,128)S(1)} %get-tuple-element.68), channel_id=1, source_target_pairs={{0,16},{1,17},{2,18},{3,19},{4,20},{5,21},{6,22},{7,23},{8,24},{9,... | collective-permute-start | bytes 98312 | tf_op jit(solution)/shard_map/ppermute | solution.py:331
  67.4 1.2 %collective-permute-start.15 = (f32[24,128]{1,0:T(8,128)S(1)}, f32[24,128]{1,0:T(8,128)S(1)}, u32[]{:S(2)}, u32[]{:S(2)}) collective-permute-start(f32[24,128]{1,0:T(8,128)S(1)} %get-tuple-element.60.mine), channel_id=1, source_target_pairs={{0,8},{1,9},{2,10},{3,11},{4,12},{5,13},{6,14},{7,15},{8,0},{9,1},... | collective-permute-start | bytes 36872 | tf_op jit(solution)/shard_map/ppermute | solution.py:331

commit v5 on v4

--- a/solution.py
+++ b/solution.py
@@ -158,7 +158,7 @@
         wide = x.astype(F32)
         own = jnp.sum(wide * wide, axis=1, keepdims=True)
         size = x.shape[0]
-        hot = hots[kind, :, part * size:(part + 1) * size].T
+        hot = hots[kind, :, part:part + size].T
         high, low = outs[2 * k:2 * k + 2]
         for i in range(2):
             turned, norms = groups[2 * i:2 * i + 2]
@@ -188,8 +188,9 @@
         piece = nn(tiles[2 * i][...], both, None)
         pieces.append(piece[:, :width] + piece[:, width:] + nn(tiles[2 * i + 1][...], top, None))
     own[...] = pieces[0].T
-    near[...] = jnp.concatenate(pieces[1:3], axis=0).T
-    far[...] = jnp.concatenate(pieces[3:5], axis=0).T
+    cut = (len(pieces) + 1) // 2
+    near[...] = jnp.concatenate(pieces[1:cut], axis=0).T
+    far[...] = jnp.concatenate(pieces[cut:], axis=0).T
 
 
 def apply_kernel(*refs):
@@ -299,21 +300,25 @@
 
 
 def routes(n_loop, n_inner):
-    def build(loop_of, inner_of):
+    def build(target):
         pairs = []
         for l in range(n_loop):
             for c in range(n_inner):
-                if 0 <= inner_of(c) < n_inner:
-                    pairs.append((l * n_inner + c, loop_of(l) * n_inner + inner_of(c)))
+                m, d = target(l, c)
+                if 0 <= d < n_inner:
+                    pairs.append((l * n_inner + c, m * n_inner + d))
         return pairs
 
-    same = lambda v: v
+    def far(l, c):
+        d = c + 1 if c % 2 else c - 1
+        return (l, d) if 0 <= d < n_inner else (l ^ 1, c)
+
     return {
-        "core": build(lambda l: l ^ 1, same),
-        "row": build(lambda l: l ^ 2, same),
-        "near": build(same, lambda c: c ^ 1),
-        "far": build(same, lambda c: c + 1 if c % 2 else c - 1),
-        "relay": build(same, lambda c: c - 2 if c % 2 else c + 2),
+        "core": build(lambda l, c: (l ^ 1, c)),
+        "row": build(lambda l, c: (l ^ 2, c)),
+        "near": build(lambda l, c: (l, c ^ 1)),
+        "far": build(far),
+        "relay": build(lambda l, c: (l, c - 2 if c % 2 else c + 2)),
     }
 
 
@@ -332,8 +337,8 @@
 
     half = row_count // 2
     across = move(snapshots, "row")
+    near_a = move(snapshots[:half], "near")
     mate = move(snapshots, "core")
-    near_a = move(snapshots[:half], "near")
     far_b = move(snapshots[half:], "far")
     near_b = move(snapshots[half:], "near")
     far_a = move(near_a, "relay")
@@ -358,7 +363,7 @@
     for blocks in (
         (((0, 0), snapshots), ((1, 0), near_a)),
         (((2, 0), far_a),),
-        (((1, 1), near_b), ((2, 1), far_b)),
+        (((1, half), near_b), ((2, half), far_b)),
     ):
         places = tuple(place for place, rows in blocks)
         outs = [((rows.shape[0], span), BF16) for place, rows in blocks for _ in range(2)]
@@ -384,13 +389,17 @@
         degree, move(degree, "row"), start_a, start_b, *tiles,
     )
     start = start_a[:, :row_count]
-    image_1 = inv_root * (own + move(near, "near") + move(far, "far"))
+    near = move(near, "near")
+    far = move(far, "far")
+    image_1 = inv_root * (own + near + far)
 
     scaled = inv_root * image_1
+    near = move(scaled, "near")
+    far = move(scaled, "far")
     keep, send = call(
         apply_kernel,
         [((width, span // 2), F32)] * 2,
-        scaled, move(scaled, "near"), move(scaled, "far"), *tiles,
+        scaled, near, far, *tiles,
     )
     keep = keep + move(send, "core")
     mine, got = keep[:, :row_count], move(keep[:, row_count:], "row")

time: 92 us -> 88.2 us (0.959)
  starting transfers between devices: 22.5 us -> 19.4 us
  blocking collectives: 17.5 us -> 15.7 us
  waiting for transfers between devices: 35.6 us -> 36.8 us
    ppermute x16, starting transfers between devices: 22.5 us -> 19.4 us  [move(): return lax.ppermute(value, ALL, route[name])]
    all_to_all x1, blocking collectives: 17.5 us -> 15.7 us  [steps(): parts = lax.all_to_all(copies, ('row', 'inner'), 0, 0)]
    ppermute x16, waiting for transfers between devices: 35.6 us -> 36.8 us  [move(): return lax.ppermute(value, ALL, route[name])]
where the time goes in v5:
time: 88.2 us; the launch traced here: 88 us
  waiting for transfers between devices  36.8 us (42%)
  starting transfers between devices  19.4 us (22%)
  blocking collectives  15.7 us (18%)
  Pallas kernels  13.5 us (15%)
  local copies, waits for them, and re-layouts  1.78 us (2%)
    ppermute x16, waiting for transfers between devices, move(): return lax.ppermute(value, ALL, route[name])  36.8 us
    ppermute x16, starting transfers between devices, move(): return lax.ppermute(value, ALL, route[name])  19.4 us
    all_to_all x1, blocking collectives, steps(): parts = lax.all_to_all(copies, ('row', 'inner'), 0, 0)  15.7 us
    pallas_call x11, Pallas kernels, call(): pl.pallas_call(kernel, out_shape=[result(shape, kind) for shape, kind in...  13.5 us
  transfers between devices with their start and end apart: 16, of which 11 were waited for; matrix products, arithmetic and copies ran while one was open for 1% of the time, Pallas kernels for 5%

profile of v5, /device:TPU:0, one launch (start us, length us, event | category | flops | bytes accessed | tf_op | source)
XLA Modules:
  0.0 88.0 jit_solution(6610811112506283314)
XLA Ops:
  0.6 3.1 %collective-permute-start.1 = (bf16[256,1024]{1,0:T(8,128)(2,1)}, bf16[256,1024]{1,0:T(8,128)(2,1)S(1)}, u32[]{:S(2)}, u32[]{:S(2)}) collective-permute-start(bf16[256,1024]{1,0:T(8,128)(2,1)} %refs_4_.1), channel_id=1, source_target_pairs={{0,16},{1,17},{2,18},{3,19},{4,20},{5,21},{6,22},{7,23},{8,24},{9,... | collective-permute-start | bytes 1572872 | tf_op jit(solution)/shard_map/ppermute | solution.py:336
  3.7 12.1 %collective-permute-done.1.r0 = bf16[256,1024]{1,0:T(8,128)(2,1)S(1)} collective-permute-done((bf16[256,1024]{1,0:T(8,128)(2,1)}, bf16[256,1024]{1,0:T(8,128)(2,1)S(1)}, u32[]{:S(2)}, u32[]{:S(2)}) %collective-permute-start.1) | collective-permute-done | bytes 524320 | tf_op jit(solution)/shard_map/ppermute | solution.py:336
  15.8 1.1 %fusion = (bf16[128,1024]{1,0:T(8,128)(2,1)S(1)}, bf16[128,1024]{1,0:T(8,128)(2,1)S(1)}) fusion(bf16[256,1024]{1,0:T(8,128)(2,1)} %refs_4_.1), kind=kLoop, calls=%fused_computation.4 | loop fusion | bytes 1048576 | tf_op jit(solution)/shard_map/slice | solution.py:340
  16.9 1.8 %collective-permute-start.5 = (bf16[128,1024]{1,0:T(8,128)(2,1)S(1)}, bf16[128,1024]{1,0:T(8,128)(2,1)S(1)}, u32[]{:S(2)}, u32[]{:S(2)}) collective-permute-start(bf16[128,1024]{1,0:T(8,128)(2,1)S(1)} %get-tuple-element.66), channel_id=1, source_target_pairs={{0,1},{1,0},{2,3},{3,2},{4,5},{5,4},{6,7},{7,6},{8,9},{9,8},{10,11... | collective-permute-start | bytes 786440 | tf_op jit(solution)/shard_map/ppermute | solution.py:336
  18.7 7.0 %collective-permute-done.5.refs_5_ = bf16[128,1024]{1,0:T(8,128)(2,1)S(1)} collective-permute-done((bf16[128,1024]{1,0:T(8,128)(2,1)S(1)}, bf16[128,1024]{1,0:T(8,128)(2,1)S(1)}, u32[]{:S(2)}, u32[]{:S(2)}) %collective-permute-start.5) | collective-permute-done | bytes 262176 | tf_op jit(solution)/shard_map/ppermute | solution.py:336
  25.7 3.7 %collective-permute-start.6 = (bf16[128,1024]{1,0:T(8,128)(2,1)S(1)}, bf16[128,1024]{1,0:T(8,128)(2,1)S(1)}, u32[]{:S(2)}, u32[]{:S(2)}) collective-permute-start(bf16[128,1024]{1,0:T(8,128)(2,1)S(1)} %collective-permute-done.5.refs_5_), channel_id=1, source_target_pairs={{0,2},{2,4},{3,1},{4,6},{5,3},{7,5},{8,10},{10,12},{11,9},{12,14},... | collective-permute-start | bytes 786440 | tf_op jit(solution)/shard_map/ppermute | solution.py:336
  29.4 0.1 collective-permute-start.3
  29.6 0.7 copy-done.2
  30.3 1.0 %shard_map.59 = (f32[3,8,256]{2,1,0:T(8,128)S(1)}, f32[3,8,1024]{2,1,0:T(8,128)S(1)}) custom-call(s32[2]{0:T(128)S(1)} %compare_select_fusion.place, s32[32,256]{1,0:T(8,128)S(1)} %reshape.7.bins, s32[2,256]{1,0:T(2,128)S(1)} %bitcast.7), custom_call_target="tpu_custom_call" | custom-call | tf_op jit(solution)/shard_map/pallas_call | solution.py:38
  31.4 0.5 shard_map.60
  31.8 0.5 shard_map.61
  32.3 1.7 %shard_map.62 = (bf16[256,1024]{1,0:T(8,128)(2,1)S(1)}, bf16[256,1024]{1,0:T(8,128)(2,1)S(1)}, bf16[128,1024]{1,0:T(8,128)(2,1)S(1)}, bf16[128,1024]{1,0:T(8,128)(2,1)S(1)}, f32[1,1024]{1,0:T(1,128)S(1)}) custom-call(f32[3,8,256]{2,1,0:T(8,128)S(1)} %get-tuple-element.33.hots, f32[3,8,1024]{2,1,0:T(8,128)S(1)} %get-tuple-element.34.all_links, ...), custom_call_target="tpu_custom_call" | custom-call | tf_op jit(solution)/shard_map/pallas_call | solution.py:38
  34.0 0.8 collective-permute-done.6.refs_4_
  34.8 0.7 shard_map.63
  35.4 5.1 %collective-permute-done.3.refs_4_ = bf16[128,1024]{1,0:T(8,128)(2,1)S(1)} collective-permute-done((bf16[128,1024]{1,0:T(8,128)(2,1)S(1)}, bf16[128,1024]{1,0:T(8,128)(2,1)S(1)}, u32[]{:S(2)}, u32[]{:S(2)}) %collective-permute-start.3) | collective-permute-done | bytes 262176 | tf_op jit(solution)/shard_map/ppermute | solution.py:336
  40.5 1.2 %shard_map.64 = (bf16[128,1024]{1,0:T(8,128)(2,1)S(1)}, bf16[128,1024]{1,0:T(8,128)(2,1)S(1)}, bf16[128,1024]{1,0:T(8,128)(2,1)S(1)}, bf16[128,1024]{1,0:T(8,128)(2,1)S(1)}, f32[1,1024]{1,0:T(1,128)S(1)}) custom-call(f32[3,8,256]{2,1,0:T(8,128)S(1)} %get-tuple-element.33.hots, f32[3,8,1024]{2,1,0:T(8,128)S(1)} %get-tuple-element.34.all_links, ...), custom_call_target="tpu_custom_call" | custom-call | tf_op jit(solution)/shard_map/pallas_call | solution.py:38
  41.7 1.2 %collective-permute-done.7 = f32[1,1024]{1,0:T(1,128)S(1)} collective-permute-done((f32[1,1024]{1,0:T(1,128)S(1)}, f32[1,1024]{1,0:T(1,128)S(1)}, u32[]{:S(2)}, u32[]{:S(2)}) %collective-permute-start.7) | collective-permute-done | bytes 4128 | tf_op jit(solution)/shard_map/ppermute | solution.py:336
  42.9 1.6 %collective-permute-start.8 = (f32[1,1024]{1,0:T(1,128)S(1)}, f32[1,1024]{1,0:T(1,128)S(1)}, u32[]{:S(2)}, u32[]{:S(2)}) collective-permute-start(f32[1,1024]{1,0:T(1,128)S(1)} %maximum_add_fusion.degree), channel_id=1, source_target_pairs={{0,16},{1,17},{2,18},{3,19},{4,20},{5,21},{6,22},{7,23},{8,24},{9,... | collective-permute-start | bytes 12296 | tf_op jit(solution)/shard_map/ppermute | solution.py:336
  44.5 2.1 %collective-permute-done.8.got = f32[1,1024]{1,0:T(1,128)S(1)} collective-permute-done((f32[1,1024]{1,0:T(1,128)S(1)}, f32[1,1024]{1,0:T(1,128)S(1)}, u32[]{:S(2)}, u32[]{:S(2)}) %collective-permute-start.8) | collective-permute-done | bytes 4128 | tf_op jit(solution)/shard_map/ppermute | solution.py:336
  46.6 1.4 %shard_map.65 = (f32[1,256]{1,0:T(1,128)S(1)}, f32[32,256]{1,0:T(8,128)S(1)}, f32[32,256]{1,0:T(8,128)S(1)}, f32[32,256]{1,0:T(8,128)S(1)}) custom-call(f32[1,1024]{1,0:T(1,128)S(1)} %maximum_add_fusion.degree, f32[1,1024]{1,0:T(1,128)S(1)} %collective-permute-done.8.got, f32[32,512]{1,0:T(8,128)S(1)} %get-tuple-element.42.start_a, ...), custom_call_target="tpu_custom_call" | custom-call | tf_op jit(solution)/shard_map/pallas_call | solution.py:38
  48.0 5.2 %collective-permute-start.9 = (f32[32,256]{1,0:T(8,128)S(1)}, f32[32,256]{1,0:T(8,128)S(1)}, u32[]{:S(2)}, u32[]{:S(2)}) collective-permute-start(f32[32,256]{1,0:T(8,128)S(1)} %get-tuple-element.56), channel_id=1, source_target_pairs={{0,1},{1,0},{2,3},{3,2},{4,5},{5,4},{6,7},{7,6},{8,9},{9,8},{10,11... | collective-permute-start | bytes 98312 | tf_op jit(solution)/shard_map/ppermute | solution.py:336
  53.2 1.9 %collective-permute-done.9 = f32[32,256]{1,0:T(8,128)S(1)} collective-permute-done((f32[32,256]{1,0:T(8,128)S(1)}, f32[32,256]{1,0:T(8,128)S(1)}, u32[]{:S(2)}, u32[]{:S(2)}) %collective-permute-start.9) | collective-permute-done | bytes 32800 | tf_op jit(solution)/shard_map/ppermute | solution.py:336
  55.1 2.1 %collective-permute-start.11 = (f32[32,256]{1,0:T(8,128)S(1)}, f32[32,256]{1,0:T(8,128)S(1)}, u32[]{:S(2)}, u32[]{:S(2)}) collective-permute-start(f32[32,256]{1,0:T(8,128)S(1)} %get-tuple-element.64.refs_0_), channel_id=1, source_target_pairs={{0,1},{1,0},{2,3},{3,2},{4,5},{5,4},{6,7},{7,6},{8,9},{9,8},{10,11... | collective-permute-start | bytes 98312 | tf_op jit(solution)/shard_map/ppermute | solution.py:336
  57.2 1.9 %collective-permute-done.11.refs_1_ = f32[32,256]{1,0:T(8,128)S(1)} collective-permute-done((f32[32,256]{1,0:T(8,128)S(1)}, f32[32,256]{1,0:T(8,128)S(1)}, u32[]{:S(2)}, u32[]{:S(2)}) %collective-permute-start.11) | collective-permute-done | bytes 32800 | tf_op jit(solution)/shard_map/ppermute | solution.py:336
  59.1 0.6 shard_map.66
  59.8 1.2 %collective-permute-done.13 = f32[32,512]{1,0:T(8,128)S(1)} collective-permute-done((f32[32,512]{1,0:T(8,128)S(1)}, f32[32,512]{1,0:T(8,128)S(1)}, u32[]{:S(2)}, u32[]{:S(2)}) %collective-permute-start.13) | collective-permute-done | bytes 65568 | tf_op jit(solution)/shard_map/ppermute | solution.py:336
  61.1 1.6 %collective-permute-start.14 = (f32[32,256]{1,0:T(8,128)S(1)}, f32[32,256]{1,0:T(8,128)S(1)}, u32[]{:S(2)}, u32[]{:S(2)}) collective-permute-start(f32[32,256]{1,0:T(8,128)S(1)} %get-tuple-element.68), channel_id=1, source_target_pairs={{0,16},{1,17},{2,18},{3,19},{4,20},{5,21},{6,22},{7,23},{8,24},{9,... | collective-permute-start | bytes 98312 | tf_op jit(solution)/shard_map/ppermute | solution.py:336
  62.7 2.4 %collective-permute-done.14.got = f32[32,256]{1,0:T(8,128)S(1)} collective-permute-done((f32[32,256]{1,0:T(8,128)S(1)}, f32[32,256]{1,0:T(8,128)S(1)}, u32[]{:S(2)}, u32[]{:S(2)}) %collective-permute-start.14) | collective-permute-done | bytes 32800 | tf_op jit(solution)/shard_map/ppermute | solution.py:336
  65.1 0.4 shard_map.67
  65.5 1.2 %collective-permute-done.15.got = f32[24,128]{1,0:T(8,128)S(1)} collective-permute-done((f32[24,128]{1,0:T(8,128)S(1)}, f32[24,128]{1,0:T(8,128)S(1)}, u32[]{:S(2)}, u32[]{:S(2)}) %collective-permute-start.15) | collective-permute-done | bytes 12320 | tf_op jit(solution)/shard_map/ppermute | solution.py:336
  66.7 15.7 %all_to_all.5.parts = f32[16,24,128]{2,1,0:T(8,128)S(1)} all-to-all(f32[16,24,128]{2,1,0:T(8,128)S(1)} %shard_map.68), channel_id=1, replica_groups=mesh['row'=2,'core'=2,'inner'=8] {'row','inner'}, dimensions={0} | all-to-all | bytes 393216 | tf_op jit(solution)/shard_map/all_to_all | solution.py:416
  82.4 5.6 %shard_map.69 = (f32[96,256]{1,0:T(8,128)}, f32[4,32,32]{2,1,0:T(8,128)}) custom-call(f32[16,24,128]{2,1,0:T(8,128)S(1)} %all_to_all.5.parts, f32[32,256]{1,0:T(8,128)S(1)} %slice.36.start.v0, f32[32,256]{1,0:T(8,128)S(1)} %get-tuple-element.65.image.v1, f32[32,256]{1,0:T(8,128)S(1)} %get-tuple-element.61.v2), custom_call_target="tpu_custom_call" | custom-call | tf_op jit(solution)/shard_map/pallas_call | solution.py:38
  (29 shorter events, 0.4 us)
Async XLA Ops:
  0.6 30.7 %copy-start = (bf16[256,1024]{1,0:T(8,128)(2,1)S(1)}, bf16[256,1024]{1,0:T(8,128)(2,1)}, u32[]{:S(2)}) copy-start(bf16[256,1024]{1,0:T(8,128)(2,1)} %refs_4_.1) | copy-start | bytes 1572868
  0.6 15.2 %collective-permute-start.1 = (bf16[256,1024]{1,0:T(8,128)(2,1)}, bf16[256,1024]{1,0:T(8,128)(2,1)S(1)}, u32[]{:S(2)}, u32[]{:S(2)}) collective-permute-start(bf16[256,1024]{1,0:T(8,128)(2,1)} %refs_4_.1), channel_id=1, source_target_pairs={{0,16},{1,17},{2,18},{3,19},{4,20},{5,21},{6,22},{7,23},{8,24},{9,... | collective-permute-start | bytes 1572872 | tf_op jit(solution)/shard_map/ppermute | solution.py:336
  3.7 27.6 %collective-permute-start = (bf16[256,1024]{1,0:T(8,128)(2,1)}, bf16[256,1024]{1,0:T(8,128)(2,1)S(1)}, u32[]{:S(2)}, u32[]{:S(2)}) collective-permute-start(bf16[256,1024]{1,0:T(8,128)(2,1)} %refs_4_.1), channel_id=1, source_target_pairs={{0,8},{1,9},{2,10},{3,11},{4,12},{5,13},{6,14},{7,15},{8,0},{9,1},... | collective-permute-start | bytes 1572872 | tf_op jit(solution)/shard_map/ppermute | solution.py:336
  15.8 16.0 %collective-permute-start.2 = (bf16[256,1024]{1,0:T(8,128)(2,1)S(1)}, bf16[256,1024]{1,0:T(8,128)(2,1)S(1)}, u32[]{:S(2)}, u32[]{:S(2)}) collective-permute-start(bf16[256,1024]{1,0:T(8,128)(2,1)S(1)} %collective-permute-done.1.r0), channel_id=1, source_target_pairs={{0,8},{1,9},{2,10},{3,11},{4,12},{5,13},{6,14},{7,15},{8,0},{9,1},... | collective-permute-start | bytes 1572872 | tf_op jit(solution)/shard_map/ppermute | solution.py:336
  15.8 13.8 %copy-start.3 = (s32[8192]{0:T(1024)S(1)}, s32[8192]{0:T(1024)}, u32[]{:S(2)}) copy-start(s32[8192]{0:T(1024)} %param.5) | copy-start | bytes 98308
  16.9 14.4 %copy-start.1 = (bf16[1024,32]{0,1:T(8,128)(2,1)S(1)}, bf16[1024,32]{0,1:T(8,128)(2,1)}, u32[]{:S(2)}) copy-start(bf16[1024,32]{0,1:T(8,128)(2,1)} %param.7) | copy-start | bytes 196612
  16.9 8.8 %collective-permute-start.5 = (bf16[128,1024]{1,0:T(8,128)(2,1)S(1)}, bf16[128,1024]{1,0:T(8,128)(2,1)S(1)}, u32[]{:S(2)}, u32[]{:S(2)}) collective-permute-start(bf16[128,1024]{1,0:T(8,128)(2,1)S(1)} %get-tuple-element.66), channel_id=1, source_target_pairs={{0,1},{1,0},{2,3},{3,2},{4,5},{5,4},{6,7},{7,6},{8,9},{9,8},{10,11... | collective-permute-start | bytes 786440 | tf_op jit(solution)/shard_map/ppermute | solution.py:336
  25.7 9.1 %collective-permute-start.6 = (bf16[128,1024]{1,0:T(8,128)(2,1)S(1)}, bf16[128,1024]{1,0:T(8,128)(2,1)S(1)}, u32[]{:S(2)}, u32[]{:S(2)}) collective-permute-start(bf16[128,1024]{1,0:T(8,128)(2,1)S(1)} %collective-permute-done.5.refs_5_), channel_id=1, source_target_pairs={{0,2},{2,4},{3,1},{4,6},{5,3},{7,5},{8,10},{10,12},{11,9},{12,14},... | collective-permute-start | bytes 786440 | tf_op jit(solution)/shard_map/ppermute | solution.py:336
  29.4 11.1 %collective-permute-start.3 = (bf16[128,1024]{1,0:T(8,128)(2,1)S(1)}, bf16[128,1024]{1,0:T(8,128)(2,1)S(1)}, u32[]{:S(2)}, u32[]{:S(2)}) collective-permute-start(bf16[128,1024]{1,0:T(8,128)(2,1)S(1)} %get-tuple-element.67), channel_id=1, source_target_pairs={{0,1},{1,0},{2,3},{3,2},{4,5},{5,4},{6,7},{7,6},{8,9},{9,8},{10,11... | collective-permute-start | bytes 786440 | tf_op jit(solution)/shard_map/ppermute | solution.py:336
  29.5 11.0 %collective-permute-start.4 = (bf16[128,1024]{1,0:T(8,128)(2,1)S(1)}, bf16[128,1024]{1,0:T(8,128)(2,1)S(1)}, u32[]{:S(2)}, u32[]{:S(2)}) collective-permute-start(bf16[128,1024]{1,0:T(8,128)(2,1)S(1)} %get-tuple-element.67), channel_id=1, source_target_pairs={{0,8},{1,2},{2,1},{3,4},{4,3},{5,6},{6,5},{7,15},{8,0},{9,10},{10,... | collective-permute-start | bytes 786440 | tf_op jit(solution)/shard_map/ppermute | solution.py:336
  29.6 0.7 copy-start.2
  41.7 1.2 %collective-permute-start.7 = (f32[1,1024]{1,0:T(1,128)S(1)}, f32[1,1024]{1,0:T(1,128)S(1)}, u32[]{:S(2)}, u32[]{:S(2)}) collective-permute-start(f32[1,1024]{1,0:T(1,128)S(1)} %get-tuple-element.41), channel_id=1, source_target_pairs={{0,8},{1,9},{2,10},{3,11},{4,12},{5,13},{6,14},{7,15},{8,0},{9,1},... | collective-permute-start | bytes 12296 | tf_op jit(solution)/shard_map/ppermute | solution.py:336
  42.9 3.7 %collective-permute-start.8 = (f32[1,1024]{1,0:T(1,128)S(1)}, f32[1,1024]{1,0:T(1,128)S(1)}, u32[]{:S(2)}, u32[]{:S(2)}) collective-permute-start(f32[1,1024]{1,0:T(1,128)S(1)} %maximum_add_fusion.degree), channel_id=1, source_target_pairs={{0,16},{1,17},{2,18},{3,19},{4,20},{5,21},{6,22},{7,23},{8,24},{9,... | collective-permute-start | bytes 12296 | tf_op jit(solution)/shard_map/ppermute | solution.py:336
  48.0 5.3 %collective-permute-start.10 = (f32[32,256]{1,0:T(8,128)S(1)}, f32[32,256]{1,0:T(8,128)S(1)}, u32[]{:S(2)}, u32[]{:S(2)}) collective-permute-start(f32[32,256]{1,0:T(8,128)S(1)} %get-tuple-element.57), channel_id=1, source_target_pairs={{0,8},{1,2},{2,1},{3,4},{4,3},{5,6},{6,5},{7,15},{8,0},{9,10},{10,... | collective-permute-start | bytes 98312 | tf_op jit(solution)/shard_map/ppermute | solution.py:336
  48.0 7.1 %collective-permute-start.9 = (f32[32,256]{1,0:T(8,128)S(1)}, f32[32,256]{1,0:T(8,128)S(1)}, u32[]{:S(2)}, u32[]{:S(2)}) collective-permute-start(f32[32,256]{1,0:T(8,128)S(1)} %get-tuple-element.56), channel_id=1, source_target_pairs={{0,1},{1,0},{2,3},{3,2},{4,5},{5,4},{6,7},{7,6},{8,9},{9,8},{10,11... | collective-permute-start | bytes 98312 | tf_op jit(solution)/shard_map/ppermute | solution.py:336
  55.1 4.0 %collective-permute-start.11 = (f32[32,256]{1,0:T(8,128)S(1)}, f32[32,256]{1,0:T(8,128)S(1)}, u32[]{:S(2)}, u32[]{:S(2)}) collective-permute-start(f32[32,256]{1,0:T(8,128)S(1)} %get-tuple-element.64.refs_0_), channel_id=1, source_target_pairs={{0,1},{1,0},{2,3},{3,2},{4,5},{5,4},{6,7},{7,6},{8,9},{9,8},{10,11... | collective-permute-start | bytes 98312 | tf_op jit(solution)/shard_map/ppermute | solution.py:336
  57.2 1.9 %collective-permute-start.12 = (f32[32,256]{1,0:T(8,128)S(1)}, f32[32,256]{1,0:T(8,128)S(1)}, u32[]{:S(2)}, u32[]{:S(2)}) collective-permute-start(f32[32,256]{1,0:T(8,128)S(1)} %get-tuple-element.64.refs_0_), channel_id=1, source_target_pairs={{0,8},{1,2},{2,1},{3,4},{4,3},{5,6},{6,5},{7,15},{8,0},{9,10},{10,... | collective-permute-start | bytes 98312 | tf_op jit(solution)/shard_map/ppermute | solution.py:336
  59.7 1.3 %collective-permute-start.13 = (f32[32,512]{1,0:T(8,128)S(1)}, f32[32,512]{1,0:T(8,128)S(1)}, u32[]{:S(2)}, u32[]{:S(2)}) collective-permute-start(f32[32,512]{1,0:T(8,128)S(1)} %get-tuple-element.59), channel_id=1, source_target_pairs={{0,8},{1,9},{2,10},{3,11},{4,12},{5,13},{6,14},{7,15},{8,0},{9,1},... | collective-permute-start | bytes 196616 | tf_op jit(solution)/shard_map/ppermute | solution.py:336
  61.1 4.0 %collective-permute-start.14 = (f32[32,256]{1,0:T(8,128)S(1)}, f32[32,256]{1,0:T(8,128)S(1)}, u32[]{:S(2)}, u32[]{:S(2)}) collective-permute-start(f32[32,256]{1,0:T(8,128)S(1)} %get-tuple-element.68), channel_id=1, source_target_pairs={{0,16},{1,17},{2,18},{3,19},{4,20},{5,21},{6,22},{7,23},{8,24},{9,... | collective-permute-start | bytes 98312 | tf_op jit(solution)/shard_map/ppermute | solution.py:336
  65.5 1.2 %collective-permute-start.15 = (f32[24,128]{1,0:T(8,128)S(1)}, f32[24,128]{1,0:T(8,128)S(1)}, u32[]{:S(2)}, u32[]{:S(2)}) collective-permute-start(f32[24,128]{1,0:T(8,128)S(1)} %get-tuple-element.60.mine), channel_id=1, source_target_pairs={{0,8},{1,9},{2,10},{3,11},{4,12},{5,13},{6,14},{7,15},{8,0},{9,1},... | collective-permute-start | bytes 36872 | tf_op jit(solution)/shard_map/ppermute | solution.py:336

commit v6 on v5

--- a/solution.py
+++ b/solution.py
@@ -48,46 +48,79 @@
     return jnp.broadcast_to(value, (8, LANES))
 
 
-def pivot_rows(row_a, row_b, a, b, d, lane, at):
-    row_a = jnp.where(lane == at, 1.0, jnp.where(lane == at + 1, 0.0, row_a))
-    row_b = jnp.where(lane == at, 0.0, jnp.where(lane == at + 1, 1.0, row_b))
-    inverse = 1.0 / (a * d - b * b)
-    a, b, d = a * inverse, b * inverse, d * inverse
-    return d * row_a - b * row_b, a * row_b - b * row_a
-
-
 def eliminate(groups):
     sub = lax.broadcasted_iota(jnp.int32, (8, LANES), 0)
     lane = lax.broadcasted_iota(jnp.int32, (8, LANES), 1)
     g = list(groups)
-    for j in range(0, 8 * len(g), 4):
+    count = 8 * len(g)
+
+    def lane_of(value, j):
+        return spread(value[:, j:j + 1])
+
+    def row_of(value, s):
+        return spread(value[s:s + 1, :])
+
+    p = {}
+    for k in range(4):
+        col = lane_of(g[0], k)
+        for i in range(k + 1):
+            p[i, k] = row_of(col, i)
+    for j in range(0, count, 4):
         q, s = divmod(j, 8)
-        cols = [[spread(v[:, j + k:j + k + 1]) for v in g[q:]] for k in range(4)]
-        rows = [spread(g[q][s + k:s + k + 1, :]) for k in range(4)]
-        m = [[spread(cols[k][0][s + i:s + i + 1, :]) for k in range(4)] for i in range(4)]
+        cols = [[lane_of(v, j + k) for v in g[q:]] for k in range(4)]
+        rows = [row_of(g[q], s + k) for k in range(4)]
         first_pair = jnp.logical_or(lane == j, lane == j + 1)
         last_pair = jnp.logical_or(lane == j + 2, lane == j + 3)
-        w0, w1 = pivot_rows(rows[0], rows[1], m[0][0], m[0][1], m[1][1], lane, j)
-        inverse = 1.0 / (m[0][0] * m[1][1] - m[0][1] * m[0][1])
-        u = [
-            ((m[1][1] * m[0][k] - m[0][1] * m[1][k]) * inverse,
-             (m[0][0] * m[1][k] - m[0][1] * m[0][k]) * inverse)
-            for k in (2, 3)
-        ]
-        third = jnp.where(first_pair, 0.0, rows[2]) - (m[2][0] * w0 + m[2][1] * w1)
-        fourth = jnp.where(first_pair, 0.0, rows[3]) - (m[3][0] * w0 + m[3][1] * w1)
-        a = m[2][2] - (m[2][0] * u[0][0] + m[2][1] * u[0][1])
-        b = m[2][3] - (m[2][0] * u[1][0] + m[2][1] * u[1][1])
-        d = m[3][3] - (m[3][0] * u[1][0] + m[3][1] * u[1][1])
-        w2, w3 = pivot_rows(third, fourth, a, b, d, lane, j + 2)
+        pair = jnp.logical_or(first_pair, last_pair)
+
+        inverse = 1.0 / (p[0, 0] * p[1, 1] - p[0, 1] * p[0, 1])
+        d0, b0, a0 = p[1, 1] * inverse, p[0, 1] * inverse, p[0, 0] * inverse
+
+        def first_two(x, y):
+            return d0 * x - b0 * y, a0 * y - b0 * x
+
+        u2, u3 = first_two(p[0, 2], p[1, 2]), first_two(p[0, 3], p[1, 3])
+        a = p[2, 2] - (p[0, 2] * u2[0] + p[1, 2] * u2[1])
+        b = p[2, 3] - (p[0, 2] * u3[0] + p[1, 2] * u3[1])
+        d = p[3, 3] - (p[0, 3] * u3[0] + p[1, 3] * u3[1])
+        inverse = 1.0 / (a * d - b * b)
+        d1, b1, a1 = d * inverse, b * inverse, a * inverse
+
+        def last_two(x, y):
+            return d1 * x - b1 * y, a1 * y - b1 * x
+
+        n = j + 4
+        if n < count:
+            r, t = divmod(n, 8)
+            c = [[row_of(cols[k][r - q], t + i) for i in range(4)] for k in range(4)]
+            w01 = [first_two(c[0][i], c[1][i]) for i in range(4)]
+            c2 = [c[2][i] - (c[0][i] * u2[0] + c[1][i] * u2[1]) for i in range(4)]
+            c3 = [c[3][i] - (c[0][i] * u3[0] + c[1][i] * u3[1]) for i in range(4)]
+            w23 = [last_two(c2[i], c3[i]) for i in range(4)]
+            p = {}
+            for k in range(4):
+                col = lane_of(g[r], n + k)
+                for i in range(k + 1):
+                    p[i, k] = row_of(col, t + i) - (
+                        (c[0][i] * w01[k][0] + c[1][i] * w01[k][1])
+                        + (c2[i] * w23[k][0] + c3[i] * w23[k][1])
+                    )
+
+        one = jnp.where(lane == j, 1.0, jnp.where(lane == j + 1, 0.0, rows[0]))
+        two = jnp.where(lane == j, 0.0, jnp.where(lane == j + 1, 1.0, rows[1]))
+        w0, w1 = first_two(one, two)
+        third = jnp.where(first_pair, 0.0, rows[2]) - (u2[0] * one + u2[1] * two)
+        fourth = jnp.where(first_pair, 0.0, rows[3]) - (u3[0] * one + u3[1] * two)
+        three = jnp.where(lane == j + 2, 1.0, jnp.where(lane == j + 3, 0.0, third))
+        four = jnp.where(lane == j + 2, 0.0, jnp.where(lane == j + 3, 1.0, fourth))
+        w2, w3 = last_two(three, four)
         clear_0, clear_1 = jnp.where(last_pair, 0.0, w0), jnp.where(last_pair, 0.0, w1)
-        pair = jnp.logical_or(first_pair, last_pair)
         for i in range(len(g) - q):
-            c0, c1 = cols[0][i], cols[1][i]
-            c2 = cols[2][i] - (c0 * u[0][0] + c1 * u[0][1])
-            c3 = cols[3][i] - (c0 * u[1][0] + c1 * u[1][1])
+            k0, k1 = cols[0][i], cols[1][i]
+            k2 = cols[2][i] - (k0 * u2[0] + k1 * u2[1])
+            k3 = cols[3][i] - (k0 * u3[0] + k1 * u3[1])
             old = g[q + i]
-            new = jnp.where(pair, 0.0, old) - (c0 * clear_0 + c1 * clear_1) - (c2 * w2 + c3 * w3)
+            new = jnp.where(pair, 0.0, old) - ((k0 * clear_0 + k1 * clear_1) + (k2 * w2 + k3 * w3))
             if i == 0:
                 new = jnp.where(sub > s + 3, new, old)
                 new = jnp.where(sub == s + 2, third, jnp.where(sub == s + 3, fourth, new))

time: 88.2 us -> 86.8 us (0.984)
  Pallas kernels: 13.5 us -> 12.1 us
    pallas_call x11, Pallas kernels: 13.5 us -> 12.1 us  [call(): pl.pallas_call(kernel, out_shape=[result(shape, kind) for shape, kind in...]
where the time goes in v6:
time: 86.8 us; the launch traced here: 86.6 us
  waiting for transfers between devices  36.8 us (42%)
  starting transfers between devices  19.4 us (22%)
  blocking collectives  15.7 us (18%)
  Pallas kernels  12.1 us (14%)
  local copies, waits for them, and re-layouts  1.78 us (2%)
    ppermute x16, waiting for transfers between devices, move(): return lax.ppermute(value, ALL, route[name])  36.8 us
    ppermute x16, starting transfers between devices, move(): return lax.ppermute(value, ALL, route[name])  19.4 us
    all_to_all x1, blocking collectives, steps(): parts = lax.all_to_all(copies, ('row', 'inner'), 0, 0)  15.7 us
    pallas_call x11, Pallas kernels, call(): pl.pallas_call(kernel, out_shape=[result(shape, kind) for shape, kind in...  12.1 us
  transfers between devices with their start and end apart: 16, of which 11 were waited for; matrix products, arithmetic and copies ran while one was open for 1% of the time, Pallas kernels for 5%

profile of v6, /device:TPU:0, one launch (start us, length us, event | category | flops | bytes accessed | tf_op | source)
XLA Modules:
  0.0 86.6 jit_solution(17498370080674115872)
XLA Ops:
  0.6 3.1 %collective-permute-start.1 = (bf16[256,1024]{1,0:T(8,128)(2,1)}, bf16[256,1024]{1,0:T(8,128)(2,1)S(1)}, u32[]{:S(2)}, u32[]{:S(2)}) collective-permute-start(bf16[256,1024]{1,0:T(8,128)(2,1)} %refs_4_.1), channel_id=1, source_target_pairs={{0,16},{1,17},{2,18},{3,19},{4,20},{5,21},{6,22},{7,23},{8,24},{9,... | collective-permute-start | bytes 1572872 | tf_op jit(solution)/shard_map/ppermute | solution.py:369
  3.7 12.1 %collective-permute-done.1.r0 = bf16[256,1024]{1,0:T(8,128)(2,1)S(1)} collective-permute-done((bf16[256,1024]{1,0:T(8,128)(2,1)}, bf16[256,1024]{1,0:T(8,128)(2,1)S(1)}, u32[]{:S(2)}, u32[]{:S(2)}) %collective-permute-start.1) | collective-permute-done | bytes 524320 | tf_op jit(solution)/shard_map/ppermute | solution.py:369
  15.8 1.1 %fusion = (bf16[128,1024]{1,0:T(8,128)(2,1)S(1)}, bf16[128,1024]{1,0:T(8,128)(2,1)S(1)}) fusion(bf16[256,1024]{1,0:T(8,128)(2,1)} %refs_4_.1), kind=kLoop, calls=%fused_computation.4 | loop fusion | bytes 1048576 | tf_op jit(solution)/shard_map/slice | solution.py:373
  16.9 1.8 %collective-permute-start.5 = (bf16[128,1024]{1,0:T(8,128)(2,1)S(1)}, bf16[128,1024]{1,0:T(8,128)(2,1)S(1)}, u32[]{:S(2)}, u32[]{:S(2)}) collective-permute-start(bf16[128,1024]{1,0:T(8,128)(2,1)S(1)} %get-tuple-element.66), channel_id=1, source_target_pairs={{0,1},{1,0},{2,3},{3,2},{4,5},{5,4},{6,7},{7,6},{8,9},{9,8},{10,11... | collective-permute-start | bytes 786440 | tf_op jit(solution)/shard_map/ppermute | solution.py:369
  18.7 7.0 %collective-permute-done.5.refs_5_ = bf16[128,1024]{1,0:T(8,128)(2,1)S(1)} collective-permute-done((bf16[128,1024]{1,0:T(8,128)(2,1)S(1)}, bf16[128,1024]{1,0:T(8,128)(2,1)S(1)}, u32[]{:S(2)}, u32[]{:S(2)}) %collective-permute-start.5) | collective-permute-done | bytes 262176 | tf_op jit(solution)/shard_map/ppermute | solution.py:369
  25.7 3.7 %collective-permute-start.6 = (bf16[128,1024]{1,0:T(8,128)(2,1)S(1)}, bf16[128,1024]{1,0:T(8,128)(2,1)S(1)}, u32[]{:S(2)}, u32[]{:S(2)}) collective-permute-start(bf16[128,1024]{1,0:T(8,128)(2,1)S(1)} %collective-permute-done.5.refs_5_), channel_id=1, source_target_pairs={{0,2},{2,4},{3,1},{4,6},{5,3},{7,5},{8,10},{10,12},{11,9},{12,14},... | collective-permute-start | bytes 786440 | tf_op jit(solution)/shard_map/ppermute | solution.py:369
  29.4 0.1 collective-permute-start.3
  29.6 0.7 copy-done.2
  30.3 1.0 %shard_map.59 = (f32[3,8,256]{2,1,0:T(8,128)S(1)}, f32[3,8,1024]{2,1,0:T(8,128)S(1)}) custom-call(s32[2]{0:T(128)S(1)} %compare_select_fusion.place, s32[32,256]{1,0:T(8,128)S(1)} %reshape.7.bins, s32[2,256]{1,0:T(2,128)S(1)} %bitcast.7), custom_call_target="tpu_custom_call" | custom-call | tf_op jit(solution)/shard_map/pallas_call | solution.py:38
  31.4 0.5 shard_map.60
  31.8 0.5 shard_map.61
  32.3 1.7 %shard_map.62 = (bf16[256,1024]{1,0:T(8,128)(2,1)S(1)}, bf16[256,1024]{1,0:T(8,128)(2,1)S(1)}, bf16[128,1024]{1,0:T(8,128)(2,1)S(1)}, bf16[128,1024]{1,0:T(8,128)(2,1)S(1)}, f32[1,1024]{1,0:T(1,128)S(1)}) custom-call(f32[3,8,256]{2,1,0:T(8,128)S(1)} %get-tuple-element.33.hots, f32[3,8,1024]{2,1,0:T(8,128)S(1)} %get-tuple-element.34.all_links, ...), custom_call_target="tpu_custom_call" | custom-call | tf_op jit(solution)/shard_map/pallas_call | solution.py:38
  34.0 0.8 collective-permute-done.6.refs_4_
  34.8 0.7 shard_map.63
  35.4 5.1 %collective-permute-done.3.refs_4_ = bf16[128,1024]{1,0:T(8,128)(2,1)S(1)} collective-permute-done((bf16[128,1024]{1,0:T(8,128)(2,1)S(1)}, bf16[128,1024]{1,0:T(8,128)(2,1)S(1)}, u32[]{:S(2)}, u32[]{:S(2)}) %collective-permute-start.3) | collective-permute-done | bytes 262176 | tf_op jit(solution)/shard_map/ppermute | solution.py:369
  40.5 1.2 %shard_map.64 = (bf16[128,1024]{1,0:T(8,128)(2,1)S(1)}, bf16[128,1024]{1,0:T(8,128)(2,1)S(1)}, bf16[128,1024]{1,0:T(8,128)(2,1)S(1)}, bf16[128,1024]{1,0:T(8,128)(2,1)S(1)}, f32[1,1024]{1,0:T(1,128)S(1)}) custom-call(f32[3,8,256]{2,1,0:T(8,128)S(1)} %get-tuple-element.33.hots, f32[3,8,1024]{2,1,0:T(8,128)S(1)} %get-tuple-element.34.all_links, ...), custom_call_target="tpu_custom_call" | custom-call | tf_op jit(solution)/shard_map/pallas_call | solution.py:38
  41.7 1.2 %collective-permute-done.7 = f32[1,1024]{1,0:T(1,128)S(1)} collective-permute-done((f32[1,1024]{1,0:T(1,128)S(1)}, f32[1,1024]{1,0:T(1,128)S(1)}, u32[]{:S(2)}, u32[]{:S(2)}) %collective-permute-start.7) | collective-permute-done | bytes 4128 | tf_op jit(solution)/shard_map/ppermute | solution.py:369
  42.9 1.6 %collective-permute-start.8 = (f32[1,1024]{1,0:T(1,128)S(1)}, f32[1,1024]{1,0:T(1,128)S(1)}, u32[]{:S(2)}, u32[]{:S(2)}) collective-permute-start(f32[1,1024]{1,0:T(1,128)S(1)} %maximum_add_fusion.degree), channel_id=1, source_target_pairs={{0,16},{1,17},{2,18},{3,19},{4,20},{5,21},{6,22},{7,23},{8,24},{9,... | collective-permute-start | bytes 12296 | tf_op jit(solution)/shard_map/ppermute | solution.py:369
  44.5 2.1 %collective-permute-done.8.got = f32[1,1024]{1,0:T(1,128)S(1)} collective-permute-done((f32[1,1024]{1,0:T(1,128)S(1)}, f32[1,1024]{1,0:T(1,128)S(1)}, u32[]{:S(2)}, u32[]{:S(2)}) %collective-permute-start.8) | collective-permute-done | bytes 4128 | tf_op jit(solution)/shard_map/ppermute | solution.py:369
  46.6 1.4 %shard_map.65 = (f32[1,256]{1,0:T(1,128)S(1)}, f32[32,256]{1,0:T(8,128)S(1)}, f32[32,256]{1,0:T(8,128)S(1)}, f32[32,256]{1,0:T(8,128)S(1)}) custom-call(f32[1,1024]{1,0:T(1,128)S(1)} %maximum_add_fusion.degree, f32[1,1024]{1,0:T(1,128)S(1)} %collective-permute-done.8.got, f32[32,512]{1,0:T(8,128)S(1)} %get-tuple-element.42.start_a, ...), custom_call_target="tpu_custom_call" | custom-call | tf_op jit(solution)/shard_map/pallas_call | solution.py:38
  48.0 5.2 %collective-permute-start.9 = (f32[32,256]{1,0:T(8,128)S(1)}, f32[32,256]{1,0:T(8,128)S(1)}, u32[]{:S(2)}, u32[]{:S(2)}) collective-permute-start(f32[32,256]{1,0:T(8,128)S(1)} %get-tuple-element.56), channel_id=1, source_target_pairs={{0,1},{1,0},{2,3},{3,2},{4,5},{5,4},{6,7},{7,6},{8,9},{9,8},{10,11... | collective-permute-start | bytes 98312 | tf_op jit(solution)/shard_map/ppermute | solution.py:369
  53.2 1.9 %collective-permute-done.9 = f32[32,256]{1,0:T(8,128)S(1)} collective-permute-done((f32[32,256]{1,0:T(8,128)S(1)}, f32[32,256]{1,0:T(8,128)S(1)}, u32[]{:S(2)}, u32[]{:S(2)}) %collective-permute-start.9) | collective-permute-done | bytes 32800 | tf_op jit(solution)/shard_map/ppermute | solution.py:369
  55.1 2.1 %collective-permute-start.11 = (f32[32,256]{1,0:T(8,128)S(1)}, f32[32,256]{1,0:T(8,128)S(1)}, u32[]{:S(2)}, u32[]{:S(2)}) collective-permute-start(f32[32,256]{1,0:T(8,128)S(1)} %get-tuple-element.64.refs_0_), channel_id=1, source_target_pairs={{0,1},{1,0},{2,3},{3,2},{4,5},{5,4},{6,7},{7,6},{8,9},{9,8},{10,11... | collective-permute-start | bytes 98312 | tf_op jit(solution)/shard_map/ppermute | solution.py:369
  57.2 1.9 %collective-permute-done.11.refs_1_ = f32[32,256]{1,0:T(8,128)S(1)} collective-permute-done((f32[32,256]{1,0:T(8,128)S(1)}, f32[32,256]{1,0:T(8,128)S(1)}, u32[]{:S(2)}, u32[]{:S(2)}) %collective-permute-start.11) | collective-permute-done | bytes 32800 | tf_op jit(solution)/shard_map/ppermute | solution.py:369
  59.1 0.6 shard_map.66
  59.8 1.2 %collective-permute-done.13 = f32[32,512]{1,0:T(8,128)S(1)} collective-permute-done((f32[32,512]{1,0:T(8,128)S(1)}, f32[32,512]{1,0:T(8,128)S(1)}, u32[]{:S(2)}, u32[]{:S(2)}) %collective-permute-start.13) | collective-permute-done | bytes 65568 | tf_op jit(solution)/shard_map/ppermute | solution.py:369
  61.1 1.6 %collective-permute-start.14 = (f32[32,256]{1,0:T(8,128)S(1)}, f32[32,256]{1,0:T(8,128)S(1)}, u32[]{:S(2)}, u32[]{:S(2)}) collective-permute-start(f32[32,256]{1,0:T(8,128)S(1)} %get-tuple-element.68), channel_id=1, source_target_pairs={{0,16},{1,17},{2,18},{3,19},{4,20},{5,21},{6,22},{7,23},{8,24},{9,... | collective-permute-start | bytes 98312 | tf_op jit(solution)/shard_map/ppermute | solution.py:369
  62.7 2.4 %collective-permute-done.14.got = f32[32,256]{1,0:T(8,128)S(1)} collective-permute-done((f32[32,256]{1,0:T(8,128)S(1)}, f32[32,256]{1,0:T(8,128)S(1)}, u32[]{:S(2)}, u32[]{:S(2)}) %collective-permute-start.14) | collective-permute-done | bytes 32800 | tf_op jit(solution)/shard_map/ppermute | solution.py:369
  65.1 0.4 shard_map.67
  65.5 1.2 %collective-permute-done.15.got = f32[24,128]{1,0:T(8,128)S(1)} collective-permute-done((f32[24,128]{1,0:T(8,128)S(1)}, f32[24,128]{1,0:T(8,128)S(1)}, u32[]{:S(2)}, u32[]{:S(2)}) %collective-permute-start.15) | collective-permute-done | bytes 12320 | tf_op jit(solution)/shard_map/ppermute | solution.py:369
  66.7 15.7 %all_to_all.5.parts = f32[16,24,128]{2,1,0:T(8,128)S(1)} all-to-all(f32[16,24,128]{2,1,0:T(8,128)S(1)} %shard_map.68), channel_id=1, replica_groups=mesh['row'=2,'core'=2,'inner'=8] {'row','inner'}, dimensions={0} | all-to-all | bytes 393216 | tf_op jit(solution)/shard_map/all_to_all | solution.py:449
  82.4 4.2 %shard_map.69 = (f32[96,256]{1,0:T(8,128)}, f32[4,32,32]{2,1,0:T(8,128)}) custom-call(f32[16,24,128]{2,1,0:T(8,128)S(1)} %all_to_all.5.parts, f32[32,256]{1,0:T(8,128)S(1)} %slice.36.start.v0, f32[32,256]{1,0:T(8,128)S(1)} %get-tuple-element.65.image.v1, f32[32,256]{1,0:T(8,128)S(1)} %get-tuple-element.61.v2), custom_call_target="tpu_custom_call" | custom-call | tf_op jit(solution)/shard_map/pallas_call | solution.py:38
  (29 shorter events, 0.4 us)
Async XLA Ops:
  0.6 30.7 %copy-start = (bf16[256,1024]{1,0:T(8,128)(2,1)S(1)}, bf16[256,1024]{1,0:T(8,128)(2,1)}, u32[]{:S(2)}) copy-start(bf16[256,1024]{1,0:T(8,128)(2,1)} %refs_4_.1) | copy-start | bytes 1572868
  0.6 15.2 %collective-permute-start.1 = (bf16[256,1024]{1,0:T(8,128)(2,1)}, bf16[256,1024]{1,0:T(8,128)(2,1)S(1)}, u32[]{:S(2)}, u32[]{:S(2)}) collective-permute-start(bf16[256,1024]{1,0:T(8,128)(2,1)} %refs_4_.1), channel_id=1, source_target_pairs={{0,16},{1,17},{2,18},{3,19},{4,20},{5,21},{6,22},{7,23},{8,24},{9,... | collective-permute-start | bytes 1572872 | tf_op jit(solution)/shard_map/ppermute | solution.py:369
  3.7 27.6 %collective-permute-start = (bf16[256,1024]{1,0:T(8,128)(2,1)}, bf16[256,1024]{1,0:T(8,128)(2,1)S(1)}, u32[]{:S(2)}, u32[]{:S(2)}) collective-permute-start(bf16[256,1024]{1,0:T(8,128)(2,1)} %refs_4_.1), channel_id=1, source_target_pairs={{0,8},{1,9},{2,10},{3,11},{4,12},{5,13},{6,14},{7,15},{8,0},{9,1},... | collective-permute-start | bytes 1572872 | tf_op jit(solution)/shard_map/ppermute | solution.py:369
  15.8 16.0 %collective-permute-start.2 = (bf16[256,1024]{1,0:T(8,128)(2,1)S(1)}, bf16[256,1024]{1,0:T(8,128)(2,1)S(1)}, u32[]{:S(2)}, u32[]{:S(2)}) collective-permute-start(bf16[256,1024]{1,0:T(8,128)(2,1)S(1)} %collective-permute-done.1.r0), channel_id=1, source_target_pairs={{0,8},{1,9},{2,10},{3,11},{4,12},{5,13},{6,14},{7,15},{8,0},{9,1},... | collective-permute-start | bytes 1572872 | tf_op jit(solution)/shard_map/ppermute | solution.py:369
  15.8 13.8 %copy-start.3 = (s32[8192]{0:T(1024)S(1)}, s32[8192]{0:T(1024)}, u32[]{:S(2)}) copy-start(s32[8192]{0:T(1024)} %param.5) | copy-start | bytes 98308
  16.9 14.4 %copy-start.1 = (bf16[1024,32]{0,1:T(8,128)(2,1)S(1)}, bf16[1024,32]{0,1:T(8,128)(2,1)}, u32[]{:S(2)}) copy-start(bf16[1024,32]{0,1:T(8,128)(2,1)} %param.7) | copy-start | bytes 196612
  16.9 8.8 %collective-permute-start.5 = (bf16[128,1024]{1,0:T(8,128)(2,1)S(1)}, bf16[128,1024]{1,0:T(8,128)(2,1)S(1)}, u32[]{:S(2)}, u32[]{:S(2)}) collective-permute-start(bf16[128,1024]{1,0:T(8,128)(2,1)S(1)} %get-tuple-element.66), channel_id=1, source_target_pairs={{0,1},{1,0},{2,3},{3,2},{4,5},{5,4},{6,7},{7,6},{8,9},{9,8},{10,11... | collective-permute-start | bytes 786440 | tf_op jit(solution)/shard_map/ppermute | solution.py:369
  25.7 9.1 %collective-permute-start.6 = (bf16[128,1024]{1,0:T(8,128)(2,1)S(1)}, bf16[128,1024]{1,0:T(8,128)(2,1)S(1)}, u32[]{:S(2)}, u32[]{:S(2)}) collective-permute-start(bf16[128,1024]{1,0:T(8,128)(2,1)S(1)} %collective-permute-done.5.refs_5_), channel_id=1, source_target_pairs={{0,2},{2,4},{3,1},{4,6},{5,3},{7,5},{8,10},{10,12},{11,9},{12,14},... | collective-permute-start | bytes 786440 | tf_op jit(solution)/shard_map/ppermute | solution.py:369
  29.4 11.1 %collective-permute-start.3 = (bf16[128,1024]{1,0:T(8,128)(2,1)S(1)}, bf16[128,1024]{1,0:T(8,128)(2,1)S(1)}, u32[]{:S(2)}, u32[]{:S(2)}) collective-permute-start(bf16[128,1024]{1,0:T(8,128)(2,1)S(1)} %get-tuple-element.67), channel_id=1, source_target_pairs={{0,1},{1,0},{2,3},{3,2},{4,5},{5,4},{6,7},{7,6},{8,9},{9,8},{10,11... | collective-permute-start | bytes 786440 | tf_op jit(solution)/shard_map/ppermute | solution.py:369
  29.5 11.0 %collective-permute-start.4 = (bf16[128,1024]{1,0:T(8,128)(2,1)S(1)}, bf16[128,1024]{1,0:T(8,128)(2,1)S(1)}, u32[]{:S(2)}, u32[]{:S(2)}) collective-permute-start(bf16[128,1024]{1,0:T(8,128)(2,1)S(1)} %get-tuple-element.67), channel_id=1, source_target_pairs={{0,8},{1,2},{2,1},{3,4},{4,3},{5,6},{6,5},{7,15},{8,0},{9,10},{10,... | collective-permute-start | bytes 786440 | tf_op jit(solution)/shard_map/ppermute | solution.py:369
  29.6 0.7 copy-start.2
  41.7 1.2 %collective-permute-start.7 = (f32[1,1024]{1,0:T(1,128)S(1)}, f32[1,1024]{1,0:T(1,128)S(1)}, u32[]{:S(2)}, u32[]{:S(2)}) collective-permute-start(f32[1,1024]{1,0:T(1,128)S(1)} %get-tuple-element.41), channel_id=1, source_target_pairs={{0,8},{1,9},{2,10},{3,11},{4,12},{5,13},{6,14},{7,15},{8,0},{9,1},... | collective-permute-start | bytes 12296 | tf_op jit(solution)/shard_map/ppermute | solution.py:369
  42.9 3.7 %collective-permute-start.8 = (f32[1,1024]{1,0:T(1,128)S(1)}, f32[1,1024]{1,0:T(1,128)S(1)}, u32[]{:S(2)}, u32[]{:S(2)}) collective-permute-start(f32[1,1024]{1,0:T(1,128)S(1)} %maximum_add_fusion.degree), channel_id=1, source_target_pairs={{0,16},{1,17},{2,18},{3,19},{4,20},{5,21},{6,22},{7,23},{8,24},{9,... | collective-permute-start | bytes 12296 | tf_op jit(solution)/shard_map/ppermute | solution.py:369
  48.0 5.3 %collective-permute-start.10 = (f32[32,256]{1,0:T(8,128)S(1)}, f32[32,256]{1,0:T(8,128)S(1)}, u32[]{:S(2)}, u32[]{:S(2)}) collective-permute-start(f32[32,256]{1,0:T(8,128)S(1)} %get-tuple-element.57), channel_id=1, source_target_pairs={{0,8},{1,2},{2,1},{3,4},{4,3},{5,6},{6,5},{7,15},{8,0},{9,10},{10,... | collective-permute-start | bytes 98312 | tf_op jit(solution)/shard_map/ppermute | solution.py:369
  48.0 7.1 %collective-permute-start.9 = (f32[32,256]{1,0:T(8,128)S(1)}, f32[32,256]{1,0:T(8,128)S(1)}, u32[]{:S(2)}, u32[]{:S(2)}) collective-permute-start(f32[32,256]{1,0:T(8,128)S(1)} %get-tuple-element.56), channel_id=1, source_target_pairs={{0,1},{1,0},{2,3},{3,2},{4,5},{5,4},{6,7},{7,6},{8,9},{9,8},{10,11... | collective-permute-start | bytes 98312 | tf_op jit(solution)/shard_map/ppermute | solution.py:369
  55.1 4.0 %collective-permute-start.11 = (f32[32,256]{1,0:T(8,128)S(1)}, f32[32,256]{1,0:T(8,128)S(1)}, u32[]{:S(2)}, u32[]{:S(2)}) collective-permute-start(f32[32,256]{1,0:T(8,128)S(1)} %get-tuple-element.64.refs_0_), channel_id=1, source_target_pairs={{0,1},{1,0},{2,3},{3,2},{4,5},{5,4},{6,7},{7,6},{8,9},{9,8},{10,11... | collective-permute-start | bytes 98312 | tf_op jit(solution)/shard_map/ppermute | solution.py:369
  57.2 1.9 %collective-permute-start.12 = (f32[32,256]{1,0:T(8,128)S(1)}, f32[32,256]{1,0:T(8,128)S(1)}, u32[]{:S(2)}, u32[]{:S(2)}) collective-permute-start(f32[32,256]{1,0:T(8,128)S(1)} %get-tuple-element.64.refs_0_), channel_id=1, source_target_pairs={{0,8},{1,2},{2,1},{3,4},{4,3},{5,6},{6,5},{7,15},{8,0},{9,10},{10,... | collective-permute-start | bytes 98312 | tf_op jit(solution)/shard_map/ppermute | solution.py:369
  59.7 1.3 %collective-permute-start.13 = (f32[32,512]{1,0:T(8,128)S(1)}, f32[32,512]{1,0:T(8,128)S(1)}, u32[]{:S(2)}, u32[]{:S(2)}) collective-permute-start(f32[32,512]{1,0:T(8,128)S(1)} %get-tuple-element.59), channel_id=1, source_target_pairs={{0,8},{1,9},{2,10},{3,11},{4,12},{5,13},{6,14},{7,15},{8,0},{9,1},... | collective-permute-start | bytes 196616 | tf_op jit(solution)/shard_map/ppermute | solution.py:369
  61.1 4.0 %collective-permute-start.14 = (f32[32,256]{1,0:T(8,128)S(1)}, f32[32,256]{1,0:T(8,128)S(1)}, u32[]{:S(2)}, u32[]{:S(2)}) collective-permute-start(f32[32,256]{1,0:T(8,128)S(1)} %get-tuple-element.68), channel_id=1, source_target_pairs={{0,16},{1,17},{2,18},{3,19},{4,20},{5,21},{6,22},{7,23},{8,24},{9,... | collective-permute-start | bytes 98312 | tf_op jit(solution)/shard_map/ppermute | solution.py:369
  65.5 1.2 %collective-permute-start.15 = (f32[24,128]{1,0:T(8,128)S(1)}, f32[24,128]{1,0:T(8,128)S(1)}, u32[]{:S(2)}, u32[]{:S(2)}) collective-permute-start(f32[24,128]{1,0:T(8,128)S(1)} %get-tuple-element.60.mine), channel_id=1, source_target_pairs={{0,8},{1,9},{2,10},{3,11},{4,12},{5,13},{6,14},{7,15},{8,0},{9,1},... | collective-permute-start | bytes 36872 | tf_op jit(solution)/shard_map/ppermute | solution.py:369

commit v7 on v6

--- a/solution.py
+++ b/solution.py
@@ -212,18 +212,19 @@
     other = jnp.concatenate([got[:, size * i:size * (i + 1)] for i in (2, 3, 0, 1)], axis=1)
     scale = lax.rsqrt(degree[...] + other)
     inv_root[...] = scale[:, :size]
-    vectors = (jnp.concatenate([start_a[...], start_b[...]], axis=1) * scale).T
+    vectors = (jnp.concatenate([start_a[...], start_b[...]], axis=1) * scale)
     top = vectors.astype(BF16)
     low = (vectors - top.astype(F32)).astype(BF16)
-    both = jnp.concatenate([top, low], axis=1)
+    both = jnp.concatenate([top, low], axis=0)
     pieces = []
     for i in range(len(tiles) // 2):
-        piece = nn(tiles[2 * i][...], both, None)
-        pieces.append(piece[:, :width] + piece[:, width:] + nn(tiles[2 * i + 1][...], top, None))
-    own[...] = pieces[0].T
+        high = tiles[2 * i][...]
+        piece = nt(both, high, None)
+        pieces.append(piece[:width] + piece[width:] + nt(top, tiles[2 * i + 1][...], None))
+    own[...] = pieces[0]
     cut = (len(pieces) + 1) // 2
-    near[...] = jnp.concatenate(pieces[1:cut], axis=0).T
-    far[...] = jnp.concatenate(pieces[cut:], axis=0).T
+    near[...] = jnp.concatenate(pieces[1:cut], axis=1)
+    far[...] = jnp.concatenate(pieces[cut:], axis=1)
 
 
 def apply_kernel(*refs):
@@ -370,10 +371,11 @@
 
     half = row_count // 2
     across = move(snapshots, "row")
-    near_a = move(snapshots[:half], "near")
+    first_half, later = lax.optimization_barrier((snapshots[:half], snapshots))
+    near_a = move(first_half, "near")
     mate = move(snapshots, "core")
-    far_b = move(snapshots[half:], "far")
-    near_b = move(snapshots[half:], "near")
+    far_b = move(later[half:], "far")
+    near_b = move(later[half:], "near")
     far_a = move(near_a, "relay")
     across_mate = move(across, "core")
 

time: 86.8 us -> 86.5 us (level)
  no operation moved by 1% of the time
where the time goes in v7:
time: 86.5 us; the launch traced here: 86.2 us
  waiting for transfers between devices  36.3 us (42%)
  starting transfers between devices  19.3 us (22%)
  blocking collectives  15.7 us (18%)
  Pallas kernels  11.8 us (14%)
  local copies, waits for them, and re-layouts  2.24 us (3%)
    ppermute x16, waiting for transfers between devices, move(): return lax.ppermute(value, ALL, route[name])  36.3 us
    ppermute x16, starting transfers between devices, move(): return lax.ppermute(value, ALL, route[name])  19.3 us
    all_to_all x1, blocking collectives, steps(): parts = lax.all_to_all(copies, ('row', 'inner'), 0, 0)  15.7 us
    pallas_call x11, Pallas kernels, call(): pl.pallas_call(kernel, out_shape=[result(shape, kind) for shape, kind in...  11.8 us
  transfers between devices with their start and end apart: 16, of which 11 were waited for; matrix products, arithmetic and copies ran while one was open for 1% of the time, Pallas kernels for 5%

profile of v7, /device:TPU:0, one launch (start us, length us, event | category | flops | bytes accessed | tf_op | source)
XLA Modules:
  0.0 86.2 jit_solution(4526151036710018849)
XLA Ops:
  0.6 3.1 %collective-permute-start.1 = (bf16[256,1024]{1,0:T(8,128)(2,1)}, bf16[256,1024]{1,0:T(8,128)(2,1)S(1)}, u32[]{:S(2)}, u32[]{:S(2)}) collective-permute-start(bf16[256,1024]{1,0:T(8,128)(2,1)} %refs_4_.1), channel_id=1, source_target_pairs={{0,16},{1,17},{2,18},{3,19},{4,20},{5,21},{6,22},{7,23},{8,24},{9,... | collective-permute-start | bytes 1572872 | tf_op jit(solution)/shard_map/ppermute | solution.py:370
  3.7 12.1 %collective-permute-done.1.r0 = bf16[256,1024]{1,0:T(8,128)(2,1)S(1)} collective-permute-done((bf16[256,1024]{1,0:T(8,128)(2,1)}, bf16[256,1024]{1,0:T(8,128)(2,1)S(1)}, u32[]{:S(2)}, u32[]{:S(2)}) %collective-permute-start.1) | collective-permute-done | bytes 524320 | tf_op jit(solution)/shard_map/ppermute | solution.py:370
  15.8 1.0 %slice.28 = bf16[128,1024]{1,0:T(8,128)(2,1)S(1)} slice(bf16[256,1024]{1,0:T(8,128)(2,1)} %refs_4_.1), slice={[0:128], [0:1024]} | slice | bytes 524288 | tf_op jit(solution)/shard_map/slice | solution.py:374
  16.8 1.8 %collective-permute-start.5 = (bf16[128,1024]{1,0:T(8,128)(2,1)S(1)}, bf16[128,1024]{1,0:T(8,128)(2,1)S(1)}, u32[]{:S(2)}, u32[]{:S(2)}) collective-permute-start(bf16[128,1024]{1,0:T(8,128)(2,1)S(1)} %slice.28), channel_id=1, source_target_pairs={{0,1},{1,0},{2,3},{3,2},{4,5},{5,4},{6,7},{7,6},{8,9},{9,8},{10,11... | collective-permute-start | bytes 786440 | tf_op jit(solution)/shard_map/ppermute | solution.py:370
  18.6 7.0 %collective-permute-done.5.refs_5_ = bf16[128,1024]{1,0:T(8,128)(2,1)S(1)} collective-permute-done((bf16[128,1024]{1,0:T(8,128)(2,1)S(1)}, bf16[128,1024]{1,0:T(8,128)(2,1)S(1)}, u32[]{:S(2)}, u32[]{:S(2)}) %collective-permute-start.5) | collective-permute-done | bytes 262176 | tf_op jit(solution)/shard_map/ppermute | solution.py:370
  25.6 3.7 %collective-permute-start.6 = (bf16[128,1024]{1,0:T(8,128)(2,1)S(1)}, bf16[128,1024]{1,0:T(8,128)(2,1)S(1)}, u32[]{:S(2)}, u32[]{:S(2)}) collective-permute-start(bf16[128,1024]{1,0:T(8,128)(2,1)S(1)} %collective-permute-done.5.refs_5_), channel_id=1, source_target_pairs={{0,2},{2,4},{3,1},{4,6},{5,3},{7,5},{8,10},{10,12},{11,9},{12,14},... | collective-permute-start | bytes 786440 | tf_op jit(solution)/shard_map/ppermute | solution.py:370
  29.5 0.5 copy-done.3
  30.1 0.7 copy-done.2
  30.8 1.0 %shard_map.59 = (f32[3,8,256]{2,1,0:T(8,128)S(1)}, f32[3,8,1024]{2,1,0:T(8,128)S(1)}) custom-call(s32[2]{0:T(128)S(1)} %compare_select_fusion.place, s32[32,256]{1,0:T(8,128)S(1)} %reshape.7.bins, s32[2,256]{1,0:T(2,128)S(1)} %bitcast.7), custom_call_target="tpu_custom_call" | custom-call | tf_op jit(solution)/shard_map/pallas_call | solution.py:38
  31.8 0.5 shard_map.60
  32.3 0.5 shard_map.61
  32.8 1.6 %shard_map.62 = (bf16[256,1024]{1,0:T(8,128)(2,1)S(1)}, bf16[256,1024]{1,0:T(8,128)(2,1)S(1)}, bf16[128,1024]{1,0:T(8,128)(2,1)S(1)}, bf16[128,1024]{1,0:T(8,128)(2,1)S(1)}, f32[1,1024]{1,0:T(1,128)S(1)}) custom-call(f32[3,8,256]{2,1,0:T(8,128)S(1)} %get-tuple-element.35.hots, f32[3,8,1024]{2,1,0:T(8,128)S(1)} %get-tuple-element.36.all_links, ...), custom_call_target="tpu_custom_call" | custom-call | tf_op jit(solution)/shard_map/pallas_call | solution.py:38
  34.4 0.2 collective-permute-done.6.refs_4_
  34.6 0.7 shard_map.63
  35.3 5.1 %collective-permute-done.3.refs_4_ = bf16[128,1024]{1,0:T(8,128)(2,1)S(1)} collective-permute-done((bf16[128,1024]{1,0:T(8,128)(2,1)S(1)}, bf16[128,1024]{1,0:T(8,128)(2,1)S(1)}, u32[]{:S(2)}, u32[]{:S(2)}) %collective-permute-start.3) | collective-permute-done | bytes 262176 | tf_op jit(solution)/shard_map/ppermute | solution.py:370
  40.4 1.2 %shard_map.64 = (bf16[128,1024]{1,0:T(8,128)(2,1)S(1)}, bf16[128,1024]{1,0:T(8,128)(2,1)S(1)}, bf16[128,1024]{1,0:T(8,128)(2,1)S(1)}, bf16[128,1024]{1,0:T(8,128)(2,1)S(1)}, f32[1,1024]{1,0:T(1,128)S(1)}) custom-call(f32[3,8,256]{2,1,0:T(8,128)S(1)} %get-tuple-element.35.hots, f32[3,8,1024]{2,1,0:T(8,128)S(1)} %get-tuple-element.36.all_links, ...), custom_call_target="tpu_custom_call" | custom-call | tf_op jit(solution)/shard_map/pallas_call | solution.py:38
  41.7 1.2 %collective-permute-done.7 = f32[1,1024]{1,0:T(1,128)S(1)} collective-permute-done((f32[1,1024]{1,0:T(1,128)S(1)}, f32[1,1024]{1,0:T(1,128)S(1)}, u32[]{:S(2)}, u32[]{:S(2)}) %collective-permute-start.7) | collective-permute-done | bytes 4128 | tf_op jit(solution)/shard_map/ppermute | solution.py:370
  42.9 1.6 %collective-permute-start.8 = (f32[1,1024]{1,0:T(1,128)S(1)}, f32[1,1024]{1,0:T(1,128)S(1)}, u32[]{:S(2)}, u32[]{:S(2)}) collective-permute-start(f32[1,1024]{1,0:T(1,128)S(1)} %maximum_add_fusion.degree), channel_id=1, source_target_pairs={{0,16},{1,17},{2,18},{3,19},{4,20},{5,21},{6,22},{7,23},{8,24},{9,... | collective-permute-start | bytes 12296 | tf_op jit(solution)/shard_map/ppermute | solution.py:370
  44.4 2.1 %collective-permute-done.8.got = f32[1,1024]{1,0:T(1,128)S(1)} collective-permute-done((f32[1,1024]{1,0:T(1,128)S(1)}, f32[1,1024]{1,0:T(1,128)S(1)}, u32[]{:S(2)}, u32[]{:S(2)}) %collective-permute-start.8) | collective-permute-done | bytes 4128 | tf_op jit(solution)/shard_map/ppermute | solution.py:370
  46.5 1.1 %shard_map.65 = (f32[1,256]{1,0:T(1,128)S(1)}, f32[32,256]{1,0:T(8,128)S(1)}, f32[32,256]{1,0:T(8,128)S(1)}, f32[32,256]{1,0:T(8,128)S(1)}) custom-call(f32[1,1024]{1,0:T(1,128)S(1)} %maximum_add_fusion.degree, f32[1,1024]{1,0:T(1,128)S(1)} %collective-permute-done.8.got, f32[32,512]{1,0:T(8,128)S(1)} %get-tuple-element.46.start_a, ...), custom_call_target="tpu_custom_call" | custom-call | tf_op jit(solution)/shard_map/pallas_call | solution.py:38
  47.6 5.2 %collective-permute-start.9 = (f32[32,256]{1,0:T(8,128)S(1)}, f32[32,256]{1,0:T(8,128)S(1)}, u32[]{:S(2)}, u32[]{:S(2)}) collective-permute-start(f32[32,256]{1,0:T(8,128)S(1)} %get-tuple-element.60), channel_id=1, source_target_pairs={{0,1},{1,0},{2,3},{3,2},{4,5},{5,4},{6,7},{7,6},{8,9},{9,8},{10,11... | collective-permute-start | bytes 98312 | tf_op jit(solution)/shard_map/ppermute | solution.py:370
  52.8 1.9 %collective-permute-done.9 = f32[32,256]{1,0:T(8,128)S(1)} collective-permute-done((f32[32,256]{1,0:T(8,128)S(1)}, f32[32,256]{1,0:T(8,128)S(1)}, u32[]{:S(2)}, u32[]{:S(2)}) %collective-permute-start.9) | collective-permute-done | bytes 32800 | tf_op jit(solution)/shard_map/ppermute | solution.py:370
  54.7 2.1 %collective-permute-start.11 = (f32[32,256]{1,0:T(8,128)S(1)}, f32[32,256]{1,0:T(8,128)S(1)}, u32[]{:S(2)}, u32[]{:S(2)}) collective-permute-start(f32[32,256]{1,0:T(8,128)S(1)} %get-tuple-element.68.refs_0_), channel_id=1, source_target_pairs={{0,1},{1,0},{2,3},{3,2},{4,5},{5,4},{6,7},{7,6},{8,9},{9,8},{10,11... | collective-permute-start | bytes 98312 | tf_op jit(solution)/shard_map/ppermute | solution.py:370
  56.8 1.9 %collective-permute-done.11.refs_1_ = f32[32,256]{1,0:T(8,128)S(1)} collective-permute-done((f32[32,256]{1,0:T(8,128)S(1)}, f32[32,256]{1,0:T(8,128)S(1)}, u32[]{:S(2)}, u32[]{:S(2)}) %collective-permute-start.11) | collective-permute-done | bytes 32800 | tf_op jit(solution)/shard_map/ppermute | solution.py:370
  58.7 0.6 shard_map.66
  59.4 1.2 %collective-permute-done.13 = f32[32,512]{1,0:T(8,128)S(1)} collective-permute-done((f32[32,512]{1,0:T(8,128)S(1)}, f32[32,512]{1,0:T(8,128)S(1)}, u32[]{:S(2)}, u32[]{:S(2)}) %collective-permute-start.13) | collective-permute-done | bytes 65568 | tf_op jit(solution)/shard_map/ppermute | solution.py:370
  60.7 1.6 %collective-permute-start.14 = (f32[32,256]{1,0:T(8,128)S(1)}, f32[32,256]{1,0:T(8,128)S(1)}, u32[]{:S(2)}, u32[]{:S(2)}) collective-permute-start(f32[32,256]{1,0:T(8,128)S(1)} %get-tuple-element.70), channel_id=1, source_target_pairs={{0,16},{1,17},{2,18},{3,19},{4,20},{5,21},{6,22},{7,23},{8,24},{9,... | collective-permute-start | bytes 98312 | tf_op jit(solution)/shard_map/ppermute | solution.py:370
  62.3 2.4 %collective-permute-done.14.got = f32[32,256]{1,0:T(8,128)S(1)} collective-permute-done((f32[32,256]{1,0:T(8,128)S(1)}, f32[32,256]{1,0:T(8,128)S(1)}, u32[]{:S(2)}, u32[]{:S(2)}) %collective-permute-start.14) | collective-permute-done | bytes 32800 | tf_op jit(solution)/shard_map/ppermute | solution.py:370
  64.7 0.4 shard_map.67
  65.1 1.2 %collective-permute-done.15.got = f32[24,128]{1,0:T(8,128)S(1)} collective-permute-done((f32[24,128]{1,0:T(8,128)S(1)}, f32[24,128]{1,0:T(8,128)S(1)}, u32[]{:S(2)}, u32[]{:S(2)}) %collective-permute-start.15) | collective-permute-done | bytes 12320 | tf_op jit(solution)/shard_map/ppermute | solution.py:370
  66.3 15.7 %all_to_all.5.parts = f32[16,24,128]{2,1,0:T(8,128)S(1)} all-to-all(f32[16,24,128]{2,1,0:T(8,128)S(1)} %shard_map.68), channel_id=1, replica_groups=mesh['row'=2,'core'=2,'inner'=8] {'row','inner'}, dimensions={0} | all-to-all | bytes 393216 | tf_op jit(solution)/shard_map/all_to_all | solution.py:451
  82.0 4.2 %shard_map.69 = (f32[96,256]{1,0:T(8,128)}, f32[4,32,32]{2,1,0:T(8,128)}) custom-call(f32[16,24,128]{2,1,0:T(8,128)S(1)} %all_to_all.5.parts, f32[32,256]{1,0:T(8,128)S(1)} %slice.36.start.v0, f32[32,256]{1,0:T(8,128)S(1)} %get-tuple-element.69.image.v1, f32[32,256]{1,0:T(8,128)S(1)} %get-tuple-element.65.v2), custom_call_target="tpu_custom_call" | custom-call | tf_op jit(solution)/shard_map/pallas_call | solution.py:38
  (30 shorter events, 0.4 us)
Async XLA Ops:
  0.6 28.7 %copy-start = (bf16[256,1024]{1,0:T(8,128)(2,1)S(1)}, bf16[256,1024]{1,0:T(8,128)(2,1)}, u32[]{:S(2)}) copy-start(bf16[256,1024]{1,0:T(8,128)(2,1)} %refs_4_.1) | copy-start | bytes 1572868
  0.6 15.2 %collective-permute-start.1 = (bf16[256,1024]{1,0:T(8,128)(2,1)}, bf16[256,1024]{1,0:T(8,128)(2,1)S(1)}, u32[]{:S(2)}, u32[]{:S(2)}) collective-permute-start(bf16[256,1024]{1,0:T(8,128)(2,1)} %refs_4_.1), channel_id=1, source_target_pairs={{0,16},{1,17},{2,18},{3,19},{4,20},{5,21},{6,22},{7,23},{8,24},{9,... | collective-permute-start | bytes 1572872 | tf_op jit(solution)/shard_map/ppermute | solution.py:370
  3.7 28.1 %collective-permute-start = (bf16[256,1024]{1,0:T(8,128)(2,1)}, bf16[256,1024]{1,0:T(8,128)(2,1)S(1)}, u32[]{:S(2)}, u32[]{:S(2)}) collective-permute-start(bf16[256,1024]{1,0:T(8,128)(2,1)} %refs_4_.1), channel_id=1, source_target_pairs={{0,8},{1,9},{2,10},{3,11},{4,12},{5,13},{6,14},{7,15},{8,0},{9,1},... | collective-permute-start | bytes 1572872 | tf_op jit(solution)/shard_map/ppermute | solution.py:370
  15.8 16.5 %collective-permute-start.2 = (bf16[256,1024]{1,0:T(8,128)(2,1)S(1)}, bf16[256,1024]{1,0:T(8,128)(2,1)S(1)}, u32[]{:S(2)}, u32[]{:S(2)}) collective-permute-start(bf16[256,1024]{1,0:T(8,128)(2,1)S(1)} %collective-permute-done.1.r0), channel_id=1, source_target_pairs={{0,8},{1,9},{2,10},{3,11},{4,12},{5,13},{6,14},{7,15},{8,0},{9,1},... | collective-permute-start | bytes 1572872 | tf_op jit(solution)/shard_map/ppermute | solution.py:370
  16.8 8.8 %collective-permute-start.5 = (bf16[128,1024]{1,0:T(8,128)(2,1)S(1)}, bf16[128,1024]{1,0:T(8,128)(2,1)S(1)}, u32[]{:S(2)}, u32[]{:S(2)}) collective-permute-start(bf16[128,1024]{1,0:T(8,128)(2,1)S(1)} %slice.28), channel_id=1, source_target_pairs={{0,1},{1,0},{2,3},{3,2},{4,5},{5,4},{6,7},{7,6},{8,9},{9,8},{10,11... | collective-permute-start | bytes 786440 | tf_op jit(solution)/shard_map/ppermute | solution.py:370
  25.6 9.1 %collective-permute-start.6 = (bf16[128,1024]{1,0:T(8,128)(2,1)S(1)}, bf16[128,1024]{1,0:T(8,128)(2,1)S(1)}, u32[]{:S(2)}, u32[]{:S(2)}) collective-permute-start(bf16[128,1024]{1,0:T(8,128)(2,1)S(1)} %collective-permute-done.5.refs_5_), channel_id=1, source_target_pairs={{0,2},{2,4},{3,1},{4,6},{5,3},{7,5},{8,10},{10,12},{11,9},{12,14},... | collective-permute-start | bytes 786440 | tf_op jit(solution)/shard_map/ppermute | solution.py:370
  29.3 0.8 copy-start.3
  29.4 2.5 %copy-start.1 = (bf16[1024,32]{0,1:T(8,128)(2,1)S(1)}, bf16[1024,32]{0,1:T(8,128)(2,1)}, u32[]{:S(2)}) copy-start(bf16[1024,32]{0,1:T(8,128)(2,1)} %param.7) | copy-start | bytes 196612
  29.4 11.1 %collective-permute-start.3 = (bf16[128,1024]{1,0:T(8,128)(2,1)S(1)}, bf16[128,1024]{1,0:T(8,128)(2,1)S(1)}, u32[]{:S(2)}, u32[]{:S(2)}) collective-permute-start(bf16[128,1024]{1,0:T(8,128)(2,1)S(1)} %slice.29), channel_id=1, source_target_pairs={{0,1},{1,0},{2,3},{3,2},{4,5},{5,4},{6,7},{7,6},{8,9},{9,8},{10,11... | collective-permute-start | bytes 786440 | tf_op jit(solution)/shard_map/ppermute | solution.py:370
  29.4 11.0 %collective-permute-start.4 = (bf16[128,1024]{1,0:T(8,128)(2,1)S(1)}, bf16[128,1024]{1,0:T(8,128)(2,1)S(1)}, u32[]{:S(2)}, u32[]{:S(2)}) collective-permute-start(bf16[128,1024]{1,0:T(8,128)(2,1)S(1)} %slice.29), channel_id=1, source_target_pairs={{0,8},{1,2},{2,1},{3,4},{4,3},{5,6},{6,5},{7,15},{8,0},{9,10},{10,... | collective-permute-start | bytes 786440 | tf_op jit(solution)/shard_map/ppermute | solution.py:370
  30.1 0.7 copy-start.2
  41.6 1.2 %collective-permute-start.7 = (f32[1,1024]{1,0:T(1,128)S(1)}, f32[1,1024]{1,0:T(1,128)S(1)}, u32[]{:S(2)}, u32[]{:S(2)}) collective-permute-start(f32[1,1024]{1,0:T(1,128)S(1)} %get-tuple-element.45), channel_id=1, source_target_pairs={{0,8},{1,9},{2,10},{3,11},{4,12},{5,13},{6,14},{7,15},{8,0},{9,1},... | collective-permute-start | bytes 12296 | tf_op jit(solution)/shard_map/ppermute | solution.py:370
  42.9 3.7 %collective-permute-start.8 = (f32[1,1024]{1,0:T(1,128)S(1)}, f32[1,1024]{1,0:T(1,128)S(1)}, u32[]{:S(2)}, u32[]{:S(2)}) collective-permute-start(f32[1,1024]{1,0:T(1,128)S(1)} %maximum_add_fusion.degree), channel_id=1, source_target_pairs={{0,16},{1,17},{2,18},{3,19},{4,20},{5,21},{6,22},{7,23},{8,24},{9,... | collective-permute-start | bytes 12296 | tf_op jit(solution)/shard_map/ppermute | solution.py:370
  47.6 5.2 %collective-permute-start.10 = (f32[32,256]{1,0:T(8,128)S(1)}, f32[32,256]{1,0:T(8,128)S(1)}, u32[]{:S(2)}, u32[]{:S(2)}) collective-permute-start(f32[32,256]{1,0:T(8,128)S(1)} %get-tuple-element.61), channel_id=1, source_target_pairs={{0,8},{1,2},{2,1},{3,4},{4,3},{5,6},{6,5},{7,15},{8,0},{9,10},{10,... | collective-permute-start | bytes 98312 | tf_op jit(solution)/shard_map/ppermute | solution.py:370
  47.6 7.1 %collective-permute-start.9 = (f32[32,256]{1,0:T(8,128)S(1)}, f32[32,256]{1,0:T(8,128)S(1)}, u32[]{:S(2)}, u32[]{:S(2)}) collective-permute-start(f32[32,256]{1,0:T(8,128)S(1)} %get-tuple-element.60), channel_id=1, source_target_pairs={{0,1},{1,0},{2,3},{3,2},{4,5},{5,4},{6,7},{7,6},{8,9},{9,8},{10,11... | collective-permute-start | bytes 98312 | tf_op jit(solution)/shard_map/ppermute | solution.py:370
  54.7 4.0 %collective-permute-start.11 = (f32[32,256]{1,0:T(8,128)S(1)}, f32[32,256]{1,0:T(8,128)S(1)}, u32[]{:S(2)}, u32[]{:S(2)}) collective-permute-start(f32[32,256]{1,0:T(8,128)S(1)} %get-tuple-element.68.refs_0_), channel_id=1, source_target_pairs={{0,1},{1,0},{2,3},{3,2},{4,5},{5,4},{6,7},{7,6},{8,9},{9,8},{10,11... | collective-permute-start | bytes 98312 | tf_op jit(solution)/shard_map/ppermute | solution.py:370
  56.8 1.9 %collective-permute-start.12 = (f32[32,256]{1,0:T(8,128)S(1)}, f32[32,256]{1,0:T(8,128)S(1)}, u32[]{:S(2)}, u32[]{:S(2)}) collective-permute-start(f32[32,256]{1,0:T(8,128)S(1)} %get-tuple-element.68.refs_0_), channel_id=1, source_target_pairs={{0,8},{1,2},{2,1},{3,4},{4,3},{5,6},{6,5},{7,15},{8,0},{9,10},{10,... | collective-permute-start | bytes 98312 | tf_op jit(solution)/shard_map/ppermute | solution.py:370
  59.3 1.3 %collective-permute-start.13 = (f32[32,512]{1,0:T(8,128)S(1)}, f32[32,512]{1,0:T(8,128)S(1)}, u32[]{:S(2)}, u32[]{:S(2)}) collective-permute-start(f32[32,512]{1,0:T(8,128)S(1)} %get-tuple-element.63), channel_id=1, source_target_pairs={{0,8},{1,9},{2,10},{3,11},{4,12},{5,13},{6,14},{7,15},{8,0},{9,1},... | collective-permute-start | bytes 196616 | tf_op jit(solution)/shard_map/ppermute | solution.py:370
  60.7 4.0 %collective-permute-start.14 = (f32[32,256]{1,0:T(8,128)S(1)}, f32[32,256]{1,0:T(8,128)S(1)}, u32[]{:S(2)}, u32[]{:S(2)}) collective-permute-start(f32[32,256]{1,0:T(8,128)S(1)} %get-tuple-element.70), channel_id=1, source_target_pairs={{0,16},{1,17},{2,18},{3,19},{4,20},{5,21},{6,22},{7,23},{8,24},{9,... | collective-permute-start | bytes 98312 | tf_op jit(solution)/shard_map/ppermute | solution.py:370
  65.1 1.2 %collective-permute-start.15 = (f32[24,128]{1,0:T(8,128)S(1)}, f32[24,128]{1,0:T(8,128)S(1)}, u32[]{:S(2)}, u32[]{:S(2)}) collective-permute-start(f32[24,128]{1,0:T(8,128)S(1)} %get-tuple-element.64.mine), channel_id=1, source_target_pairs={{0,8},{1,9},{2,10},{3,11},{4,12},{5,13},{6,14},{7,15},{8,0},{9,1},... | collective-permute-start | bytes 36872 | tf_op jit(solution)/shard_map/ppermute | solution.py:370

commit v8 on v7

--- a/solution.py
+++ b/solution.py
@@ -310,13 +310,20 @@
         axis=0,
     )
     rows = 3 * width
+    row = lax.broadcasted_iota(jnp.int32, gram.shape, 0)
+    col = lax.broadcasted_iota(jnp.int32, gram.shape, 1)
+    diagonal = jnp.where(row == col, gram, 0.0)
+    across = jnp.sum(diagonal, axis=0, keepdims=True)
+    root = lax.rsqrt(jnp.where(col[:1, :] < rows, across, 1.0))
+    gram = gram * lax.rsqrt(jnp.sum(diagonal, axis=1, keepdims=True)) * root
     groups = [gram[8 * i:8 * i + 8, :] for i in range(rows // 8)]
     whole = jnp.concatenate(eliminate(groups), axis=0)[:, :rows]
     row = lax.broadcasted_iota(jnp.int32, (rows, rows), 0)
     col = lax.broadcasted_iota(jnp.int32, (rows, rows), 1)
-    upper = jnp.where(col >= row, whole, 0.0)
+    root = root[:, :rows]
+    upper = jnp.where(col >= row, whole, 0.0) / root
     pivot = jnp.sum(jnp.where(col == row, whole, 0.0), axis=1, keepdims=True)
-    inverse = jnp.where(col < row, whole, jnp.where(col == row, 1.0 / pivot, 0.0))
+    inverse = jnp.where(col < row, whole, jnp.where(col == row, 1.0 / pivot, 0.0)) * root
     basis[...] = nn(inverse, jnp.concatenate([v0[...], v1[...], v2[...]], axis=0))
 
     def block(value, i, j):

time: 86.5 us -> 86.5 us (level)
  no operation moved by 1% of the time
where the time goes in v8:
time: 86.5 us; the launch traced here: 86.2 us
  waiting for transfers between devices  36.3 us (42%)
  starting transfers between devices  19.3 us (22%)
  blocking collectives  15.7 us (18%)
  Pallas kernels  11.8 us (14%)
  local copies, waits for them, and re-layouts  2.24 us (3%)
    ppermute x16, waiting for transfers between devices, move(): return lax.ppermute(value, ALL, route[name])  36.3 us
    ppermute x16, starting transfers between devices, move(): return lax.ppermute(value, ALL, route[name])  19.3 us
    all_to_all x1, blocking collectives, steps(): parts = lax.all_to_all(copies, ('row', 'inner'), 0, 0)  15.7 us
    pallas_call x11, Pallas kernels, call(): pl.pallas_call(kernel, out_shape=[result(shape, kind) for shape, kind in...  11.8 us
  transfers between devices with their start and end apart: 16, of which 11 were waited for; matrix products, arithmetic and copies ran while one was open for 1% of the time, Pallas kernels for 5%

profile of v8, /device:TPU:0, one launch (start us, length us, event | category | flops | bytes accessed | tf_op | source)
XLA Modules:
  0.0 86.2 jit_solution(962660514205194727)
XLA Ops:
  0.6 3.1 %collective-permute-start.1 = (bf16[256,1024]{1,0:T(8,128)(2,1)}, bf16[256,1024]{1,0:T(8,128)(2,1)S(1)}, u32[]{:S(2)}, u32[]{:S(2)}) collective-permute-start(bf16[256,1024]{1,0:T(8,128)(2,1)} %refs_4_.1), channel_id=1, source_target_pairs={{0,16},{1,17},{2,18},{3,19},{4,20},{5,21},{6,22},{7,23},{8,24},{9,... | collective-permute-start | bytes 1572872 | tf_op jit(solution)/shard_map/ppermute | solution.py:377
  3.7 12.1 %collective-permute-done.1.r0 = bf16[256,1024]{1,0:T(8,128)(2,1)S(1)} collective-permute-done((bf16[256,1024]{1,0:T(8,128)(2,1)}, bf16[256,1024]{1,0:T(8,128)(2,1)S(1)}, u32[]{:S(2)}, u32[]{:S(2)}) %collective-permute-start.1) | collective-permute-done | bytes 524320 | tf_op jit(solution)/shard_map/ppermute | solution.py:377
  15.8 1.0 %slice.28 = bf16[128,1024]{1,0:T(8,128)(2,1)S(1)} slice(bf16[256,1024]{1,0:T(8,128)(2,1)} %refs_4_.1), slice={[0:128], [0:1024]} | slice | bytes 524288 | tf_op jit(solution)/shard_map/slice | solution.py:381
  16.8 1.8 %collective-permute-start.5 = (bf16[128,1024]{1,0:T(8,128)(2,1)S(1)}, bf16[128,1024]{1,0:T(8,128)(2,1)S(1)}, u32[]{:S(2)}, u32[]{:S(2)}) collective-permute-start(bf16[128,1024]{1,0:T(8,128)(2,1)S(1)} %slice.28), channel_id=1, source_target_pairs={{0,1},{1,0},{2,3},{3,2},{4,5},{5,4},{6,7},{7,6},{8,9},{9,8},{10,11... | collective-permute-start | bytes 786440 | tf_op jit(solution)/shard_map/ppermute | solution.py:377
  18.6 7.0 %collective-permute-done.5.refs_5_ = bf16[128,1024]{1,0:T(8,128)(2,1)S(1)} collective-permute-done((bf16[128,1024]{1,0:T(8,128)(2,1)S(1)}, bf16[128,1024]{1,0:T(8,128)(2,1)S(1)}, u32[]{:S(2)}, u32[]{:S(2)}) %collective-permute-start.5) | collective-permute-done | bytes 262176 | tf_op jit(solution)/shard_map/ppermute | solution.py:377
  25.6 3.7 %collective-permute-start.6 = (bf16[128,1024]{1,0:T(8,128)(2,1)S(1)}, bf16[128,1024]{1,0:T(8,128)(2,1)S(1)}, u32[]{:S(2)}, u32[]{:S(2)}) collective-permute-start(bf16[128,1024]{1,0:T(8,128)(2,1)S(1)} %collective-permute-done.5.refs_5_), channel_id=1, source_target_pairs={{0,2},{2,4},{3,1},{4,6},{5,3},{7,5},{8,10},{10,12},{11,9},{12,14},... | collective-permute-start | bytes 786440 | tf_op jit(solution)/shard_map/ppermute | solution.py:377
  29.5 0.5 copy-done.3
  30.1 0.7 copy-done.2
  30.8 1.0 %shard_map.59 = (f32[3,8,256]{2,1,0:T(8,128)S(1)}, f32[3,8,1024]{2,1,0:T(8,128)S(1)}) custom-call(s32[2]{0:T(128)S(1)} %compare_select_fusion.place, s32[32,256]{1,0:T(8,128)S(1)} %reshape.7.bins, s32[2,256]{1,0:T(2,128)S(1)} %bitcast.7), custom_call_target="tpu_custom_call" | custom-call | tf_op jit(solution)/shard_map/pallas_call | solution.py:38
  31.8 0.5 shard_map.60
  32.3 0.5 shard_map.61
  32.8 1.6 %shard_map.62 = (bf16[256,1024]{1,0:T(8,128)(2,1)S(1)}, bf16[256,1024]{1,0:T(8,128)(2,1)S(1)}, bf16[128,1024]{1,0:T(8,128)(2,1)S(1)}, bf16[128,1024]{1,0:T(8,128)(2,1)S(1)}, f32[1,1024]{1,0:T(1,128)S(1)}) custom-call(f32[3,8,256]{2,1,0:T(8,128)S(1)} %get-tuple-element.35.hots, f32[3,8,1024]{2,1,0:T(8,128)S(1)} %get-tuple-element.36.all_links, ...), custom_call_target="tpu_custom_call" | custom-call | tf_op jit(solution)/shard_map/pallas_call | solution.py:38
  34.4 0.2 collective-permute-done.6.refs_4_
  34.6 0.7 shard_map.63
  35.3 5.1 %collective-permute-done.3.refs_4_ = bf16[128,1024]{1,0:T(8,128)(2,1)S(1)} collective-permute-done((bf16[128,1024]{1,0:T(8,128)(2,1)S(1)}, bf16[128,1024]{1,0:T(8,128)(2,1)S(1)}, u32[]{:S(2)}, u32[]{:S(2)}) %collective-permute-start.3) | collective-permute-done | bytes 262176 | tf_op jit(solution)/shard_map/ppermute | solution.py:377
  40.4 1.2 %shard_map.64 = (bf16[128,1024]{1,0:T(8,128)(2,1)S(1)}, bf16[128,1024]{1,0:T(8,128)(2,1)S(1)}, bf16[128,1024]{1,0:T(8,128)(2,1)S(1)}, bf16[128,1024]{1,0:T(8,128)(2,1)S(1)}, f32[1,1024]{1,0:T(1,128)S(1)}) custom-call(f32[3,8,256]{2,1,0:T(8,128)S(1)} %get-tuple-element.35.hots, f32[3,8,1024]{2,1,0:T(8,128)S(1)} %get-tuple-element.36.all_links, ...), custom_call_target="tpu_custom_call" | custom-call | tf_op jit(solution)/shard_map/pallas_call | solution.py:38
  41.7 1.2 %collective-permute-done.7 = f32[1,1024]{1,0:T(1,128)S(1)} collective-permute-done((f32[1,1024]{1,0:T(1,128)S(1)}, f32[1,1024]{1,0:T(1,128)S(1)}, u32[]{:S(2)}, u32[]{:S(2)}) %collective-permute-start.7) | collective-permute-done | bytes 4128 | tf_op jit(solution)/shard_map/ppermute | solution.py:377
  42.9 1.6 %collective-permute-start.8 = (f32[1,1024]{1,0:T(1,128)S(1)}, f32[1,1024]{1,0:T(1,128)S(1)}, u32[]{:S(2)}, u32[]{:S(2)}) collective-permute-start(f32[1,1024]{1,0:T(1,128)S(1)} %maximum_add_fusion.degree), channel_id=1, source_target_pairs={{0,16},{1,17},{2,18},{3,19},{4,20},{5,21},{6,22},{7,23},{8,24},{9,... | collective-permute-start | bytes 12296 | tf_op jit(solution)/shard_map/ppermute | solution.py:377
  44.4 2.1 %collective-permute-done.8.got = f32[1,1024]{1,0:T(1,128)S(1)} collective-permute-done((f32[1,1024]{1,0:T(1,128)S(1)}, f32[1,1024]{1,0:T(1,128)S(1)}, u32[]{:S(2)}, u32[]{:S(2)}) %collective-permute-start.8) | collective-permute-done | bytes 4128 | tf_op jit(solution)/shard_map/ppermute | solution.py:377
  46.5 1.1 %shard_map.65 = (f32[1,256]{1,0:T(1,128)S(1)}, f32[32,256]{1,0:T(8,128)S(1)}, f32[32,256]{1,0:T(8,128)S(1)}, f32[32,256]{1,0:T(8,128)S(1)}) custom-call(f32[1,1024]{1,0:T(1,128)S(1)} %maximum_add_fusion.degree, f32[1,1024]{1,0:T(1,128)S(1)} %collective-permute-done.8.got, f32[32,512]{1,0:T(8,128)S(1)} %get-tuple-element.46.start_a, ...), custom_call_target="tpu_custom_call" | custom-call | tf_op jit(solution)/shard_map/pallas_call | solution.py:38
  47.6 5.2 %collective-permute-start.9 = (f32[32,256]{1,0:T(8,128)S(1)}, f32[32,256]{1,0:T(8,128)S(1)}, u32[]{:S(2)}, u32[]{:S(2)}) collective-permute-start(f32[32,256]{1,0:T(8,128)S(1)} %get-tuple-element.60), channel_id=1, source_target_pairs={{0,1},{1,0},{2,3},{3,2},{4,5},{5,4},{6,7},{7,6},{8,9},{9,8},{10,11... | collective-permute-start | bytes 98312 | tf_op jit(solution)/shard_map/ppermute | solution.py:377
  52.8 1.9 %collective-permute-done.9 = f32[32,256]{1,0:T(8,128)S(1)} collective-permute-done((f32[32,256]{1,0:T(8,128)S(1)}, f32[32,256]{1,0:T(8,128)S(1)}, u32[]{:S(2)}, u32[]{:S(2)}) %collective-permute-start.9) | collective-permute-done | bytes 32800 | tf_op jit(solution)/shard_map/ppermute | solution.py:377
  54.7 2.1 %collective-permute-start.11 = (f32[32,256]{1,0:T(8,128)S(1)}, f32[32,256]{1,0:T(8,128)S(1)}, u32[]{:S(2)}, u32[]{:S(2)}) collective-permute-start(f32[32,256]{1,0:T(8,128)S(1)} %get-tuple-element.68.refs_0_), channel_id=1, source_target_pairs={{0,1},{1,0},{2,3},{3,2},{4,5},{5,4},{6,7},{7,6},{8,9},{9,8},{10,11... | collective-permute-start | bytes 98312 | tf_op jit(solution)/shard_map/ppermute | solution.py:377
  56.8 1.9 %collective-permute-done.11.refs_1_ = f32[32,256]{1,0:T(8,128)S(1)} collective-permute-done((f32[32,256]{1,0:T(8,128)S(1)}, f32[32,256]{1,0:T(8,128)S(1)}, u32[]{:S(2)}, u32[]{:S(2)}) %collective-permute-start.11) | collective-permute-done | bytes 32800 | tf_op jit(solution)/shard_map/ppermute | solution.py:377
  58.7 0.6 shard_map.66
  59.4 1.2 %collective-permute-done.13 = f32[32,512]{1,0:T(8,128)S(1)} collective-permute-done((f32[32,512]{1,0:T(8,128)S(1)}, f32[32,512]{1,0:T(8,128)S(1)}, u32[]{:S(2)}, u32[]{:S(2)}) %collective-permute-start.13) | collective-permute-done | bytes 65568 | tf_op jit(solution)/shard_map/ppermute | solution.py:377
  60.7 1.6 %collective-permute-start.14 = (f32[32,256]{1,0:T(8,128)S(1)}, f32[32,256]{1,0:T(8,128)S(1)}, u32[]{:S(2)}, u32[]{:S(2)}) collective-permute-start(f32[32,256]{1,0:T(8,128)S(1)} %get-tuple-element.70), channel_id=1, source_target_pairs={{0,16},{1,17},{2,18},{3,19},{4,20},{5,21},{6,22},{7,23},{8,24},{9,... | collective-permute-start | bytes 98312 | tf_op jit(solution)/shard_map/ppermute | solution.py:377
  62.3 2.4 %collective-permute-done.14.got = f32[32,256]{1,0:T(8,128)S(1)} collective-permute-done((f32[32,256]{1,0:T(8,128)S(1)}, f32[32,256]{1,0:T(8,128)S(1)}, u32[]{:S(2)}, u32[]{:S(2)}) %collective-permute-start.14) | collective-permute-done | bytes 32800 | tf_op jit(solution)/shard_map/ppermute | solution.py:377
  64.7 0.4 shard_map.67
  65.1 1.2 %collective-permute-done.15.got = f32[24,128]{1,0:T(8,128)S(1)} collective-permute-done((f32[24,128]{1,0:T(8,128)S(1)}, f32[24,128]{1,0:T(8,128)S(1)}, u32[]{:S(2)}, u32[]{:S(2)}) %collective-permute-start.15) | collective-permute-done | bytes 12320 | tf_op jit(solution)/shard_map/ppermute | solution.py:377
  66.3 15.7 %all_to_all.5.parts = f32[16,24,128]{2,1,0:T(8,128)S(1)} all-to-all(f32[16,24,128]{2,1,0:T(8,128)S(1)} %shard_map.68), channel_id=1, replica_groups=mesh['row'=2,'core'=2,'inner'=8] {'row','inner'}, dimensions={0} | all-to-all | bytes 393216 | tf_op jit(solution)/shard_map/all_to_all | solution.py:458
  82.0 4.2 %shard_map.69 = (f32[96,256]{1,0:T(8,128)}, f32[4,32,32]{2,1,0:T(8,128)}) custom-call(f32[16,24,128]{2,1,0:T(8,128)S(1)} %all_to_all.5.parts, f32[32,256]{1,0:T(8,128)S(1)} %slice.36.start.v0, f32[32,256]{1,0:T(8,128)S(1)} %get-tuple-element.69.image.v1, f32[32,256]{1,0:T(8,128)S(1)} %get-tuple-element.65.v2), custom_call_target="tpu_custom_call" | custom-call | tf_op jit(solution)/shard_map/pallas_call | solution.py:38
  (30 shorter events, 0.4 us)
Async XLA Ops:
  0.6 28.7 %copy-start = (bf16[256,1024]{1,0:T(8,128)(2,1)S(1)}, bf16[256,1024]{1,0:T(8,128)(2,1)}, u32[]{:S(2)}) copy-start(bf16[256,1024]{1,0:T(8,128)(2,1)} %refs_4_.1) | copy-start | bytes 1572868
  0.6 15.2 %collective-permute-start.1 = (bf16[256,1024]{1,0:T(8,128)(2,1)}, bf16[256,1024]{1,0:T(8,128)(2,1)S(1)}, u32[]{:S(2)}, u32[]{:S(2)}) collective-permute-start(bf16[256,1024]{1,0:T(8,128)(2,1)} %refs_4_.1), channel_id=1, source_target_pairs={{0,16},{1,17},{2,18},{3,19},{4,20},{5,21},{6,22},{7,23},{8,24},{9,... | collective-permute-start | bytes 1572872 | tf_op jit(solution)/shard_map/ppermute | solution.py:377
  3.7 28.1 %collective-permute-start = (bf16[256,1024]{1,0:T(8,128)(2,1)}, bf16[256,1024]{1,0:T(8,128)(2,1)S(1)}, u32[]{:S(2)}, u32[]{:S(2)}) collective-permute-start(bf16[256,1024]{1,0:T(8,128)(2,1)} %refs_4_.1), channel_id=1, source_target_pairs={{0,8},{1,9},{2,10},{3,11},{4,12},{5,13},{6,14},{7,15},{8,0},{9,1},... | collective-permute-start | bytes 1572872 | tf_op jit(solution)/shard_map/ppermute | solution.py:377
  15.8 16.5 %collective-permute-start.2 = (bf16[256,1024]{1,0:T(8,128)(2,1)S(1)}, bf16[256,1024]{1,0:T(8,128)(2,1)S(1)}, u32[]{:S(2)}, u32[]{:S(2)}) collective-permute-start(bf16[256,1024]{1,0:T(8,128)(2,1)S(1)} %collective-permute-done.1.r0), channel_id=1, source_target_pairs={{0,8},{1,9},{2,10},{3,11},{4,12},{5,13},{6,14},{7,15},{8,0},{9,1},... | collective-permute-start | bytes 1572872 | tf_op jit(solution)/shard_map/ppermute | solution.py:377
  16.8 8.8 %collective-permute-start.5 = (bf16[128,1024]{1,0:T(8,128)(2,1)S(1)}, bf16[128,1024]{1,0:T(8,128)(2,1)S(1)}, u32[]{:S(2)}, u32[]{:S(2)}) collective-permute-start(bf16[128,1024]{1,0:T(8,128)(2,1)S(1)} %slice.28), channel_id=1, source_target_pairs={{0,1},{1,0},{2,3},{3,2},{4,5},{5,4},{6,7},{7,6},{8,9},{9,8},{10,11... | collective-permute-start | bytes 786440 | tf_op jit(solution)/shard_map/ppermute | solution.py:377
  25.6 9.1 %collective-permute-start.6 = (bf16[128,1024]{1,0:T(8,128)(2,1)S(1)}, bf16[128,1024]{1,0:T(8,128)(2,1)S(1)}, u32[]{:S(2)}, u32[]{:S(2)}) collective-permute-start(bf16[128,1024]{1,0:T(8,128)(2,1)S(1)} %collective-permute-done.5.refs_5_), channel_id=1, source_target_pairs={{0,2},{2,4},{3,1},{4,6},{5,3},{7,5},{8,10},{10,12},{11,9},{12,14},... | collective-permute-start | bytes 786440 | tf_op jit(solution)/shard_map/ppermute | solution.py:377
  29.3 0.8 copy-start.3
  29.4 2.5 %copy-start.1 = (bf16[1024,32]{0,1:T(8,128)(2,1)S(1)}, bf16[1024,32]{0,1:T(8,128)(2,1)}, u32[]{:S(2)}) copy-start(bf16[1024,32]{0,1:T(8,128)(2,1)} %param.7) | copy-start | bytes 196612
  29.4 11.1 %collective-permute-start.3 = (bf16[128,1024]{1,0:T(8,128)(2,1)S(1)}, bf16[128,1024]{1,0:T(8,128)(2,1)S(1)}, u32[]{:S(2)}, u32[]{:S(2)}) collective-permute-start(bf16[128,1024]{1,0:T(8,128)(2,1)S(1)} %slice.29), channel_id=1, source_target_pairs={{0,1},{1,0},{2,3},{3,2},{4,5},{5,4},{6,7},{7,6},{8,9},{9,8},{10,11... | collective-permute-start | bytes 786440 | tf_op jit(solution)/shard_map/ppermute | solution.py:377
  29.4 11.0 %collective-permute-start.4 = (bf16[128,1024]{1,0:T(8,128)(2,1)S(1)}, bf16[128,1024]{1,0:T(8,128)(2,1)S(1)}, u32[]{:S(2)}, u32[]{:S(2)}) collective-permute-start(bf16[128,1024]{1,0:T(8,128)(2,1)S(1)} %slice.29), channel_id=1, source_target_pairs={{0,8},{1,2},{2,1},{3,4},{4,3},{5,6},{6,5},{7,15},{8,0},{9,10},{10,... | collective-permute-start | bytes 786440 | tf_op jit(solution)/shard_map/ppermute | solution.py:377
  30.1 0.7 copy-start.2
  41.6 1.2 %collective-permute-start.7 = (f32[1,1024]{1,0:T(1,128)S(1)}, f32[1,1024]{1,0:T(1,128)S(1)}, u32[]{:S(2)}, u32[]{:S(2)}) collective-permute-start(f32[1,1024]{1,0:T(1,128)S(1)} %get-tuple-element.45), channel_id=1, source_target_pairs={{0,8},{1,9},{2,10},{3,11},{4,12},{5,13},{6,14},{7,15},{8,0},{9,1},... | collective-permute-start | bytes 12296 | tf_op jit(solution)/shard_map/ppermute | solution.py:377
  42.9 3.7 %collective-permute-start.8 = (f32[1,1024]{1,0:T(1,128)S(1)}, f32[1,1024]{1,0:T(1,128)S(1)}, u32[]{:S(2)}, u32[]{:S(2)}) collective-permute-start(f32[1,1024]{1,0:T(1,128)S(1)} %maximum_add_fusion.degree), channel_id=1, source_target_pairs={{0,16},{1,17},{2,18},{3,19},{4,20},{5,21},{6,22},{7,23},{8,24},{9,... | collective-permute-start | bytes 12296 | tf_op jit(solution)/shard_map/ppermute | solution.py:377
  47.6 5.2 %collective-permute-start.10 = (f32[32,256]{1,0:T(8,128)S(1)}, f32[32,256]{1,0:T(8,128)S(1)}, u32[]{:S(2)}, u32[]{:S(2)}) collective-permute-start(f32[32,256]{1,0:T(8,128)S(1)} %get-tuple-element.61), channel_id=1, source_target_pairs={{0,8},{1,2},{2,1},{3,4},{4,3},{5,6},{6,5},{7,15},{8,0},{9,10},{10,... | collective-permute-start | bytes 98312 | tf_op jit(solution)/shard_map/ppermute | solution.py:377
  47.6 7.1 %collective-permute-start.9 = (f32[32,256]{1,0:T(8,128)S(1)}, f32[32,256]{1,0:T(8,128)S(1)}, u32[]{:S(2)}, u32[]{:S(2)}) collective-permute-start(f32[32,256]{1,0:T(8,128)S(1)} %get-tuple-element.60), channel_id=1, source_target_pairs={{0,1},{1,0},{2,3},{3,2},{4,5},{5,4},{6,7},{7,6},{8,9},{9,8},{10,11... | collective-permute-start | bytes 98312 | tf_op jit(solution)/shard_map/ppermute | solution.py:377
  54.7 4.0 %collective-permute-start.11 = (f32[32,256]{1,0:T(8,128)S(1)}, f32[32,256]{1,0:T(8,128)S(1)}, u32[]{:S(2)}, u32[]{:S(2)}) collective-permute-start(f32[32,256]{1,0:T(8,128)S(1)} %get-tuple-element.68.refs_0_), channel_id=1, source_target_pairs={{0,1},{1,0},{2,3},{3,2},{4,5},{5,4},{6,7},{7,6},{8,9},{9,8},{10,11... | collective-permute-start | bytes 98312 | tf_op jit(solution)/shard_map/ppermute | solution.py:377
  56.8 1.9 %collective-permute-start.12 = (f32[32,256]{1,0:T(8,128)S(1)}, f32[32,256]{1,0:T(8,128)S(1)}, u32[]{:S(2)}, u32[]{:S(2)}) collective-permute-start(f32[32,256]{1,0:T(8,128)S(1)} %get-tuple-element.68.refs_0_), channel_id=1, source_target_pairs={{0,8},{1,2},{2,1},{3,4},{4,3},{5,6},{6,5},{7,15},{8,0},{9,10},{10,... | collective-permute-start | bytes 98312 | tf_op jit(solution)/shard_map/ppermute | solution.py:377
  59.3 1.3 %collective-permute-start.13 = (f32[32,512]{1,0:T(8,128)S(1)}, f32[32,512]{1,0:T(8,128)S(1)}, u32[]{:S(2)}, u32[]{:S(2)}) collective-permute-start(f32[32,512]{1,0:T(8,128)S(1)} %get-tuple-element.63), channel_id=1, source_target_pairs={{0,8},{1,9},{2,10},{3,11},{4,12},{5,13},{6,14},{7,15},{8,0},{9,1},... | collective-permute-start | bytes 196616 | tf_op jit(solution)/shard_map/ppermute | solution.py:377
  60.7 4.0 %collective-permute-start.14 = (f32[32,256]{1,0:T(8,128)S(1)}, f32[32,256]{1,0:T(8,128)S(1)}, u32[]{:S(2)}, u32[]{:S(2)}) collective-permute-start(f32[32,256]{1,0:T(8,128)S(1)} %get-tuple-element.70), channel_id=1, source_target_pairs={{0,16},{1,17},{2,18},{3,19},{4,20},{5,21},{6,22},{7,23},{8,24},{9,... | collective-permute-start | bytes 98312 | tf_op jit(solution)/shard_map/ppermute | solution.py:377
  65.1 1.2 %collective-permute-start.15 = (f32[24,128]{1,0:T(8,128)S(1)}, f32[24,128]{1,0:T(8,128)S(1)}, u32[]{:S(2)}, u32[]{:S(2)}) collective-permute-start(f32[24,128]{1,0:T(8,128)S(1)} %get-tuple-element.64.mine), channel_id=1, source_target_pairs={{0,8},{1,9},{2,10},{3,11},{4,12},{5,13},{6,14},{7,15},{8,0},{9,1},... | collective-permute-start | bytes 36872 | tf_op jit(solution)/shard_map/ppermute | solution.py:377

commit v9 on v8

--- a/solution.py
+++ b/solution.py
@@ -189,7 +189,7 @@
     for k, (kind, part) in enumerate(places):
         x = others[k][...]
         wide = x.astype(F32)
-        own = jnp.sum(wide * wide, axis=1, keepdims=True)
+        own = scale * jnp.sum(wide * wide, axis=1, keepdims=True)
         size = x.shape[0]
         hot = hots[kind, :, part:part + size].T
         high, low = outs[2 * k:2 * k + 2]
@@ -197,8 +197,8 @@
             turned, norms = groups[2 * i:2 * i + 2]
             at = slice(i * span, (i + 1) * span)
             mask = nn(hot, all_links[kind, :, at], None)
-            distance = own + norms[...] - 2.0 * nn(x, turned[...], None)
-            value = mask * jnp.exp(distance * scale)
+            power = own + scale * norms[...] - (2.0 * scale) * nn(x, turned[...], None)
+            value = mask * jnp.exp(power)
             top = value.astype(BF16)
             high[:, at] = top
             low[:, at] = (value - top.astype(F32)).astype(BF16)

time: 86.5 us -> 86.5 us (level)
  no operation moved by 1% of the time
where the time goes in v9:
time: 86.5 us; the launch traced here: 86.2 us
  waiting for transfers between devices  36.3 us (42%)
  starting transfers between devices  19.4 us (22%)
  blocking collectives  15.7 us (18%)
  Pallas kernels  11.8 us (14%)
  local copies, waits for them, and re-layouts  2.24 us (3%)
    ppermute x16, waiting for transfers between devices, move(): return lax.ppermute(value, ALL, route[name])  36.3 us
    ppermute x16, starting transfers between devices, move(): return lax.ppermute(value, ALL, route[name])  19.4 us
    all_to_all x1, blocking collectives, steps(): parts = lax.all_to_all(copies, ('row', 'inner'), 0, 0)  15.7 us
    pallas_call x11, Pallas kernels, call(): pl.pallas_call(kernel, out_shape=[result(shape, kind) for shape, kind in...  11.8 us
  transfers between devices with their start and end apart: 16, of which 11 were waited for; matrix products, arithmetic and copies ran while one was open for 1% of the time, Pallas kernels for 5%

profile of v9, /device:TPU:0, one launch (start us, length us, event | category | flops | bytes accessed | tf_op | source)
XLA Modules:
  0.0 86.2 jit_solution(13094164813618691915)
XLA Ops:
  0.6 3.1 %collective-permute-start.1 = (bf16[256,1024]{1,0:T(8,128)(2,1)}, bf16[256,1024]{1,0:T(8,128)(2,1)S(1)}, u32[]{:S(2)}, u32[]{:S(2)}) collective-permute-start(bf16[256,1024]{1,0:T(8,128)(2,1)} %refs_4_.1), channel_id=1, source_target_pairs={{0,16},{1,17},{2,18},{3,19},{4,20},{5,21},{6,22},{7,23},{8,24},{9,... | collective-permute-start | bytes 1572872 | tf_op jit(solution)/shard_map/ppermute | solution.py:377
  3.7 12.1 %collective-permute-done.1.r0 = bf16[256,1024]{1,0:T(8,128)(2,1)S(1)} collective-permute-done((bf16[256,1024]{1,0:T(8,128)(2,1)}, bf16[256,1024]{1,0:T(8,128)(2,1)S(1)}, u32[]{:S(2)}, u32[]{:S(2)}) %collective-permute-start.1) | collective-permute-done | bytes 524320 | tf_op jit(solution)/shard_map/ppermute | solution.py:377
  15.8 1.0 %slice.28 = bf16[128,1024]{1,0:T(8,128)(2,1)S(1)} slice(bf16[256,1024]{1,0:T(8,128)(2,1)} %refs_4_.1), slice={[0:128], [0:1024]} | slice | bytes 524288 | tf_op jit(solution)/shard_map/slice | solution.py:381
  16.8 1.8 %collective-permute-start.5 = (bf16[128,1024]{1,0:T(8,128)(2,1)S(1)}, bf16[128,1024]{1,0:T(8,128)(2,1)S(1)}, u32[]{:S(2)}, u32[]{:S(2)}) collective-permute-start(bf16[128,1024]{1,0:T(8,128)(2,1)S(1)} %slice.28), channel_id=1, source_target_pairs={{0,1},{1,0},{2,3},{3,2},{4,5},{5,4},{6,7},{7,6},{8,9},{9,8},{10,11... | collective-permute-start | bytes 786440 | tf_op jit(solution)/shard_map/ppermute | solution.py:377
  18.6 7.0 %collective-permute-done.5.refs_5_ = bf16[128,1024]{1,0:T(8,128)(2,1)S(1)} collective-permute-done((bf16[128,1024]{1,0:T(8,128)(2,1)S(1)}, bf16[128,1024]{1,0:T(8,128)(2,1)S(1)}, u32[]{:S(2)}, u32[]{:S(2)}) %collective-permute-start.5) | collective-permute-done | bytes 262176 | tf_op jit(solution)/shard_map/ppermute | solution.py:377
  25.6 3.7 %collective-permute-start.6 = (bf16[128,1024]{1,0:T(8,128)(2,1)S(1)}, bf16[128,1024]{1,0:T(8,128)(2,1)S(1)}, u32[]{:S(2)}, u32[]{:S(2)}) collective-permute-start(bf16[128,1024]{1,0:T(8,128)(2,1)S(1)} %collective-permute-done.5.refs_5_), channel_id=1, source_target_pairs={{0,2},{2,4},{3,1},{4,6},{5,3},{7,5},{8,10},{10,12},{11,9},{12,14},... | collective-permute-start | bytes 786440 | tf_op jit(solution)/shard_map/ppermute | solution.py:377
  29.5 0.5 copy-done.3
  30.1 0.7 copy-done.2
  30.8 1.0 %shard_map.59 = (f32[3,8,256]{2,1,0:T(8,128)S(1)}, f32[3,8,1024]{2,1,0:T(8,128)S(1)}) custom-call(s32[2]{0:T(128)S(1)} %compare_select_fusion.place, s32[32,256]{1,0:T(8,128)S(1)} %reshape.7.bins, s32[2,256]{1,0:T(2,128)S(1)} %bitcast.7), custom_call_target="tpu_custom_call" | custom-call | tf_op jit(solution)/shard_map/pallas_call | solution.py:38
  31.8 0.5 shard_map.60
  32.3 0.5 shard_map.61
  32.8 1.6 %shard_map.62 = (bf16[256,1024]{1,0:T(8,128)(2,1)S(1)}, bf16[256,1024]{1,0:T(8,128)(2,1)S(1)}, bf16[128,1024]{1,0:T(8,128)(2,1)S(1)}, bf16[128,1024]{1,0:T(8,128)(2,1)S(1)}, f32[1,1024]{1,0:T(1,128)S(1)}) custom-call(f32[3,8,256]{2,1,0:T(8,128)S(1)} %get-tuple-element.35.hots, f32[3,8,1024]{2,1,0:T(8,128)S(1)} %get-tuple-element.36.all_links, ...), custom_call_target="tpu_custom_call" | custom-call | tf_op jit(solution)/shard_map/pallas_call | solution.py:38
  34.4 0.2 collective-permute-done.6.refs_4_
  34.6 0.7 shard_map.63
  35.3 5.1 %collective-permute-done.3.refs_4_ = bf16[128,1024]{1,0:T(8,128)(2,1)S(1)} collective-permute-done((bf16[128,1024]{1,0:T(8,128)(2,1)S(1)}, bf16[128,1024]{1,0:T(8,128)(2,1)S(1)}, u32[]{:S(2)}, u32[]{:S(2)}) %collective-permute-start.3) | collective-permute-done | bytes 262176 | tf_op jit(solution)/shard_map/ppermute | solution.py:377
  40.4 1.2 %shard_map.64 = (bf16[128,1024]{1,0:T(8,128)(2,1)S(1)}, bf16[128,1024]{1,0:T(8,128)(2,1)S(1)}, bf16[128,1024]{1,0:T(8,128)(2,1)S(1)}, bf16[128,1024]{1,0:T(8,128)(2,1)S(1)}, f32[1,1024]{1,0:T(1,128)S(1)}) custom-call(f32[3,8,256]{2,1,0:T(8,128)S(1)} %get-tuple-element.35.hots, f32[3,8,1024]{2,1,0:T(8,128)S(1)} %get-tuple-element.36.all_links, ...), custom_call_target="tpu_custom_call" | custom-call | tf_op jit(solution)/shard_map/pallas_call | solution.py:38
  41.7 1.2 %collective-permute-done.7 = f32[1,1024]{1,0:T(1,128)S(1)} collective-permute-done((f32[1,1024]{1,0:T(1,128)S(1)}, f32[1,1024]{1,0:T(1,128)S(1)}, u32[]{:S(2)}, u32[]{:S(2)}) %collective-permute-start.7) | collective-permute-done | bytes 4128 | tf_op jit(solution)/shard_map/ppermute | solution.py:377
  42.9 1.6 %collective-permute-start.8 = (f32[1,1024]{1,0:T(1,128)S(1)}, f32[1,1024]{1,0:T(1,128)S(1)}, u32[]{:S(2)}, u32[]{:S(2)}) collective-permute-start(f32[1,1024]{1,0:T(1,128)S(1)} %maximum_add_fusion.degree), channel_id=1, source_target_pairs={{0,16},{1,17},{2,18},{3,19},{4,20},{5,21},{6,22},{7,23},{8,24},{9,... | collective-permute-start | bytes 12296 | tf_op jit(solution)/shard_map/ppermute | solution.py:377
  44.5 2.1 %collective-permute-done.8.got = f32[1,1024]{1,0:T(1,128)S(1)} collective-permute-done((f32[1,1024]{1,0:T(1,128)S(1)}, f32[1,1024]{1,0:T(1,128)S(1)}, u32[]{:S(2)}, u32[]{:S(2)}) %collective-permute-start.8) | collective-permute-done | bytes 4128 | tf_op jit(solution)/shard_map/ppermute | solution.py:377
  46.5 1.1 %shard_map.65 = (f32[1,256]{1,0:T(1,128)S(1)}, f32[32,256]{1,0:T(8,128)S(1)}, f32[32,256]{1,0:T(8,128)S(1)}, f32[32,256]{1,0:T(8,128)S(1)}) custom-call(f32[1,1024]{1,0:T(1,128)S(1)} %maximum_add_fusion.degree, f32[1,1024]{1,0:T(1,128)S(1)} %collective-permute-done.8.got, f32[32,512]{1,0:T(8,128)S(1)} %get-tuple-element.46.start_a, ...), custom_call_target="tpu_custom_call" | custom-call | tf_op jit(solution)/shard_map/pallas_call | solution.py:38
  47.6 5.2 %collective-permute-start.9 = (f32[32,256]{1,0:T(8,128)S(1)}, f32[32,256]{1,0:T(8,128)S(1)}, u32[]{:S(2)}, u32[]{:S(2)}) collective-permute-start(f32[32,256]{1,0:T(8,128)S(1)} %get-tuple-element.60), channel_id=1, source_target_pairs={{0,1},{1,0},{2,3},{3,2},{4,5},{5,4},{6,7},{7,6},{8,9},{9,8},{10,11... | collective-permute-start | bytes 98312 | tf_op jit(solution)/shard_map/ppermute | solution.py:377
  52.9 1.9 %collective-permute-done.9 = f32[32,256]{1,0:T(8,128)S(1)} collective-permute-done((f32[32,256]{1,0:T(8,128)S(1)}, f32[32,256]{1,0:T(8,128)S(1)}, u32[]{:S(2)}, u32[]{:S(2)}) %collective-permute-start.9) | collective-permute-done | bytes 32800 | tf_op jit(solution)/shard_map/ppermute | solution.py:377
  54.8 2.1 %collective-permute-start.11 = (f32[32,256]{1,0:T(8,128)S(1)}, f32[32,256]{1,0:T(8,128)S(1)}, u32[]{:S(2)}, u32[]{:S(2)}) collective-permute-start(f32[32,256]{1,0:T(8,128)S(1)} %get-tuple-element.68.refs_0_), channel_id=1, source_target_pairs={{0,1},{1,0},{2,3},{3,2},{4,5},{5,4},{6,7},{7,6},{8,9},{9,8},{10,11... | collective-permute-start | bytes 98312 | tf_op jit(solution)/shard_map/ppermute | solution.py:377
  56.9 1.9 %collective-permute-done.11.refs_1_ = f32[32,256]{1,0:T(8,128)S(1)} collective-permute-done((f32[32,256]{1,0:T(8,128)S(1)}, f32[32,256]{1,0:T(8,128)S(1)}, u32[]{:S(2)}, u32[]{:S(2)}) %collective-permute-start.11) | collective-permute-done | bytes 32800 | tf_op jit(solution)/shard_map/ppermute | solution.py:377
  58.8 0.6 shard_map.66
  59.4 1.2 %collective-permute-done.13 = f32[32,512]{1,0:T(8,128)S(1)} collective-permute-done((f32[32,512]{1,0:T(8,128)S(1)}, f32[32,512]{1,0:T(8,128)S(1)}, u32[]{:S(2)}, u32[]{:S(2)}) %collective-permute-start.13) | collective-permute-done | bytes 65568 | tf_op jit(solution)/shard_map/ppermute | solution.py:377
  60.7 1.6 %collective-permute-start.14 = (f32[32,256]{1,0:T(8,128)S(1)}, f32[32,256]{1,0:T(8,128)S(1)}, u32[]{:S(2)}, u32[]{:S(2)}) collective-permute-start(f32[32,256]{1,0:T(8,128)S(1)} %get-tuple-element.70), channel_id=1, source_target_pairs={{0,16},{1,17},{2,18},{3,19},{4,20},{5,21},{6,22},{7,23},{8,24},{9,... | collective-permute-start | bytes 98312 | tf_op jit(solution)/shard_map/ppermute | solution.py:377
  62.3 2.4 %collective-permute-done.14.got = f32[32,256]{1,0:T(8,128)S(1)} collective-permute-done((f32[32,256]{1,0:T(8,128)S(1)}, f32[32,256]{1,0:T(8,128)S(1)}, u32[]{:S(2)}, u32[]{:S(2)}) %collective-permute-start.14) | collective-permute-done | bytes 32800 | tf_op jit(solution)/shard_map/ppermute | solution.py:377
  64.7 0.4 shard_map.67
  65.1 1.2 %collective-permute-done.15.got = f32[24,128]{1,0:T(8,128)S(1)} collective-permute-done((f32[24,128]{1,0:T(8,128)S(1)}, f32[24,128]{1,0:T(8,128)S(1)}, u32[]{:S(2)}, u32[]{:S(2)}) %collective-permute-start.15) | collective-permute-done | bytes 12320 | tf_op jit(solution)/shard_map/ppermute | solution.py:377
  66.3 15.7 %all_to_all.5.parts = f32[16,24,128]{2,1,0:T(8,128)S(1)} all-to-all(f32[16,24,128]{2,1,0:T(8,128)S(1)} %shard_map.68), channel_id=1, replica_groups=mesh['row'=2,'core'=2,'inner'=8] {'row','inner'}, dimensions={0} | all-to-all | bytes 393216 | tf_op jit(solution)/shard_map/all_to_all | solution.py:458
  82.0 4.2 %shard_map.69 = (f32[96,256]{1,0:T(8,128)}, f32[4,32,32]{2,1,0:T(8,128)}) custom-call(f32[16,24,128]{2,1,0:T(8,128)S(1)} %all_to_all.5.parts, f32[32,256]{1,0:T(8,128)S(1)} %slice.36.start.v0, f32[32,256]{1,0:T(8,128)S(1)} %get-tuple-element.69.image.v1, f32[32,256]{1,0:T(8,128)S(1)} %get-tuple-element.65.v2), custom_call_target="tpu_custom_call" | custom-call | tf_op jit(solution)/shard_map/pallas_call | solution.py:38
  (30 shorter events, 0.4 us)
Async XLA Ops:
  0.6 28.7 %copy-start = (bf16[256,1024]{1,0:T(8,128)(2,1)S(1)}, bf16[256,1024]{1,0:T(8,128)(2,1)}, u32[]{:S(2)}) copy-start(bf16[256,1024]{1,0:T(8,128)(2,1)} %refs_4_.1) | copy-start | bytes 1572868
  0.6 15.2 %collective-permute-start.1 = (bf16[256,1024]{1,0:T(8,128)(2,1)}, bf16[256,1024]{1,0:T(8,128)(2,1)S(1)}, u32[]{:S(2)}, u32[]{:S(2)}) collective-permute-start(bf16[256,1024]{1,0:T(8,128)(2,1)} %refs_4_.1), channel_id=1, source_target_pairs={{0,16},{1,17},{2,18},{3,19},{4,20},{5,21},{6,22},{7,23},{8,24},{9,... | collective-permute-start | bytes 1572872 | tf_op jit(solution)/shard_map/ppermute | solution.py:377
  3.7 28.1 %collective-permute-start = (bf16[256,1024]{1,0:T(8,128)(2,1)}, bf16[256,1024]{1,0:T(8,128)(2,1)S(1)}, u32[]{:S(2)}, u32[]{:S(2)}) collective-permute-start(bf16[256,1024]{1,0:T(8,128)(2,1)} %refs_4_.1), channel_id=1, source_target_pairs={{0,8},{1,9},{2,10},{3,11},{4,12},{5,13},{6,14},{7,15},{8,0},{9,1},... | collective-permute-start | bytes 1572872 | tf_op jit(solution)/shard_map/ppermute | solution.py:377
  15.8 16.5 %collective-permute-start.2 = (bf16[256,1024]{1,0:T(8,128)(2,1)S(1)}, bf16[256,1024]{1,0:T(8,128)(2,1)S(1)}, u32[]{:S(2)}, u32[]{:S(2)}) collective-permute-start(bf16[256,1024]{1,0:T(8,128)(2,1)S(1)} %collective-permute-done.1.r0), channel_id=1, source_target_pairs={{0,8},{1,9},{2,10},{3,11},{4,12},{5,13},{6,14},{7,15},{8,0},{9,1},... | collective-permute-start | bytes 1572872 | tf_op jit(solution)/shard_map/ppermute | solution.py:377
  16.8 8.8 %collective-permute-start.5 = (bf16[128,1024]{1,0:T(8,128)(2,1)S(1)}, bf16[128,1024]{1,0:T(8,128)(2,1)S(1)}, u32[]{:S(2)}, u32[]{:S(2)}) collective-permute-start(bf16[128,1024]{1,0:T(8,128)(2,1)S(1)} %slice.28), channel_id=1, source_target_pairs={{0,1},{1,0},{2,3},{3,2},{4,5},{5,4},{6,7},{7,6},{8,9},{9,8},{10,11... | collective-permute-start | bytes 786440 | tf_op jit(solution)/shard_map/ppermute | solution.py:377
  25.6 9.1 %collective-permute-start.6 = (bf16[128,1024]{1,0:T(8,128)(2,1)S(1)}, bf16[128,1024]{1,0:T(8,128)(2,1)S(1)}, u32[]{:S(2)}, u32[]{:S(2)}) collective-permute-start(bf16[128,1024]{1,0:T(8,128)(2,1)S(1)} %collective-permute-done.5.refs_5_), channel_id=1, source_target_pairs={{0,2},{2,4},{3,1},{4,6},{5,3},{7,5},{8,10},{10,12},{11,9},{12,14},... | collective-permute-start | bytes 786440 | tf_op jit(solution)/shard_map/ppermute | solution.py:377
  29.3 0.8 copy-start.3
  29.4 2.5 %copy-start.1 = (bf16[1024,32]{0,1:T(8,128)(2,1)S(1)}, bf16[1024,32]{0,1:T(8,128)(2,1)}, u32[]{:S(2)}) copy-start(bf16[1024,32]{0,1:T(8,128)(2,1)} %param.7) | copy-start | bytes 196612
  29.4 11.1 %collective-permute-start.3 = (bf16[128,1024]{1,0:T(8,128)(2,1)S(1)}, bf16[128,1024]{1,0:T(8,128)(2,1)S(1)}, u32[]{:S(2)}, u32[]{:S(2)}) collective-permute-start(bf16[128,1024]{1,0:T(8,128)(2,1)S(1)} %slice.29), channel_id=1, source_target_pairs={{0,1},{1,0},{2,3},{3,2},{4,5},{5,4},{6,7},{7,6},{8,9},{9,8},{10,11... | collective-permute-start | bytes 786440 | tf_op jit(solution)/shard_map/ppermute | solution.py:377
  29.4 11.0 %collective-permute-start.4 = (bf16[128,1024]{1,0:T(8,128)(2,1)S(1)}, bf16[128,1024]{1,0:T(8,128)(2,1)S(1)}, u32[]{:S(2)}, u32[]{:S(2)}) collective-permute-start(bf16[128,1024]{1,0:T(8,128)(2,1)S(1)} %slice.29), channel_id=1, source_target_pairs={{0,8},{1,2},{2,1},{3,4},{4,3},{5,6},{6,5},{7,15},{8,0},{9,10},{10,... | collective-permute-start | bytes 786440 | tf_op jit(solution)/shard_map/ppermute | solution.py:377
  30.1 0.7 copy-start.2
  41.6 1.2 %collective-permute-start.7 = (f32[1,1024]{1,0:T(1,128)S(1)}, f32[1,1024]{1,0:T(1,128)S(1)}, u32[]{:S(2)}, u32[]{:S(2)}) collective-permute-start(f32[1,1024]{1,0:T(1,128)S(1)} %get-tuple-element.45), channel_id=1, source_target_pairs={{0,8},{1,9},{2,10},{3,11},{4,12},{5,13},{6,14},{7,15},{8,0},{9,1},... | collective-permute-start | bytes 12296 | tf_op jit(solution)/shard_map/ppermute | solution.py:377
  42.9 3.7 %collective-permute-start.8 = (f32[1,1024]{1,0:T(1,128)S(1)}, f32[1,1024]{1,0:T(1,128)S(1)}, u32[]{:S(2)}, u32[]{:S(2)}) collective-permute-start(f32[1,1024]{1,0:T(1,128)S(1)} %maximum_add_fusion.degree), channel_id=1, source_target_pairs={{0,16},{1,17},{2,18},{3,19},{4,20},{5,21},{6,22},{7,23},{8,24},{9,... | collective-permute-start | bytes 12296 | tf_op jit(solution)/shard_map/ppermute | solution.py:377
  47.6 5.3 %collective-permute-start.10 = (f32[32,256]{1,0:T(8,128)S(1)}, f32[32,256]{1,0:T(8,128)S(1)}, u32[]{:S(2)}, u32[]{:S(2)}) collective-permute-start(f32[32,256]{1,0:T(8,128)S(1)} %get-tuple-element.61), channel_id=1, source_target_pairs={{0,8},{1,2},{2,1},{3,4},{4,3},{5,6},{6,5},{7,15},{8,0},{9,10},{10,... | collective-permute-start | bytes 98312 | tf_op jit(solution)/shard_map/ppermute | solution.py:377
  47.6 7.1 %collective-permute-start.9 = (f32[32,256]{1,0:T(8,128)S(1)}, f32[32,256]{1,0:T(8,128)S(1)}, u32[]{:S(2)}, u32[]{:S(2)}) collective-permute-start(f32[32,256]{1,0:T(8,128)S(1)} %get-tuple-element.60), channel_id=1, source_target_pairs={{0,1},{1,0},{2,3},{3,2},{4,5},{5,4},{6,7},{7,6},{8,9},{9,8},{10,11... | collective-permute-start | bytes 98312 | tf_op jit(solution)/shard_map/ppermute | solution.py:377
  54.8 4.0 %collective-permute-start.11 = (f32[32,256]{1,0:T(8,128)S(1)}, f32[32,256]{1,0:T(8,128)S(1)}, u32[]{:S(2)}, u32[]{:S(2)}) collective-permute-start(f32[32,256]{1,0:T(8,128)S(1)} %get-tuple-element.68.refs_0_), channel_id=1, source_target_pairs={{0,1},{1,0},{2,3},{3,2},{4,5},{5,4},{6,7},{7,6},{8,9},{9,8},{10,11... | collective-permute-start | bytes 98312 | tf_op jit(solution)/shard_map/ppermute | solution.py:377
  56.9 1.9 %collective-permute-start.12 = (f32[32,256]{1,0:T(8,128)S(1)}, f32[32,256]{1,0:T(8,128)S(1)}, u32[]{:S(2)}, u32[]{:S(2)}) collective-permute-start(f32[32,256]{1,0:T(8,128)S(1)} %get-tuple-element.68.refs_0_), channel_id=1, source_target_pairs={{0,8},{1,2},{2,1},{3,4},{4,3},{5,6},{6,5},{7,15},{8,0},{9,10},{10,... | collective-permute-start | bytes 98312 | tf_op jit(solution)/shard_map/ppermute | solution.py:377
  59.4 1.3 %collective-permute-start.13 = (f32[32,512]{1,0:T(8,128)S(1)}, f32[32,512]{1,0:T(8,128)S(1)}, u32[]{:S(2)}, u32[]{:S(2)}) collective-permute-start(f32[32,512]{1,0:T(8,128)S(1)} %get-tuple-element.63), channel_id=1, source_target_pairs={{0,8},{1,9},{2,10},{3,11},{4,12},{5,13},{6,14},{7,15},{8,0},{9,1},... | collective-permute-start | bytes 196616 | tf_op jit(solution)/shard_map/ppermute | solution.py:377
  60.7 4.0 %collective-permute-start.14 = (f32[32,256]{1,0:T(8,128)S(1)}, f32[32,256]{1,0:T(8,128)S(1)}, u32[]{:S(2)}, u32[]{:S(2)}) collective-permute-start(f32[32,256]{1,0:T(8,128)S(1)} %get-tuple-element.70), channel_id=1, source_target_pairs={{0,16},{1,17},{2,18},{3,19},{4,20},{5,21},{6,22},{7,23},{8,24},{9,... | collective-permute-start | bytes 98312 | tf_op jit(solution)/shard_map/ppermute | solution.py:377
  65.1 1.2 %collective-permute-start.15 = (f32[24,128]{1,0:T(8,128)S(1)}, f32[24,128]{1,0:T(8,128)S(1)}, u32[]{:S(2)}, u32[]{:S(2)}) collective-permute-start(f32[24,128]{1,0:T(8,128)S(1)} %get-tuple-element.64.mine), channel_id=1, source_target_pairs={{0,8},{1,9},{2,10},{3,11},{4,12},{5,13},{6,14},{7,15},{8,0},{9,1},... | collective-permute-start | bytes 36872 | tf_op jit(solution)/shard_map/ppermute | solution.py:377
